TPU v7x, 512 devices: a whole 4x8x8 slice. The times are simulated.
512 devices in a mesh: row: 16 (over x, z_hi), col: 32 (over z_lo, y, core).
Axes of the slice: x: 4, y: 8, z: 8 (z_hi: 4, z_lo: 2; z = z_hi * 2 + z_lo), core: 2. Of those that a mesh axis runs over, the one named last changes fastest.
Arguments:
- inputs: bfloat16 [512, 1792, 128], P('row', 'col'), may hold values from -6 to 6
- cotangent: bfloat16 [512, 1792, 128], P('row', 'col'), may hold values from -6 to 6
- w_conv: bfloat16 [3, 3, 128, 128], replicated, may hold values from -0.1875 to 0.1875
- w_down: bfloat16 [3, 3, 128, 256], replicated, may hold values from -0.1875 to 0.1875
- w_up: bfloat16 [2, 2, 256, 128], replicated, may hold values from -0.375 to 0.375
Outputs:
- output: bfloat16 [512, 1792, 128], P('row', 'col')
- grad_inputs: bfloat16 [512, 1792, 128], P('row', 'col')
- grad_conv: float32 [147456], P(('row', 'col'))
- grad_down: float32 [294912], P(('row', 'col'))
- grad_up: float32 [131072], P(('row', 'col'))
All inputs are finite; a program needn't handle non-finite values.
Results may differ from a plain program's by a relative error of at most 0.013.
Values may be sent and summed in bfloat16 or wider, within the bound.
No kernel may reach another device: no remote copies, remote signals or barrier semaphores. Data moves between devices by JAX's collectives and lax.ppermute only.
A program may use at most 64 MiB of HBM per device.

v0:
```python
import math

import jax
import jax.numpy as jnp
from jax import lax
from jax.sharding import PartitionSpec as P


def extended(block, sides, width):
    for axis, dim in sides:
        count = lax.axis_size(axis)
        forward = [(i, i + 1) for i in range(count - 1)]
        backward = [(target, source) for source, target in forward]
        low = lax.ppermute(
            lax.slice_in_dim(block, block.shape[dim] - width, None, axis=dim), axis, forward
        )
        high = lax.ppermute(lax.slice_in_dim(block, 0, width, axis=dim), axis, backward)
        block = jnp.concatenate([low, block, high], axis=dim)
    return block


def from_behind(value, axis, steps):
    count = lax.axis_size(axis)
    leading, last = (max(0, -steps), min(count, count - steps))
    return lax.ppermute(value, axis, [(source, source + steps) for source in range(leading, last)])


def silu_slope(value):
    sig = jax.nn.sigmoid(value)
    return sig * (1.0 + value * (1.0 - sig))


def conv_taps(padded, kernel, count_r, count_c):
    width = padded.shape[2]
    total = None
    for pos_r in range(3):
        for pos_c in range(3):
            window = padded[pos_r : pos_r + count_r, pos_c : pos_c + count_c].reshape(-1, width)
            term = jnp.dot(window, kernel[pos_r, pos_c], preferred_element_type=jnp.float32)
            total = term if total is None else total + term
    return total.reshape(count_r, count_c, -1)


def body(inputs, cotangent, w_conv, w_down, w_up):
    rows, cols, width = inputs.shape
    wide = w_down.shape[3]
    half_r = rows // 2
    half_c = cols // 2
    n_row = lax.axis_size("row")
    n_col = lax.axis_size("col")
    padded = extended(inputs, (("row", 0), ("col", 1)), 1)
    pre = conv_taps(padded, w_conv, rows, cols)
    fine_own = jax.nn.silu(pre).astype(jnp.bfloat16)
    top = from_behind(fine_own[-1:], "row", 1)
    fine_rows = jnp.concatenate([top, fine_own], axis=0)
    left = from_behind(fine_rows[:, -1:], "col", 1)
    fine_ext = jnp.concatenate([left, fine_rows], axis=1)
    fine = fine_ext[1:, 1:]
    strided = {}
    coarse_pre = None
    for pos_r in range(3):
        for pos_c in range(3):
            window = fine_ext[
                pos_r : pos_r + 2 * half_r - 1 : 2, pos_c : pos_c + 2 * half_c - 1 : 2
            ].reshape(-1, width)
            strided[pos_r, pos_c] = window
            term = jnp.dot(window, w_down[pos_r, pos_c], preferred_element_type=jnp.float32)
            coarse_pre = term if coarse_pre is None else coarse_pre + term
    coarse_pre = coarse_pre.reshape(half_r, half_c, wide)
    coarse = jax.nn.silu(coarse_pre).astype(jnp.bfloat16)
    upsampled = jnp.einsum(
        "mnc,pqco->mpnqo", coarse, w_up, preferred_element_type=jnp.float32
    ).reshape(rows, cols, width)
    output = (fine.astype(jnp.float32) + upsampled).astype(jnp.bfloat16)
    cot_r = cotangent.reshape(half_r, 2, half_c, 2, width)
    grad_coarse = jnp.einsum("mpnqo,pqco->mnc", cot_r, w_up, preferred_element_type=jnp.float32)
    up_local = jnp.einsum("mnc,mpnqo->pqco", coarse, cot_r, preferred_element_type=jnp.float32)
    grad_cpre = (grad_coarse * silu_slope(coarse_pre)).astype(jnp.bfloat16)
    below = from_behind(grad_cpre[:1], "row", -1)
    grad_rows = jnp.concatenate([grad_cpre, below], axis=0)
    right = from_behind(grad_rows[:, :1], "col", -1)
    grad_ext = jnp.concatenate([grad_rows, right], axis=1)
    phase_of = (1, 0, 1)
    offset_of = (1, 0, 0)
    phases = {}
    grad_flat = grad_cpre.reshape(-1, wide)
    down_parts = []
    for pos_r in range(3):
        for pos_c in range(3):
            start_r = offset_of[pos_r]
            start_c = offset_of[pos_c]
            window = grad_ext[start_r : start_r + half_r, start_c : start_c + half_c].reshape(
                -1, wide
            )
            term = lax.dot_general(
                window,
                w_down[pos_r, pos_c],
                (((1,), (1,)), ((), ())),
                preferred_element_type=jnp.float32,
            )
            slot = (phase_of[pos_r], phase_of[pos_c])
            phases[slot] = term if slot not in phases else phases[slot] + term
            down_parts.append(
                lax.dot_general(
                    strided[pos_r, pos_c],
                    grad_flat,
                    (((0,), (0,)), ((), ())),
                    preferred_element_type=jnp.float32,
                )
            )
    down_local = jnp.stack(down_parts).reshape(3, 3, width, wide)
    even_rows = jnp.stack(
        [phases[0, 0].reshape(half_r, half_c, width), phases[0, 1].reshape(half_r, half_c, width)],
        axis=2,
    )
    odd_rows = jnp.stack(
        [phases[1, 0].reshape(half_r, half_c, width), phases[1, 1].reshape(half_r, half_c, width)],
        axis=2,
    )
    spread = jnp.stack([even_rows, odd_rows], axis=1).reshape(rows, cols, width)
    grad_fine = cotangent.astype(jnp.float32) + spread
    grad_pre = (grad_fine * silu_slope(pre)).astype(jnp.bfloat16)
    grad_pad = extended(grad_pre, (("row", 0), ("col", 1)), 1)
    grad_x = None
    conv_parts = []
    grad_pre_flat = grad_pre.reshape(-1, width)
    for pos_r in range(3):
        for pos_c in range(3):
            window = grad_pad[2 - pos_r : 2 - pos_r + rows, 2 - pos_c : 2 - pos_c + cols].reshape(
                -1, width
            )
            term = lax.dot_general(
                window,
                w_conv[pos_r, pos_c],
                (((1,), (1,)), ((), ())),
                preferred_element_type=jnp.float32,
            )
            grad_x = term if grad_x is None else grad_x + term
            source = padded[pos_r : pos_r + rows, pos_c : pos_c + cols].reshape(-1, width)
            conv_parts.append(
                lax.dot_general(
                    source,
                    grad_pre_flat,
                    (((0,), (0,)), ((), ())),
                    preferred_element_type=jnp.float32,
                )
            )
    grad_inputs = grad_x.reshape(rows, cols, width).astype(jnp.bfloat16)
    conv_local = jnp.stack(conv_parts).reshape(-1)
    conv_sum, down_sum, up_sum = (
        lax.psum_scatter(conv_local, ("row", "col"), scatter_dimension=0, tiled=True),
        lax.psum_scatter(down_local.reshape(-1), ("row", "col"), scatter_dimension=0, tiled=True),
        lax.psum_scatter(up_local.reshape(-1), ("row", "col"), scatter_dimension=0, tiled=True),
    )
    scale = 1.0 / math.sqrt(rows * n_row * cols * n_col)
    return (output, grad_inputs, conv_sum * scale, down_sum * scale, up_sum * scale)


def solution(mesh):
    return jax.shard_map(
        body,
        mesh=mesh,
        in_specs=(P("row", "col", None), P("row", "col", None), P(), P(), P()),
        out_specs=(
            P("row", "col", None),
            P("row", "col", None),
            P(("row", "col")),
            P(("row", "col")),
            P(("row", "col")),
        ),
        check_vma=False,
    )
```

profile of v0, /device:TPU:17, one launch (start us, length us, event | category | flops | bytes accessed | tf_op | source)
XLA Modules:
  0.0 443.1 jit_solution(6632770296590648248)
XLA Ops:
  7.2 0.8 fusion.122
  8.0 5.8 %collective-permute-start = (bf16[1,56,128]{2,1,0:T(8,128)(2,1)S(1)}, bf16[1,56,128]{2,1,0:T(8,128)(2,1)S(1)}, u32[]{:S(2)}, u32[]{:S(2)}) collective-permute-start(bf16[1,56,128]{2,1,0:T(8,128)(2,1)S(1)} %get-tuple-element.37), channel_id=1, source_target_pairs={{0,32},{32,64},{64,96},{96,128},{128,160},{160,192},{192,224},{224... | collective-permute-start | bytes 43016 | tf_op jit(solution)/shard_map/ppermute | solution.py:14
  13.8 1.3 collective-permute-start.1
  15.1 1.3 constant_dynamic-update-slice_fusion.3
  16.4 5.5 %collective-permute-done.1 = bf16[1,56,128]{2,1,0:T(8,128)(2,1)S(1)} collective-permute-done((bf16[1,56,128]{2,1,0:T(8,128)(2,1)S(1)}, bf16[1,56,128]{2,1,0:T(8,128)(2,1)S(1)}, u32[]{:S(2)}, u32[]{:S(2)}) %collective-permute-start.1) | collective-permute-done | bytes 14368 | tf_op jit(solution)/shard_map/ppermute | solution.py:17
  22.0 4.9 %collective-permute-start.2 = (bf16[34,1,128]{2,1,0:T(2,128)(2,1)S(1)}, bf16[34,1,128]{2,1,0:T(2,128)(2,1)S(1)}, u32[]{:S(2)}, u32[]{:S(2)}) collective-permute-start(bf16[34,1,128]{2,1,0:T(2,128)(2,1)S(1)} %get-tuple-element.27), channel_id=1, source_target_pairs={{0,1},{1,2},{2,3},{3,4},{4,5},{5,6},{6,7},{7,8},{8,9},{9,10},{10,1... | collective-permute-start | bytes 26120 | tf_op jit(solution)/shard_map/ppermute | solution.py:14
  26.9 1.9 collective-permute-start.3
  29.5 2.5 collective-permute-done.3
  36.0 5.7 %collective-permute-start.4 = (bf16[1,56,128]{2,1,0:T(8,128)(2,1)S(1)}, bf16[1,56,128]{2,1,0:T(8,128)(2,1)S(1)}, u32[]{:S(2)}, u32[]{:S(2)}) collective-permute-start(bf16[1,56,128]{2,1,0:T(8,128)(2,1)S(1)} %slice.288), channel_id=1, source_target_pairs={{0,32},{32,64},{64,96},{96,128},{128,160},{160,192},{192,224},{224... | collective-permute-start | bytes 43016 | tf_op jit(solution)/shard_map/ppermute | solution.py:25
  42.8 0.9 slice.255
  43.8 0.8 slice.257
  47.9 2.6 collective-permute-start.5
  50.5 0.8 pad_maximum_fusion.1
  51.3 6.2 %slice.243 = bf16[16,28,128]{2,1,0:T(8,128)(2,1)S(1)} slice(bf16[33,56,128]{2,1,0:T(8,128)(2,1)} %pad_maximum_fusion.1), slice={[0:31:2], [0:55:2], [0:128:1]} | slice | bytes 229376 | tf_op jit(solution)/shard_map/slice | solution.py:63
  58.8 1.1 fusion.53
  59.9 8.2 %slice.245 = bf16[16,28,128]{2,1,0:T(8,128)(2,1)} slice(bf16[33,56,128]{2,1,0:T(8,128)(2,1)} %pad_maximum_fusion.1), slice={[0:31:2], [1:56:2], [0:128:1]} | slice | bytes 229376 | tf_op jit(solution)/shard_map/slice | solution.py:63
  68.1 0.9 reshape.162
  69.1 1.7 maximum_maximum_fusion.1
  70.8 6.2 %slice.241 = bf16[16,28,128]{2,1,0:T(8,128)(2,1)S(1)} slice(bf16[33,57,128]{2,1,0:T(8,128)(2,1)} %maximum_maximum_fusion.1), slice={[0:31:2], [0:55:2], [0:128:1]} | slice | bytes 229376 | tf_op jit(solution)/shard_map/slice | solution.py:63
  77.0 6.3 %slice.247 = bf16[16,28,128]{2,1,0:T(8,128)(2,1)S(1)} slice(bf16[33,57,128]{2,1,0:T(8,128)(2,1)} %maximum_maximum_fusion.1), slice={[1:32:2], [0:55:2], [0:128:1]} | slice | bytes 229376 | tf_op jit(solution)/shard_map/slice | solution.py:63
  83.3 6.3 %slice.253 = bf16[16,28,128]{2,1,0:T(8,128)(2,1)S(1)} slice(bf16[33,57,128]{2,1,0:T(8,128)(2,1)} %maximum_maximum_fusion.1), slice={[2:33:2], [0:55:2], [0:128:1]} | slice | bytes 229376 | tf_op jit(solution)/shard_map/slice | solution.py:63
  91.6 1.1 convolution_add_fusion.20
  95.4 1.0 multiply_convert_fusion.3
  96.5 1.4 fusion.5
  97.9 0.9 fusion.14
  98.8 0.9 fusion.38
  99.7 0.9 fusion.43
  100.7 1.3 convolution_bitcast_fusion
  101.9 0.9 fusion.13
  102.8 0.9 fusion.12
  103.7 0.9 fusion.11
  104.6 0.9 fusion.10
  105.5 0.9 fusion.9
  106.4 0.9 fusion.8
  107.3 0.9 fusion.7
  108.2 0.9 fusion.6
  109.0 1.3 collective-permute-start.6
  110.3 1.7 reshape.210
  112.0 2.2 fusion.24
  114.9 1.0 add_convert_fusion
  115.9 0.9 convolution_bitcast_fusion.2
  116.9 2.9 copy.29
  119.9 2.1 collective-permute-start.7
  122.0 1.1 convolution_add_fusion.24
  123.1 0.9 fusion.49
  124.8 1.9 collective-permute-done.7
  126.8 0.7 reshape.175
  127.6 1.3 convolution_add_fusion.23
  129.1 0.9 convolution_add_fusion.21
  130.0 1.7 stack_reshape.12
  131.7 1.2 convolution_add_fusion.25
  132.9 1.0 maximum_bitcast_fusion
  134.0 0.7 copy.20
  139.9 5.2 %collective-permute-start.8 = (bf16[1,56,128]{2,1,0:T(8,128)(2,1)S(1)}, bf16[1,56,128]{2,1,0:T(8,128)(2,1)S(1)}, u32[]{:S(2)}, u32[]{:S(2)}) collective-permute-start(bf16[1,56,128]{2,1,0:T(8,128)(2,1)S(1)} %get-tuple-element.31), channel_id=1, source_target_pairs={{0,32},{32,64},{64,96},{96,128},{128,160},{160,192},{192,224},{224... | collective-permute-start | bytes 43016 | tf_op jit(solution)/shard_map/ppermute | solution.py:14
  145.0 1.3 collective-permute-start.9
  146.7 0.8 copy-done.38
  147.5 2.9 collective-permute-done.9
  150.4 1.9 collective-permute-start.10
  152.4 4.9 %collective-permute-start.11 = (bf16[34,1,128]{2,1,0:T(2,128)(2,1)S(1)}, bf16[34,1,128]{2,1,0:T(2,128)(2,1)S(1)}, u32[]{:S(2)}, u32[]{:S(2)}) collective-permute-start(bf16[34,1,128]{2,1,0:T(2,128)(2,1)S(1)} %get-tuple-element.23), channel_id=1, source_target_pairs={{0,1},{1,2},{2,3},{3,4},{4,5},{5,6},{6,7},{7,8},{8,9},{9,10},{10,1... | collective-permute-start | bytes 26120 | tf_op jit(solution)/shard_map/ppermute | solution.py:14
  160.9 1.1 fusion.3
  161.9 270.3 %all-reduce.6.cloned.1.call-done = (f32[147456]{0:T(1024)}, f32[294912]{0:T(1024)}, f32[131072]{0:T(1024)}) async-done(((f32[147456]{0:T(1024)}, f32[294912]{0:T(1024)}, f32[131072]{0:T(1024)}), (f32[147456]{0:T(1024)}, f32[294912]{0:T(1024)}, f32[131072]{0:T(1024)})) %all-reduce.6.cloned.1.call-update) | async-done | bytes 2293776
  432.2 1.4 dynamic-slice_multiply_fusion
  433.6 1.3 dynamic-slice_multiply_fusion.1
  434.9 1.3 dynamic-slice_multiply_fusion.2
  (181 shorter events, 26.0 us)
Async XLA Ops:
  7.2 89.3 %copy-start = (bf16[2,2,256,128]{3,2,1,0:T(8,128)(2,1)S(1)}, bf16[2,2,256,128]{3,2,1,0:T(8,128)(2,1)}, u32[]{:S(2)}) copy-start(bf16[2,2,256,128]{3,2,1,0:T(8,128)(2,1)} %param.9) | copy-start | bytes 786436
  7.2 425.0 %all-reduce.6.cloned.1.call-start = ((), (), s32[]{:S(2)}) async-start(), calls=%async_computation | async-start | bytes 4587520
  8.0 7.1 %collective-permute-start = (bf16[1,56,128]{2,1,0:T(8,128)(2,1)S(1)}, bf16[1,56,128]{2,1,0:T(8,128)(2,1)S(1)}, u32[]{:S(2)}, u32[]{:S(2)}) collective-permute-start(bf16[1,56,128]{2,1,0:T(8,128)(2,1)S(1)} %get-tuple-element.37), channel_id=1, source_target_pairs={{0,32},{32,64},{64,96},{96,128},{128,160},{160,192},{192,224},{224... | collective-permute-start | bytes 43016 | tf_op jit(solution)/shard_map/ppermute | solution.py:14
  13.8 8.1 %collective-permute-start.1 = (bf16[1,56,128]{2,1,0:T(8,128)(2,1)S(1)}, bf16[1,56,128]{2,1,0:T(8,128)(2,1)S(1)}, u32[]{:S(2)}, u32[]{:S(2)}) collective-permute-start(bf16[1,56,128]{2,1,0:T(8,128)(2,1)S(1)} %get-tuple-element.36), channel_id=1, source_target_pairs={{32,0},{64,32},{96,64},{128,96},{160,128},{192,160},{224,192},{256... | collective-permute-start | bytes 43016 | tf_op jit(solution)/shard_map/ppermute | solution.py:17
  16.4 12.8 %copy-start.39 = (bf16[33,56,128]{2,1,0:T(8,128)(2,1)}, bf16[33,56,128]{2,1,0:T(8,128)(2,1)S(1)}, u32[]{:S(2)}) copy-start(bf16[33,56,128]{2,1,0:T(8,128)(2,1)S(1)} %get-tuple-element.33) | copy-start | bytes 1419268
  16.4 12.5 %copy-start.17 = (bf16[3,3,128,128]{3,2,1,0:T(8,128)(2,1)S(1)}, bf16[3,3,128,128]{3,2,1,0:T(8,128)(2,1)}, u32[]{:S(2)}) copy-start(bf16[3,3,128,128]{3,2,1,0:T(8,128)(2,1)} %param.7) | copy-start | bytes 884740
  21.9 7.3 %copy-start.15 = (bf16[33,56,128]{2,1,0:T(8,128)(2,1)}, bf16[33,56,128]{2,1,0:T(8,128)(2,1)S(1)}, u32[]{:S(2)}) copy-start(bf16[33,56,128]{2,1,0:T(8,128)(2,1)S(1)} %get-tuple-element.42) | copy-start | bytes 1419268
  22.0 7.5 %collective-permute-start.2 = (bf16[34,1,128]{2,1,0:T(2,128)(2,1)S(1)}, bf16[34,1,128]{2,1,0:T(2,128)(2,1)S(1)}, u32[]{:S(2)}, u32[]{:S(2)}) collective-permute-start(bf16[34,1,128]{2,1,0:T(2,128)(2,1)S(1)} %get-tuple-element.27), channel_id=1, source_target_pairs={{0,1},{1,2},{2,3},{3,4},{4,5},{5,6},{6,7},{7,8},{8,9},{9,10},{10,1... | collective-permute-start | bytes 26120 | tf_op jit(solution)/shard_map/ppermute | solution.py:14
  26.9 5.1 %collective-permute-start.3 = (bf16[34,1,128]{2,1,0:T(2,128)(2,1)S(1)}, bf16[34,1,128]{2,1,0:T(2,128)(2,1)S(1)}, u32[]{:S(2)}, u32[]{:S(2)}) collective-permute-start(bf16[34,1,128]{2,1,0:T(2,128)(2,1)S(1)} %get-tuple-element.28), channel_id=1, source_target_pairs={{1,0},{2,1},{3,2},{4,3},{5,4},{6,5},{7,6},{8,7},{9,8},{10,9},{11,1... | collective-permute-start | bytes 26120 | tf_op jit(solution)/shard_map/ppermute | solution.py:17
  32.5 0.8 copy-start.3
  32.5 0.9 copy-start.13
  32.5 1.1 copy-start.11
  32.5 1.3 copy-start.9
  32.5 2.6 copy-start.7
  32.5 2.9 copy-start.5
  33.8 1.0 copy-start.1
  36.0 11.3 %collective-permute-start.4 = (bf16[1,56,128]{2,1,0:T(8,128)(2,1)S(1)}, bf16[1,56,128]{2,1,0:T(8,128)(2,1)S(1)}, u32[]{:S(2)}, u32[]{:S(2)}) collective-permute-start(bf16[1,56,128]{2,1,0:T(8,128)(2,1)S(1)} %slice.288), channel_id=1, source_target_pairs={{0,32},{32,64},{64,96},{96,128},{128,160},{160,192},{192,224},{224... | collective-permute-start | bytes 43016 | tf_op jit(solution)/shard_map/ppermute | solution.py:25
  42.2 3.0 copy-start.24
  42.8 8.5 %copy-start.22 = (bf16[16,28,128]{2,1,0:T(8,128)(2,1)}, bf16[16,28,128]{2,1,0:T(8,128)(2,1)S(1)}, u32[]{:S(2)}) copy-start(bf16[16,28,128]{2,1,0:T(8,128)(2,1)S(1)} %slice.251) | copy-start | bytes 344068
  43.8 7.6 %copy-start.20 = (bf16[16,28,128]{2,1,0:T(8,128)(2,1)}, bf16[16,28,128]{2,1,0:T(8,128)(2,1)S(1)}, u32[]{:S(2)}) copy-start(bf16[16,28,128]{2,1,0:T(8,128)(2,1)S(1)} %slice.255) | copy-start | bytes 344068
  44.6 6.8 %copy-start.18 = (bf16[16,28,128]{2,1,0:T(8,128)(2,1)}, bf16[16,28,128]{2,1,0:T(8,128)(2,1)S(1)}, u32[]{:S(2)}) copy-start(bf16[16,28,128]{2,1,0:T(8,128)(2,1)S(1)} %slice.257) | copy-start | bytes 344068
  45.9 12.9 %copy-start.2 = (bf16[3,3,128,256]{3,2,1,0:T(8,128)(2,1)S(1)}, bf16[3,3,128,256]{3,2,1,0:T(8,128)(2,1)}, u32[]{:S(2)}) copy-start(bf16[3,3,128,256]{3,2,1,0:T(8,128)(2,1)} %param.8) | copy-start | bytes 1769476
  47.3 3.2 copy-start.48
  47.9 21.2 %collective-permute-start.5 = (bf16[33,1,128]{2,1,0:T(2,128)(2,1)}, bf16[33,1,128]{2,1,0:T(2,128)(2,1)}, u32[]{:S(2)}, u32[]{:S(2)}) collective-permute-start(bf16[33,1,128]{2,1,0:T(2,128)(2,1)} %fusion.116), channel_id=1, source_target_pairs={{0,1},{1,2},{2,3},{3,4},{4,5},{5,6},{6,7},{7,8},{8,9},{9,10},{10,1... | collective-permute-start | bytes 25352 | tf_op jit(solution)/shard_map/ppermute | solution.py:25
  57.5 0.6 copy-start.26
  77.0 13.9 %copy-start.33 = (bf16[16,28,128]{2,1,0:T(8,128)(2,1)}, bf16[16,28,128]{2,1,0:T(8,128)(2,1)S(1)}, u32[]{:S(2)}) copy-start(bf16[16,28,128]{2,1,0:T(8,128)(2,1)S(1)} %slice.241) | copy-start | bytes 344068
  83.3 7.7 %copy-start.31 = (bf16[16,28,128]{2,1,0:T(8,128)(2,1)}, bf16[16,28,128]{2,1,0:T(8,128)(2,1)S(1)}, u32[]{:S(2)}) copy-start(bf16[16,28,128]{2,1,0:T(8,128)(2,1)S(1)} %slice.247) | copy-start | bytes 344068
  89.5 1.4 copy-start.29
  91.6 1.4 copy-start.45
  92.7 0.9 copy-start.43
  92.9 0.9 copy-start.42
  93.6 0.9 copy-start.44
  93.9 0.9 copy-start.41
  94.5 0.9 copy-start.49
  96.5 1.4 copy-start.34
  100.6 1.3 copy-start.27
  100.7 2.2 copy-start.28
  100.7 3.1 copy-start.32
  101.9 2.7 copy-start.25
  101.9 3.5 copy-start.23
  102.8 3.6 copy-start.30
  103.7 3.5 copy-start.21
  104.6 3.5 copy-start.19
  105.5 6.5 %copy-start.46 = (bf16[32,56,128]{2,1,0:T(8,128)(2,1)S(1)}, bf16[32,56,128]{2,1,0:T(8,128)(2,1)}, u32[]{:S(2)}) copy-start(bf16[32,56,128]{2,1,0:T(8,128)(2,1)} %param.6) | copy-start | bytes 1376260
  109.0 10.7 %collective-permute-start.6 = (bf16[1,28,256]{2,1,0:T(8,128)(2,1)S(1)}, bf16[1,28,256]{2,1,0:T(8,128)(2,1)S(1)}, u32[]{:S(2)}, u32[]{:S(2)}) collective-permute-start(bf16[1,28,256]{2,1,0:T(8,128)(2,1)S(1)} %slice.291), channel_id=1, source_target_pairs={{32,0},{64,32},{96,64},{128,96},{160,128},{192,160},{224,192},{256... | collective-permute-start | bytes 43016 | tf_op jit(solution)/shard_map/ppermute | solution.py:25
  112.0 2.2 copy-start.35
  119.9 6.8 %collective-permute-start.7 = (bf16[17,1,256]{2,1,0:T(2,128)(2,1)S(1)}, bf16[17,1,256]{2,1,0:T(2,128)(2,1)S(1)}, u32[]{:S(2)}, u32[]{:S(2)}) collective-permute-start(bf16[17,1,256]{2,1,0:T(2,128)(2,1)S(1)} %pad_maximum_fusion.12), channel_id=1, source_target_pairs={{1,0},{2,1},{3,2},{4,3},{5,4},{6,5},{7,6},{8,7},{9,8},{10,9},{11,1... | collective-permute-start | bytes 26120 | tf_op jit(solution)/shard_map/ppermute | solution.py:25
  129.0 3.8 copy-start.36
  129.1 3.8 copy-start.37
  134.0 1.0 copy-start.47
  135.0 1.0 copy-start.14
  135.1 1.4 copy-start.40
  136.1 1.1 copy-start.12
  136.4 1.1 copy-start.10
  137.5 1.0 copy-start.8
  137.8 1.1 copy-start.6
  138.5 1.1 copy-start.16
  138.8 7.5 %copy-start.4 = (bf16[32,56,128]{2,1,0:T(8,128)(2,1)S(1)}, bf16[32,56,128]{2,1,0:T(8,128)(2,1)}, u32[]{:S(2)}) copy-start(bf16[32,56,128]{2,1,0:T(8,128)(2,1)} %copy-done.3) | copy-start | bytes 1376260
  139.9 7.7 %collective-permute-start.8 = (bf16[1,56,128]{2,1,0:T(8,128)(2,1)S(1)}, bf16[1,56,128]{2,1,0:T(8,128)(2,1)S(1)}, u32[]{:S(2)}, u32[]{:S(2)}) collective-permute-start(bf16[1,56,128]{2,1,0:T(8,128)(2,1)S(1)} %get-tuple-element.31), channel_id=1, source_target_pairs={{0,32},{32,64},{64,96},{96,128},{128,160},{160,192},{192,224},{224... | collective-permute-start | bytes 43016 | tf_op jit(solution)/shard_map/ppermute | solution.py:14
  145.0 5.4 %collective-permute-start.9 = (bf16[1,56,128]{2,1,0:T(8,128)(2,1)S(1)}, bf16[1,56,128]{2,1,0:T(8,128)(2,1)S(1)}, u32[]{:S(2)}, u32[]{:S(2)}) collective-permute-start(bf16[1,56,128]{2,1,0:T(8,128)(2,1)S(1)} %get-tuple-element.32), channel_id=1, source_target_pairs={{32,0},{64,32},{96,64},{128,96},{160,128},{192,160},{224,192},{256... | collective-permute-start | bytes 43016 | tf_op jit(solution)/shard_map/ppermute | solution.py:17
  146.7 0.8 copy-start.38
  150.4 7.2 %collective-permute-start.10 = (bf16[34,1,128]{2,1,0:T(2,128)(2,1)S(1)}, bf16[34,1,128]{2,1,0:T(2,128)(2,1)S(1)}, u32[]{:S(2)}, u32[]{:S(2)}) collective-permute-start(bf16[34,1,128]{2,1,0:T(2,128)(2,1)S(1)} %get-tuple-element.22), channel_id=1, source_target_pairs={{1,0},{2,1},{3,2},{4,3},{5,4},{6,5},{7,6},{8,7},{9,8},{10,9},{11,1... | collective-permute-start | bytes 26120 | tf_op jit(solution)/shard_map/ppermute | solution.py:17
  152.4 5.8 %collective-permute-start.11 = (bf16[34,1,128]{2,1,0:T(2,128)(2,1)S(1)}, bf16[34,1,128]{2,1,0:T(2,128)(2,1)S(1)}, u32[]{:S(2)}, u32[]{:S(2)}) collective-permute-start(bf16[34,1,128]{2,1,0:T(2,128)(2,1)S(1)} %get-tuple-element.23), channel_id=1, source_target_pairs={{0,1},{1,2},{2,3},{3,4},{4,5},{5,6},{6,7},{7,8},{8,9},{9,10},{10,1... | collective-permute-start | bytes 26120 | tf_op jit(solution)/shard_map/ppermute | solution.py:14
Sparse Core Ops, SparseCore 0:
  147.7 284.5 all-reduce.5
where the time goes:
time: 447 us; the launch traced here: 443 us
  waiting for transfers between devices  284 us (64%)
  local copies, waits for them, and re-layouts  60.4 us (14%)
  starting transfers between devices  38.9 us (9%)
  matrix products  34.1 us (8%)
  between operations  15 us (3%)
  other arithmetic  11 us (2%)
    unnamed x2, waiting for transfers between devices  270 us
    slice x9, local copies, waits for them, and re-layouts, body(): fine_ext[pos_r:pos_r + 2 * half_r - 1:2, pos_c:pos_c + 2 * half_c - 1:2]  35.8 us
    ppermute x4, starting transfers between devices, extended(): lax.ppermute(lax.slice_in_dim(block, block.shape[dim] - width, None, axis...  20.8 us
    ppermute x4, starting transfers between devices, from_behind(): lax.ppermute(value, axis, [(source, source + steps) for source in range(l...  11.7 us
    ppermute x4, waiting for transfers between devices, extended(): lax.ppermute(lax.slice_in_dim(block, 0, width, axis=dim), axis, backward)  10.9 us
    unnamed x102, local copies, waits for them, and re-layouts  9.16 us
  transfers between devices with their start and end apart: 13, of which 6 were waited for; matrix products, arithmetic and copies ran while one was open for 9% of the time, Pallas kernels for 0%

commit v1 on v0

v1 whole, which is shorter than its diff:
```python
import functools
import math

import jax
import jax.numpy as jnp
from jax import lax
from jax.experimental import pallas as pl
from jax.experimental.pallas import tpu as pltpu
from jax.sharding import PartitionSpec as P

BF = jnp.bfloat16
F32 = jnp.float32
NN = (((1,), (0,)), ((), ()))
NT = (((1,), (1,)), ((), ()))
TN = (((0,), (0,)), ((), ()))
LANES = 32


def mm(left, right, dims):
    return lax.dot_general(left, right, dims, preferred_element_type=F32)


def sigmoid(value):
    return 1.0 / (1.0 + jnp.exp(-value))


def weights_kernel(wc, wd, wu, conv_fwd, conv_bwd, up, down_even, down_odd):
    zero = jnp.zeros((128, 128), BF)
    for p in range(3):
        for blk in range(4):
            rows = slice(blk * 128, (blk + 1) * 128)
            conv_fwd[p, rows, 0:128] = wc[p, blk] if blk < 3 else zero
            conv_fwd[p, rows, 128:256] = wc[p, blk - 1] if blk > 0 else zero
            conv_bwd[p, 0:128, rows] = wc[p, 2 - blk] if blk < 3 else zero
            conv_bwd[p, 128:256, rows] = wc[p, 3 - blk] if blk > 0 else zero
    for p in range(2):
        for q in range(2):
            up[:, (2 * p + q) * 128 : (2 * p + q + 1) * 128] = wu[p, q]
    wide = jnp.zeros((128, 256), BF)
    down_even[0:128, 0:256] = wd[1, 1]
    down_even[0:128, 256:512] = wide
    down_even[128:256, 0:256] = wd[1, 2]
    down_even[128:256, 256:512] = wd[1, 0]
    down_odd[0:128, 0:256] = wd[2, 1]
    down_odd[0:128, 256:512] = wide
    down_odd[0:128, 512:768] = wd[0, 1]
    down_odd[0:128, 768:1024] = wide
    down_odd[128:256, 0:256] = wd[2, 2]
    down_odd[128:256, 256:512] = wd[2, 0]
    down_odd[128:256, 512:768] = wd[0, 2]
    down_odd[128:256, 768:1024] = wd[0, 0]


def prepare_weights(w_conv, w_down, w_up):
    shapes = ((3, 512, 256), (3, 256, 512), (256, 512), (256, 512), (256, 1024))
    return pl.pallas_call(
        weights_kernel,
        out_shape=tuple(jax.ShapeDtypeStruct(s, BF) for s in shapes),
        name="weights",
    )(w_conv, w_down, w_up)


CONV_ROWS = ((0, 1, 2), (2, 3, 4), (4, 5, 6), (6, 7, 8))
DOWN_ROWS = ((0, 1, 2, 3, 4), (4, 5, 6, 7, 8), (9, 10, 11, 12, 13), (13, 14, 15, 16, 17))
UP_ROWS = ((0, 1), (2, 3), (4, 5), (6, 7))


def pack(core, ref, conv_acc, down_acc, up_acc):
    k = 0
    for owner in (core, core + 2):
        for row in CONV_ROWS[owner]:
            value = conv_acc[pl.ds(row, 128, stride=9), :]
            ref[:, 32 * k : 32 * k + 32, :] = value.reshape(4, 32, 128).astype(BF)
            k += 1
        for row in DOWN_ROWS[owner]:
            value = down_acc[row % 2, pl.ds(row // 2, 128, stride=9), :]
            ref[:, 32 * k : 32 * k + 32, :] = value.reshape(4, 32, 128).astype(BF)
            k += 1
        for row in UP_ROWS[owner]:
            value = up_acc[pl.ds(row, 128, stride=8), :]
            ref[:, 32 * k : 32 * k + 32, :] = value.reshape(4, 32, 128).astype(BF)
            k += 1


def level_kernel(
    edge, x, c, top, bot, left, right, w_fwd, w_bwd, w_down, w_up, w_even, w_odd,
    out, gx, keep, send,
    conv_acc, down_acc, up_acc, xs, cs, x4, c4, f3, slope, gs, coarse_own, g_own, g4, pre_own, mix,
):
    for ref in (xs, cs):
        ref[:, 0:8, :] = jnp.zeros((ref.shape[0], 8, 128), F32)
        ref[:, 64:72, :] = jnp.zeros((ref.shape[0], 8, 128), F32)
    xs[4:36, 8:64, :] = x[...].astype(F32)
    xs[0:4, 8:64, :] = top[0:4].astype(F32)
    xs[36:39, 8:64, :] = bot[0:3].astype(F32)
    xs[0:39, 4:8, :] = left[0:39].astype(F32)
    xs[0:39, 64:68, :] = right[0:39].astype(F32)
    cs[2:34, 8:64, :] = c[...].astype(F32)
    cs[0:2, 8:64, :] = top[4:6].astype(F32)
    cs[34:36, 8:64, :] = bot[3:5].astype(F32)
    cs[0:36, 4:8, :] = left[39:75].astype(F32)
    cs[0:36, 64:68, :] = right[39:75].astype(F32)
    for r in range(39):
        for k in range(4):
            x4[r, :, k * 128 : (k + 1) * 128] = xs[r, pl.ds(3 + k, 32, stride=2), :].astype(BF)
    x4[39] = jnp.zeros((32, 512), BF)
    for ai in range(18):
        for p in range(2):
            for q in range(2):
                k = 2 * p + q
                c4[ai, :, k * 128 : (k + 1) * 128] = cs[
                    2 * ai + p, pl.ds(4 + q, 32, stride=2), :
                ].astype(BF)

    is_top, is_bot = edge[0] > 0, edge[1] > 0
    is_left, is_right = edge[2] > 0, edge[3] > 0
    half = lax.broadcasted_iota(jnp.int32, (32, 256), 0) - 2
    in_grid = ((half >= 0) | jnp.logical_not(is_left)) & ((half < 28) | jnp.logical_not(is_right))
    in_grid = jnp.where(in_grid, 1.0, 0.0)
    own = jnp.where((half >= 0) & (half < 28), 1.0, 0.0)
    keep_top = jnp.where(is_top, 0.0, 1.0)
    keep_bot = jnp.where(is_bot, 0.0, 1.0)

    for first, count in ((0, 8), (8, 8), (16, 8), (24, 8), (32, 6)):
        pre = None
        for p in range(3):
            window = x4[first + p : first + p + count].reshape(count * 32, 512)
            term = mm(window, w_fwd[p], NN)
            pre = term if pre is None else pre + term
        sig = sigmoid(pre)
        slope[first : first + count] = (sig * (1.0 + pre * (1.0 - sig))).reshape(count, 32, 256)
        fine = ((pre * sig).reshape(count, 32, 256) * in_grid[None]).reshape(count * 32, 256)
        if first == 0 or first == 32:
            row = lax.broadcasted_iota(jnp.int32, (count * 32, 256), 0) // 32
            if first == 0:
                fine = jnp.where(row < 3, fine * keep_top, fine)
            else:
                fine = jnp.where(row >= 3, fine * keep_bot, fine)
        rounded = fine.astype(BF).reshape(count, 32, 256)
        behind = pltpu.roll(fine[:, 128:256], 1, 0).astype(BF).reshape(count, 32, 128)
        f3[first : first + count, :, 0:128] = behind
        f3[first : first + count, :, 128:384] = rounded

    for first, count in ((0, 9), (9, 9)):
        parts = []
        for p in range(3):
            parts.append(
                jnp.concatenate([f3[2 * ai + p] for ai in range(first, first + count)], axis=0)
            )
        cpre = mm(jnp.concatenate(parts, axis=1), w_down[...], NN)
        sig = sigmoid(cpre)
        coarse = cpre * sig
        slope_c = sig * (1.0 + cpre * (1.0 - sig))
        grad_coarse = mm(c4[first : first + count].reshape(count * 32, 512), w_up[...], NT)
        grad = grad_coarse * slope_c
        ahead = pltpu.roll(grad, count * 32 - 1, 0)
        gs[first : first + count, :, 0:256] = grad.astype(BF).reshape(count, 32, 256)
        gs[first : first + count, :, 256:512] = ahead.astype(BF).reshape(count, 32, 256)
        low, high = max(first, 1), min(first + count, 17)
        inner = slice((low - first) * 32, (high - first) * 32)
        coarse_own[low - 1 : high - 1] = (
            (coarse[inner].reshape(high - low, 32, 256) * own[None]).astype(BF)
        )
        g_own[low - 1 : high - 1] = (
            (grad[inner].reshape(high - low, 32, 256) * own[None]).astype(BF)
        )

    for first in (0, 8):
        up = mm(coarse_own[first : first + 8].reshape(256, 256), w_up[...], NN)
        for a in range(first, first + 8):
            for p in range(2):
                for q in range(2):
                    k = 2 * p + q
                    value = up[(a - first) * 32 : (a - first + 1) * 32, k * 128 : (k + 1) * 128]
                    value = value + f3[2 * a + p + 3, :, 128 + q * 128 : 256 + q * 128].astype(F32)
                    mix[2 * a + p, pl.ds(4 + q, 32, stride=2), :] = value
    out[...] = mix[:, 8:64, :].astype(BF)
    coarse_flat = coarse_own[...].reshape(512, 256)
    res = mm(coarse_flat, c4[1:17].reshape(512, 512), TN)
    for k in range(4):
        up_acc[k * 256 : (k + 1) * 256, :] = res[:, k * 128 : (k + 1) * 128]
    g_flat = g_own[...].reshape(512, 256)
    for p in range(3):
        window = jnp.concatenate([f3[2 * a + p + 2] for a in range(16)], axis=0)
        res = mm(window, g_flat, TN)
        for side in range(2):
            down_acc[side, p * 384 : (p + 1) * 384, :] = res[:, side * 128 : (side + 1) * 128]

    for first, count in ((0, 9), (9, 8)):
        for odd in (True, False):
            here = gs[first : first + count].reshape(count * 32, 512)
            below = gs[first + 1 : first + 1 + count].reshape(count * 32, 512)
            if odd:
                spread = mm(jnp.concatenate([here, below], axis=1), w_odd[...], NT)
                cot = c4[first : first + count, :, 256:512].reshape(count * 32, 256)
                at = 2
            else:
                spread = mm(below, w_even[...], NT)
                cot = c4[first + 1 : first + 1 + count, :, 0:256].reshape(count * 32, 256)
                at = 3
            slopes = jnp.concatenate([slope[2 * ai + at] for ai in range(first, first + count)], 0)
            grad = (cot.astype(F32) + spread) * slopes
            grad = (grad.reshape(count, 32, 256) * in_grid[None]).reshape(count * 32, 256)
            if first == 0 and odd:
                row = lax.broadcasted_iota(jnp.int32, (count * 32, 256), 0)
                grad = jnp.where(row < 32, grad * keep_top, grad)
            if first != 0 and not odd:
                row = lax.broadcasted_iota(jnp.int32, (count * 32, 256), 0)
                grad = jnp.where(row >= (count - 1) * 32, grad * keep_bot, grad)
            behind = pltpu.roll(grad[:, 128:256], 1, 0).astype(BF)
            ahead = pltpu.roll(grad[:, 0:128], count * 32 - 1, 0).astype(BF)
            rounded = grad.astype(BF)
            kept = (grad.reshape(count, 32, 256) * own[None]).astype(BF)
            for ai in range(first, first + count):
                g_row = 2 * ai + (0 if odd else 1)
                rows = slice((ai - first) * 32, (ai - first + 1) * 32)
                g4[g_row, :, 0:128] = behind[rows]
                g4[g_row, :, 128:384] = rounded[rows]
                g4[g_row, :, 384:512] = ahead[rows]
                if 1 <= g_row <= 32:
                    pre_own[g_row - 1] = kept[ai - first]

    for first in (0, 8, 16, 24):
        total = None
        for p in range(3):
            window = g4[first + 2 - p : first + 10 - p].reshape(256, 512)
            term = mm(window, w_bwd[p], NT)
            total = term if total is None else total + term
        for i in range(first, first + 8):
            for q in range(2):
                mix[i, pl.ds(4 + q, 32, stride=2), :] = total[
                    (i - first) * 32 : (i - first + 1) * 32, q * 128 : (q + 1) * 128
                ]
    gx[...] = mix[:, 8:64, :].astype(BF)
    flat = pre_own[...].reshape(1024, 256)
    for p in range(3):
        res = mm(flat, x4[p + 3 : p + 35].reshape(1024, 512), TN)
        for q in range(3):
            tap = res[0:128, q * 128 : (q + 1) * 128] + res[128:256, (q + 1) * 128 : (q + 2) * 128]
            conv_acc[(3 * p + q) * 128 : (3 * p + q + 1) * 128, :] = tap.T

    @pl.when(edge[4] == 0)
    def _():
        pack(0, keep, conv_acc, down_acc, up_acc)
        pack(1, send, conv_acc, down_acc, up_acc)

    @pl.when(edge[4] != 0)
    def _():
        pack(1, keep, conv_acc, down_acc, up_acc)
        pack(0, send, conv_acc, down_acc, up_acc)


def level(edge, x, c, top, bot, left, right, weights, w_down):
    w_fwd, w_bwd, w_up, w_even, w_odd = weights
    vmem = pl.BlockSpec(memory_space=pltpu.VMEM)
    return pl.pallas_call(
        level_kernel,
        out_shape=(
            jax.ShapeDtypeStruct((32, 56, 128), BF),
            jax.ShapeDtypeStruct((32, 56, 128), BF),
            jax.ShapeDtypeStruct((4, 640, 128), BF),
            jax.ShapeDtypeStruct((4, 640, 128), BF),
        ),
        in_specs=[pl.BlockSpec(memory_space=pltpu.SMEM)] + [vmem] * 12,
        out_specs=(vmem,) * 4,
        scratch_shapes=[
            pltpu.VMEM((1160, 128), F32),
            pltpu.VMEM((2, 1160, 128), F32),
            pltpu.VMEM((1032, 128), F32),
            pltpu.VMEM((39, 72, 128), F32),
            pltpu.VMEM((36, 72, 128), F32),
            pltpu.VMEM((40, 32, 512), BF),
            pltpu.VMEM((18, 32, 512), BF),
            pltpu.VMEM((38, 32, 384), BF),
            pltpu.VMEM((38, 32, 256), F32),
            pltpu.VMEM((18, 32, 512), BF),
            pltpu.VMEM((16, 32, 256), BF),
            pltpu.VMEM((16, 32, 256), BF),
            pltpu.VMEM((34, 32, 512), BF),
            pltpu.VMEM((32, 32, 256), BF),
            pltpu.VMEM((32, 72, 128), F32),
        ],
        compiler_params=pltpu.CompilerParams(vmem_limit_bytes=56 * 1024 * 1024),
        name="level",
    )(edge, x, c, top, bot, left, right, w_fwd, w_bwd, w_down, w_up, w_even, w_odd)


def chain(axis, step):
    count = lax.axis_size(axis)
    return [(i, i + step) for i in range(count) if 0 <= i + step < count]


def rows_kernel(x_last, x_first, c_last, c_first, down, up):
    down[0:4] = x_last[...]
    down[4:6] = c_last[...]
    up[0:3] = x_first[0:3]
    up[3:5] = c_first[...]


def cols_kernel(
    x_last, x_first, c_last, c_first, top_last, top_first, bot_last, bot_first, right, left
):
    for out, cols, x, c, top, bot in (
        (right, slice(4, 8), x_last, c_last, top_last, bot_last),
        (left, slice(0, 4), x_first, c_first, top_first, bot_first),
    ):
        out[0:4] = top[0:4, cols, :]
        out[4:36] = x[:, cols, :]
        out[36:39] = bot[0:3, cols, :]
        out[39:41] = top[4:6, cols, :]
        out[41:73] = c[:, cols, :]
        out[73:75] = bot[3:5, cols, :]


def row_block(count, at):
    return pl.BlockSpec((count, 56, 128), lambda i: (at, 0, 0))


def col_block(count, at):
    return pl.BlockSpec((count, 8, 128), lambda i: (0, at, 0))


def exchange(x, c):
    down, up = pl.pallas_call(
        rows_kernel,
        grid=(1,),
        out_shape=(
            jax.ShapeDtypeStruct((6, 56, 128), BF),
            jax.ShapeDtypeStruct((5, 56, 128), BF),
        ),
        in_specs=[row_block(4, 7), row_block(4, 0), row_block(2, 15), row_block(2, 0)],
        out_specs=(row_block(6, 0), row_block(5, 0)),
        name="rows",
    )(x, x, c, c)
    top = lax.ppermute(down, "row", chain("row", 1))
    bot = lax.ppermute(up, "row", chain("row", -1))
    whole = pl.BlockSpec((75, 4, 128), lambda i: (0, 0, 0))
    going_right, going_left = pl.pallas_call(
        cols_kernel,
        grid=(1,),
        out_shape=(jax.ShapeDtypeStruct((75, 4, 128), BF),) * 2,
        in_specs=[col_block(n, at) for n in (32, 32, 6, 5) for at in (6, 0)],
        out_specs=(whole, whole),
        name="cols",
    )(x, x, c, c, top, top, bot, bot)
    left = lax.ppermute(going_right, "col", chain("col", 1))
    right = lax.ppermute(going_left, "col", chain("col", -1))
    return top, bot, left, right


def local_terms(inputs, cotangent, w_conv, w_down, w_up):
    n_row, n_col = lax.axis_size("row"), lax.axis_size("col")
    at_row, at_col = lax.axis_index("row"), lax.axis_index("col")
    edge = jnp.stack(
        [at_row == 0, at_row == n_row - 1, at_col == 0, at_col == n_col - 1, at_col % 2 == 1]
    ).astype(jnp.int32)
    weights = prepare_weights(w_conv, w_down, w_up)
    halo = exchange(inputs, cotangent)
    return level(edge, inputs, cotangent, *halo, weights, w_down.reshape(1152, 256))


def spread_kernel(received, out, total):
    total[0:640, :] = jnp.sum(received[...].astype(F32), axis=0)
    for z in range(8):
        for y in range(8):
            first = (y % 2) * 320 + z * 4 + y // 2
            out[8 * z + y, 0:10, :] = total[pl.ds(first, 10, stride=32), :].astype(BF)


def finish_kernel(scale, at, received, conv, down, up):
    rows = jnp.sum(received[...].astype(F32), axis=0)[0:10] * scale
    for which in range(4):

        @pl.when(at[0] == which)
        def _():
            for ref, base, names, size in (
                (conv, 0, CONV_ROWS, 288), (down, 3, DOWN_ROWS, 576), (up, 8, UP_ROWS, 256)
            ):
                start = (base - names[which][0]) * 128 + which * size
                done = 0
                while done < size:
                    row, lane = divmod(start + done, 128)
                    count = min(128 - lane, size - done)
                    ref[0:1, done : done + count] = rows[row : row + 1, lane : lane + count]
                    done += count


def coordinates():
    def device(x, y, z, core):
        return (x * 4 + z // 2) * 32 + (z % 2) * 16 + y * 2 + core

    across = [
        [device(x, y, z, k) for x in range(4)]
        for z in range(8) for y in range(8) for k in range(2)
    ]
    plane = [
        [device(x, y, z, k) for z in range(8) for y in range(8)]
        for x in range(4) for k in range(2)
    ]
    return across, plane


def reduce_owners(keep, send, scale):
    mesh = ("row", "col")
    across, plane = coordinates()
    other = lax.ppermute(send, "col", [(i, i ^ 1) for i in range(32)])
    pair = (keep.astype(F32) + other.astype(F32)).astype(BF)
    got = lax.all_to_all(pair, mesh, 0, 0, axis_index_groups=across, tiled=True)
    spread = pl.pallas_call(
        spread_kernel,
        out_shape=jax.ShapeDtypeStruct((64, 16, 128), BF),
        scratch_shapes=[pltpu.VMEM((672, 128), F32)],
        name="spread",
    )(got)
    got = lax.all_to_all(spread, mesh, 0, 0, axis_index_groups=plane, tiled=True)
    at = (lax.axis_index("col") % 4).astype(jnp.int32).reshape(1)
    sums = pl.pallas_call(
        functools.partial(finish_kernel, scale),
        out_shape=tuple(jax.ShapeDtypeStruct((1, n), F32) for n in (288, 576, 256)),
        in_specs=[
            pl.BlockSpec(memory_space=pltpu.SMEM),
            pl.BlockSpec(memory_space=pltpu.VMEM),
        ],
        name="finish",
    )(at, got)
    return [part.reshape(-1) for part in sums]


def body(inputs, cotangent, w_conv, w_down, w_up):
    output, grad_inputs, keep, send = local_terms(inputs, cotangent, w_conv, w_down, w_up)
    rows, cols, _ = inputs.shape
    scale = 1.0 / math.sqrt(rows * lax.axis_size("row") * cols * lax.axis_size("col"))
    return (output, grad_inputs, *reduce_owners(keep, send, scale))


def solution(mesh):
    grid = P("row", "col", None)
    flat = P(("row", "col"))
    return jax.shard_map(
        body,
        mesh=mesh,
        in_specs=(grid, grid, P(), P(), P()),
        out_specs=(grid, grid, flat, flat, flat),
        check_vma=False,
    )
```

time: 447 us -> 96.4 us (0.22)
  the two profiles are of different devices: /device:TPU:17 before, /device:TPU:8 now
where the time goes in v1:
time: 96.4 us; the launch traced here: 95.8 us
  starting transfers between devices  28.6 us (30%)
  waiting for transfers between devices  24.9 us (26%)
  Pallas kernels  18.9 us (20%)
  blocking collectives  15.6 us (16%)
  other arithmetic  4.33 us (4%)
  local copies, waits for them, and re-layouts  2.69 us (3%)
    all_to_all x1, blocking collectives, reduce_owners(): got = lax.all_to_all(pair, mesh, 0, 0, axis_index_groups=across, tiled=True)  15.6 us
    all_to_all x1, starting transfers between devices, reduce_owners(): lax.all_to_all(spread, mesh, 0, 0, axis_index_groups=plane, tiled=True)  13.3 us
    all_to_all x1, waiting for transfers between devices, reduce_owners(): lax.all_to_all(spread, mesh, 0, 0, axis_index_groups=plane, tiled=True)  13.2 us
    ppermute x1, waiting for transfers between devices, exchange(): bot = lax.ppermute(up, 'row', chain('row', -1))  9.82 us
    pallas_call x1, Pallas kernels, level(): pl.pallas_call(level_kernel, out_shape=(jax.ShapeDtypeStruct((32, 56, 128...  9.09 us
    ppermute x1, starting transfers between devices, exchange(): top = lax.ppermute(down, 'row', chain('row', 1))  6.08 us
    ppermute x1, starting transfers between devices, exchange(): right = lax.ppermute(going_left, 'col', chain('col', -1))  3.64 us
    pallas_call x1, Pallas kernels, prepare_weights(): pl.pallas_call(weights_kernel, out_shape=tuple((jax.ShapeDtypeStruct(s, B...  2.83 us
  transfers between devices with their start and end apart: 6, of which 3 were waited for; matrix products, arithmetic and copies ran while one was open for 1% of the time, Pallas kernels for 3%

profile of v1, /device:TPU:8, one launch (start us, length us, event | category | flops | bytes accessed | tf_op | source)
XLA Modules:
  0.0 95.8 jit_solution(6873588038523982202)
XLA Ops:
  0.6 1.5 %rows.1 = (bf16[6,56,128]{2,1,0:T(8,128)(2,1)}, bf16[5,56,128]{2,1,0:T(8,128)(2,1)}) custom-call(bf16[32,56,128]{2,1,0:T(8,128)(2,1)} %x.1, bf16[32,56,128]{2,1,0:T(8,128)(2,1)} %x.1, bf16[32,56,128]{2,1,0:T(8,128)(2,1)} %c.1, bf16[32,56,128]{2,1,0:T(8,128)(2,1)} %c.1), custom_call_target="tpu_custom_call" | custom-call | tf_op jit(solution)/shard_map/rows/pallas_call | solution.py:324
  2.2 6.1 %collective-permute-start = (bf16[6,56,128]{2,1,0:T(8,128)(2,1)}, bf16[6,56,128]{2,1,0:T(8,128)(2,1)S(1)}, u32[]{:S(2)}, u32[]{:S(2)}) collective-permute-start(bf16[6,56,128]{2,1,0:T(8,128)(2,1)} %get-tuple-element.21), channel_id=1, source_target_pairs={{0,32},{32,64},{64,96},{96,128},{128,160},{160,192},{192,224},{224... | collective-permute-start | bytes 258056 | tf_op jit(solution)/shard_map/ppermute | solution.py:335
  8.2 1.3 %collective-permute-start.1 = (bf16[5,56,128]{2,1,0:T(8,128)(2,1)}, bf16[5,56,128]{2,1,0:T(8,128)(2,1)S(1)}, u32[]{:S(2)}, u32[]{:S(2)}) collective-permute-start(bf16[5,56,128]{2,1,0:T(8,128)(2,1)} %get-tuple-element.22), channel_id=1, source_target_pairs={{32,0},{64,32},{96,64},{128,96},{160,128},{192,160},{224,192},{256... | collective-permute-start | bytes 215048 | tf_op jit(solution)/shard_map/ppermute | solution.py:336
  9.5 9.8 %collective-permute-done.1.bot_last.bot_first.bot = bf16[5,56,128]{2,1,0:T(8,128)(2,1)S(1)} collective-permute-done((bf16[5,56,128]{2,1,0:T(8,128)(2,1)}, bf16[5,56,128]{2,1,0:T(8,128)(2,1)S(1)}, u32[]{:S(2)}, u32[]{:S(2)}) %collective-permute-start.1) | collective-permute-done | bytes 71712 | tf_op jit(solution)/shard_map/ppermute | solution.py:336
  19.4 0.0 copy-start.2
  19.4 0.0 collective-permute-done.top_last.top_first.top
  19.4 0.6 copy-done.2
  20.0 0.0 copy-start.1
  20.0 0.6 copy-done.1
  20.6 1.7 %cols.1 = (bf16[75,4,128]{2,1,0:T(4,128)(2,1)}, bf16[75,4,128]{2,1,0:T(4,128)(2,1)}) custom-call(bf16[32,56,128]{2,1,0:T(8,128)(2,1)} %x.1, bf16[32,56,128]{2,1,0:T(8,128)(2,1)} %x.1, bf16[32,56,128]{2,1,0:T(8,128)(2,1)} %c.1, bf16[32,56,128]{2,1,0:T(8,128)(2,1)} %c.1, bf16[6,56,128]{2,1,0:T(8,128)(2,1)} %copy-done.1, bf16[6,56,128]{2,1,0:T(8,128)(2,1)} %copy-done.1, ...), custom_call_target="tpu_custom_call" | custom-call | tf_op jit(solution)/shard_map/cols/pallas_call | solution.py:338
  22.3 1.9 %collective-permute-start.2 = (bf16[75,4,128]{2,1,0:T(4,128)(2,1)}, bf16[75,4,128]{2,1,0:T(4,128)(2,1)S(1)}, u32[]{:S(2)}, u32[]{:S(2)}) collective-permute-start(bf16[75,4,128]{2,1,0:T(4,128)(2,1)} %get-tuple-element.23), channel_id=1, source_target_pairs={{0,1},{1,2},{2,3},{3,4},{4,5},{5,6},{6,7},{7,8},{8,9},{9,10},{10,1... | collective-permute-start | bytes 230408 | tf_op jit(solution)/shard_map/ppermute | solution.py:346
  24.2 3.6 %collective-permute-start.3 = (bf16[75,4,128]{2,1,0:T(4,128)(2,1)}, bf16[75,4,128]{2,1,0:T(4,128)(2,1)S(1)}, u32[]{:S(2)}, u32[]{:S(2)}) collective-permute-start(bf16[75,4,128]{2,1,0:T(4,128)(2,1)} %get-tuple-element.24), channel_id=1, source_target_pairs={{1,0},{2,1},{3,2},{4,3},{5,4},{6,5},{7,6},{8,7},{9,8},{10,9},{11,1... | collective-permute-start | bytes 230408 | tf_op jit(solution)/shard_map/ppermute | solution.py:347
  27.9 0.1 stack.23
  28.0 0.5 convert_element_type.12.edge
  28.5 2.8 %weights.1 = (bf16[3,512,256]{2,1,0:T(8,128)(2,1)}, bf16[3,256,512]{2,1,0:T(8,128)(2,1)}, bf16[256,512]{1,0:T(8,128)(2,1)}, bf16[256,512]{1,0:T(8,128)(2,1)}, bf16[256,1024]{1,0:T(8,128)(2,1)}) custom-call(bf16[3,3,128,128]{3,2,1,0:T(8,128)(2,1)} %wc.1, bf16[3,3,128,256]{3,2,1,0:T(8,128)(2,1)} %wd.1, bf16[2,2,256,128]{3,2,1,0:T(8,128)(2,1)} %wu.1), custom_call_target="tpu_custom_call" | custom-call | tf_op jit(solution)/shard_map/weights/pallas_call | solution.py:56
  31.3 0.0 collective-permute-done.2.left
  31.3 0.0 copy-start.3
  31.3 0.0 collective-permute-done.3.right
  31.3 0.0 copy-start.4
  31.4 0.6 copy-done.3
  32.0 0.0 copy-done.4
  32.0 9.1 %level.1 = (bf16[32,56,128]{2,1,0:T(8,128)(2,1)}, bf16[32,56,128]{2,1,0:T(8,128)(2,1)}, bf16[4,640,128]{2,1,0:T(8,128)(2,1)}, bf16[4,640,128]{2,1,0:T(8,128)(2,1)}) custom-call(s32[5]{0:T(128)} %convert_element_type.12.edge, bf16[32,56,128]{2,1,0:T(8,128)(2,1)} %x.1, bf16[32,56,128]{2,1,0:T(8,128)(2,1)} %c.1, bf16[6,56,128]{2,1,0:T(8,128)(2,1)} %copy-done.1, ...), custom_call_target="tpu_custom_call" | custom-call | tf_op jit(solution)/shard_map/level/pallas_call | solution.py:256
  41.1 2.3 %collective-permute-start.4 = (bf16[4,640,128]{2,1,0:T(8,128)(2,1)}, bf16[4,640,128]{2,1,0:T(8,128)(2,1)S(1)}, u32[]{:S(2)}, u32[]{:S(2)}) collective-permute-start(bf16[4,640,128]{2,1,0:T(8,128)(2,1)} %get-tuple-element.33), channel_id=1, source_target_pairs={{0,1},{1,0},{2,3},{3,2},{4,5},{5,4},{6,7},{7,6},{8,9},{9,8},{10,11... | collective-permute-start | bytes 1966088 | tf_op jit(solution)/shard_map/ppermute | solution.py:406
  43.4 1.9 %collective-permute-done.4 = bf16[4,640,128]{2,1,0:T(8,128)(2,1)S(1)} collective-permute-done((bf16[4,640,128]{2,1,0:T(8,128)(2,1)}, bf16[4,640,128]{2,1,0:T(8,128)(2,1)S(1)}, u32[]{:S(2)}, u32[]{:S(2)}) %collective-permute-start.4) | collective-permute-done | bytes 655392 | tf_op jit(solution)/shard_map/ppermute | solution.py:406
  45.3 1.3 %add_convert_fusion = bf16[4,640,128]{2,1,0:T(8,128)(2,1)S(1)} fusion(bf16[4,640,128]{2,1,0:T(8,128)(2,1)S(1)} %collective-permute-done.4, bf16[4,640,128]{2,1,0:T(8,128)(2,1)} %get-tuple-element.32), kind=kLoop, calls=%fused_computation | loop fusion | flops 1310720 | bytes 1966080 | tf_op jit(solution)/shard_map/convert_element_type | solution.py:407
  46.6 15.6 %all_to_all.10.received = bf16[4,640,128]{2,1,0:T(8,128)(2,1)} all-to-all(bf16[4,640,128]{2,1,0:T(8,128)(2,1)S(1)} %add_convert_fusion), channel_id=1, replica_groups={{0,128,256,384},{1,129,257,385},{2,130,258,386},{3,131,259,387},{4,132,..., dimensions={0} | all-to-all | bytes 1310720 | tf_op jit(solution)/shard_map/all_to_all | solution.py:408
  62.2 2.1 %spread.1 = bf16[64,16,128]{2,1,0:T(8,128)(2,1)} custom-call(bf16[4,640,128]{2,1,0:T(8,128)(2,1)} %all_to_all.10.received), custom_call_target="tpu_custom_call" | custom-call | tf_op jit(solution)/shard_map/spread/pallas_call | solution.py:409
  64.3 13.3 %all-to-all-start.1 = ((bf16[64,16,128]{2,1,0:T(8,128)(2,1)}), bf16[64,16,128]{2,1,0:T(8,128)(2,1)S(1)}, u32[]{:S(2)}, u32[]{:S(2)}) async-start(bf16[64,16,128]{2,1,0:T(8,128)(2,1)} %spread.1), calls=%async_computation.1 | async-start | bytes 524288 | tf_op jit(solution)/shard_map/all_to_all | solution.py:415
  77.6 13.2 %all-to-all-done.1.received = bf16[64,16,128]{2,1,0:T(8,128)(2,1)S(1)} async-done(((bf16[64,16,128]{2,1,0:T(8,128)(2,1)}), bf16[64,16,128]{2,1,0:T(8,128)(2,1)S(1)}, u32[]{:S(2)}, u32[]{:S(2)}) %all-to-all-start.1) | async-done | bytes 262176 | tf_op jit(solution)/shard_map/all_to_all | solution.py:415
  90.8 0.0 copy-start
  90.8 0.7 copy-done
  91.5 1.7 %finish.1 = (f32[1,288]{1,0:T(1,128)}, f32[1,576]{1,0:T(1,128)}, f32[1,256]{1,0:T(1,128)}) custom-call(s32[1]{0:T(128)} %bitcast.6.at, bf16[64,16,128]{2,1,0:T(8,128)(2,1)} %copy-done), custom_call_target="tpu_custom_call" | custom-call | tf_op jit(solution)/shard_map/finish/pallas_call | solution.py:417
  93.2 1.3 %reduce = f32[288]{0:T(512)} reduce(f32[1,288]{1,0:T(1,128)} %get-tuple-element.34, f32[]{:T(128)} %constant.40), dimensions={0}, to_apply=%get-tuple-element.34.reduce_sub_computation | reduce | bytes 2308 | tf_op jit(solution)/shard_map/finish/pallas_call | solution.py:417
  94.5 1.3 %reduce.1 = f32[576]{0:T(1024)} reduce(f32[1,576]{1,0:T(1,128)} %get-tuple-element.35, f32[]{:T(128)} %constant.40), dimensions={0}, to_apply=%get-tuple-element.35.reduce_sub_computation | reduce | bytes 4612 | tf_op jit(solution)/shard_map/finish/pallas_call | solution.py:417
Async XLA Ops:
  2.2 17.2 %collective-permute-start = (bf16[6,56,128]{2,1,0:T(8,128)(2,1)}, bf16[6,56,128]{2,1,0:T(8,128)(2,1)S(1)}, u32[]{:S(2)}, u32[]{:S(2)}) collective-permute-start(bf16[6,56,128]{2,1,0:T(8,128)(2,1)} %get-tuple-element.21), channel_id=1, source_target_pairs={{0,32},{32,64},{64,96},{96,128},{128,160},{160,192},{192,224},{224... | collective-permute-start | bytes 258056 | tf_op jit(solution)/shard_map/ppermute | solution.py:335
  8.2 11.1 %collective-permute-start.1 = (bf16[5,56,128]{2,1,0:T(8,128)(2,1)}, bf16[5,56,128]{2,1,0:T(8,128)(2,1)S(1)}, u32[]{:S(2)}, u32[]{:S(2)}) collective-permute-start(bf16[5,56,128]{2,1,0:T(8,128)(2,1)} %get-tuple-element.22), channel_id=1, source_target_pairs={{32,0},{64,32},{96,64},{128,96},{160,128},{192,160},{224,192},{256... | collective-permute-start | bytes 215048 | tf_op jit(solution)/shard_map/ppermute | solution.py:336
  19.4 0.6 copy-start.2
  20.0 0.6 copy-start.1
  22.3 9.0 %collective-permute-start.2 = (bf16[75,4,128]{2,1,0:T(4,128)(2,1)}, bf16[75,4,128]{2,1,0:T(4,128)(2,1)S(1)}, u32[]{:S(2)}, u32[]{:S(2)}) collective-permute-start(bf16[75,4,128]{2,1,0:T(4,128)(2,1)} %get-tuple-element.23), channel_id=1, source_target_pairs={{0,1},{1,2},{2,3},{3,4},{4,5},{5,6},{6,7},{7,8},{8,9},{9,10},{10,1... | collective-permute-start | bytes 230408 | tf_op jit(solution)/shard_map/ppermute | solution.py:346
  24.2 7.1 %collective-permute-start.3 = (bf16[75,4,128]{2,1,0:T(4,128)(2,1)}, bf16[75,4,128]{2,1,0:T(4,128)(2,1)S(1)}, u32[]{:S(2)}, u32[]{:S(2)}) collective-permute-start(bf16[75,4,128]{2,1,0:T(4,128)(2,1)} %get-tuple-element.24), channel_id=1, source_target_pairs={{1,0},{2,1},{3,2},{4,3},{5,4},{6,5},{7,6},{8,7},{9,8},{10,9},{11,1... | collective-permute-start | bytes 230408 | tf_op jit(solution)/shard_map/ppermute | solution.py:347
  31.3 0.6 copy-start.3
  31.3 0.7 copy-start.4
  41.1 4.3 %collective-permute-start.4 = (bf16[4,640,128]{2,1,0:T(8,128)(2,1)}, bf16[4,640,128]{2,1,0:T(8,128)(2,1)S(1)}, u32[]{:S(2)}, u32[]{:S(2)}) collective-permute-start(bf16[4,640,128]{2,1,0:T(8,128)(2,1)} %get-tuple-element.33), channel_id=1, source_target_pairs={{0,1},{1,0},{2,3},{3,2},{4,5},{5,4},{6,7},{7,6},{8,9},{9,8},{10,11... | collective-permute-start | bytes 1966088 | tf_op jit(solution)/shard_map/ppermute | solution.py:406
  64.3 26.5 %all-to-all-start.1 = ((bf16[64,16,128]{2,1,0:T(8,128)(2,1)}), bf16[64,16,128]{2,1,0:T(8,128)(2,1)S(1)}, u32[]{:S(2)}, u32[]{:S(2)}) async-start(bf16[64,16,128]{2,1,0:T(8,128)(2,1)} %spread.1), calls=%async_computation.1 | async-start | bytes 524288 | tf_op jit(solution)/shard_map/all_to_all | solution.py:415
  90.8 0.7 copy-start

commit v2 on v1

--- a/solution.py
+++ b/solution.py
@@ -14,6 +14,18 @@
 NT = (((1,), (1,)), ((), ()))
 TN = (((0,), (0,)), ((), ()))
 LANES = 32
+
+
+def held(shape, dtype=BF):
+    return pltpu.VMEM(shape, dtype)
+
+
+def far(*arrays):
+    return tuple(pltpu.with_memory_space_constraint(a, pltpu.HBM) for a in arrays)
+
+
+def pin(*arrays):
+    return tuple(pltpu.with_memory_space_constraint(a, pltpu.VMEM) for a in arrays)
 
 
 def mm(left, right, dims):
@@ -258,8 +270,8 @@
         out_shape=(
             jax.ShapeDtypeStruct((32, 56, 128), BF),
             jax.ShapeDtypeStruct((32, 56, 128), BF),
-            jax.ShapeDtypeStruct((4, 640, 128), BF),
-            jax.ShapeDtypeStruct((4, 640, 128), BF),
+            held((4, 640, 128)),
+            held((4, 640, 128)),
         ),
         in_specs=[pl.BlockSpec(memory_space=pltpu.SMEM)] + [vmem] * 12,
         out_specs=(vmem,) * 4,
@@ -280,9 +292,11 @@
             pltpu.VMEM((32, 32, 256), BF),
             pltpu.VMEM((32, 72, 128), F32),
         ],
-        compiler_params=pltpu.CompilerParams(vmem_limit_bytes=56 * 1024 * 1024),
+        compiler_params=pltpu.CompilerParams(vmem_limit_bytes=18 * 1024 * 1024),
         name="level",
-    )(edge, x, c, top, bot, left, right, w_fwd, w_bwd, w_down, w_up, w_even, w_odd)
+    )(
+        edge, x, c, top, bot, *pin(left, right), w_fwd, w_bwd, w_down, w_up, w_even, w_odd
+    )
 
 
 def chain(axis, step):
@@ -298,17 +312,17 @@
 
 
 def cols_kernel(
-    x_last, x_first, c_last, c_first, top_last, top_first, bot_last, bot_first, right, left
+    x_last, x_first, c_last, c_first, top, bot, w_odd, right, left
 ):
-    for out, cols, x, c, top, bot in (
-        (right, slice(4, 8), x_last, c_last, top_last, bot_last),
-        (left, slice(0, 4), x_first, c_first, top_first, bot_first),
+    for out, cols, near, x, c in (
+        (right, slice(52, 56), slice(4, 8), x_last, c_last),
+        (left, slice(0, 4), slice(0, 4), x_first, c_first),
     ):
         out[0:4] = top[0:4, cols, :]
-        out[4:36] = x[:, cols, :]
+        out[4:36] = x[:, near, :]
         out[36:39] = bot[0:3, cols, :]
         out[39:41] = top[4:6, cols, :]
-        out[41:73] = c[:, cols, :]
+        out[41:73] = c[:, near, :]
         out[73:75] = bot[3:5, cols, :]
 
 
@@ -320,7 +334,7 @@
     return pl.BlockSpec((count, 8, 128), lambda i: (0, at, 0))
 
 
-def exchange(x, c):
+def exchange(x, c, w_odd):
     down, up = pl.pallas_call(
         rows_kernel,
         grid=(1,),
@@ -331,7 +345,7 @@
         in_specs=[row_block(4, 7), row_block(4, 0), row_block(2, 15), row_block(2, 0)],
         out_specs=(row_block(6, 0), row_block(5, 0)),
         name="rows",
-    )(x, x, c, c)
+    )(*far(x, x, c, c))
     top = lax.ppermute(down, "row", chain("row", 1))
     bot = lax.ppermute(up, "row", chain("row", -1))
     whole = pl.BlockSpec((75, 4, 128), lambda i: (0, 0, 0))
@@ -339,10 +353,11 @@
         cols_kernel,
         grid=(1,),
         out_shape=(jax.ShapeDtypeStruct((75, 4, 128), BF),) * 2,
-        in_specs=[col_block(n, at) for n in (32, 32, 6, 5) for at in (6, 0)],
+        in_specs=[col_block(32, at) for at in (6, 0, 6, 0)]
+        + [row_block(6, 0), row_block(5, 0), pl.BlockSpec(memory_space=pl.ANY)],
         out_specs=(whole, whole),
         name="cols",
-    )(x, x, c, c, top, top, bot, bot)
+    )(*far(x, x, c, c), *pin(top, bot), *far(w_odd))
     left = lax.ppermute(going_right, "col", chain("col", 1))
     right = lax.ppermute(going_left, "col", chain("col", -1))
     return top, bot, left, right
@@ -351,27 +366,28 @@
 def local_terms(inputs, cotangent, w_conv, w_down, w_up):
     n_row, n_col = lax.axis_size("row"), lax.axis_size("col")
     at_row, at_col = lax.axis_index("row"), lax.axis_index("col")
-    edge = jnp.stack(
-        [at_row == 0, at_row == n_row - 1, at_col == 0, at_col == n_col - 1, at_col % 2 == 1]
+    edge = jnp.array(
+        [at_row == 0, at_row == n_row - 1, at_col == 0, at_col == n_col - 1, at_col & 1, at_col & 3]
     ).astype(jnp.int32)
     weights = prepare_weights(w_conv, w_down, w_up)
-    halo = exchange(inputs, cotangent)
-    return level(edge, inputs, cotangent, *halo, weights, w_down.reshape(1152, 256))
-
-
-def spread_kernel(received, out, total):
+    halo = exchange(inputs, cotangent, weights[4])
+    return edge, level(edge, inputs, cotangent, *halo, weights, w_down.reshape(1152, 256))
+
+
+def spread_kernel(received, out, spare, total):
     total[0:640, :] = jnp.sum(received[...].astype(F32), axis=0)
+    spare[...] = jnp.zeros((8, 128), F32)
     for z in range(8):
         for y in range(8):
             first = (y % 2) * 320 + z * 4 + y // 2
-            out[8 * z + y, 0:10, :] = total[pl.ds(first, 10, stride=32), :].astype(BF)
-
-
-def finish_kernel(scale, at, received, conv, down, up):
-    rows = jnp.sum(received[...].astype(F32), axis=0)[0:10] * scale
+            out[8 * z + y] = total[pl.ds(first, 10, stride=32), :].astype(BF)
+
+
+def finish_kernel(scale, edge, received, conv, down, up):
+    rows = jnp.sum(received[...].astype(F32), axis=0) * scale
     for which in range(4):
 
-        @pl.when(at[0] == which)
+        @pl.when(edge[5] == which)
         def _():
             for ref, base, names, size in (
                 (conv, 0, CONV_ROWS, 288), (down, 3, DOWN_ROWS, 576), (up, 8, UP_ROWS, 256)
@@ -381,7 +397,7 @@
                 while done < size:
                     row, lane = divmod(start + done, 128)
                     count = min(128 - lane, size - done)
-                    ref[0:1, done : done + count] = rows[row : row + 1, lane : lane + count]
+                    ref[pl.ds(done, count)] = rows[row, lane : lane + count]
                     done += count
 
 
@@ -400,37 +416,37 @@
     return across, plane
 
 
-def reduce_owners(keep, send, scale):
+def reduce_owners(edge, keep, send, scale):
     mesh = ("row", "col")
     across, plane = coordinates()
     other = lax.ppermute(send, "col", [(i, i ^ 1) for i in range(32)])
     pair = (keep.astype(F32) + other.astype(F32)).astype(BF)
     got = lax.all_to_all(pair, mesh, 0, 0, axis_index_groups=across, tiled=True)
-    spread = pl.pallas_call(
+    spread, _ = pl.pallas_call(
         spread_kernel,
-        out_shape=jax.ShapeDtypeStruct((64, 16, 128), BF),
+        out_shape=(held((64, 10, 128)), held((8, 128), F32)),
         scratch_shapes=[pltpu.VMEM((672, 128), F32)],
         name="spread",
-    )(got)
+    )(*pin(got))
     got = lax.all_to_all(spread, mesh, 0, 0, axis_index_groups=plane, tiled=True)
-    at = (lax.axis_index("col") % 4).astype(jnp.int32).reshape(1)
     sums = pl.pallas_call(
         functools.partial(finish_kernel, scale),
-        out_shape=tuple(jax.ShapeDtypeStruct((1, n), F32) for n in (288, 576, 256)),
+        out_shape=tuple(jax.ShapeDtypeStruct((n,), F32) for n in (288, 576, 256)),
         in_specs=[
             pl.BlockSpec(memory_space=pltpu.SMEM),
             pl.BlockSpec(memory_space=pltpu.VMEM),
         ],
         name="finish",
-    )(at, got)
-    return [part.reshape(-1) for part in sums]
+    )(edge, *pin(got))
+    return sums
 
 
 def body(inputs, cotangent, w_conv, w_down, w_up):
-    output, grad_inputs, keep, send = local_terms(inputs, cotangent, w_conv, w_down, w_up)
+    edge, parts = local_terms(inputs, cotangent, w_conv, w_down, w_up)
+    output, grad_inputs, keep, send = parts
     rows, cols, _ = inputs.shape
     scale = 1.0 / math.sqrt(rows * lax.axis_size("row") * cols * lax.axis_size("col"))
-    return (output, grad_inputs, *reduce_owners(keep, send, scale))
+    return (output, grad_inputs, *reduce_owners(edge, keep, send, scale))
 
 
 def solution(mesh):

time: 96.4 us -> 88.1 us (0.914)
  blocking collectives: 15.6 us -> 41.6 us
  waiting for transfers between devices: 24.9 us -> 10.8 us
  starting transfers between devices: 28.6 us -> 16.5 us
  other arithmetic: 4.33 us -> 0.17 us
  Pallas kernels: 18.9 us -> 15.4 us
    all_to_all x0 -> x1, blocking collectives: none -> 26.1 us  [reduce_owners(): lax.all_to_all(spread, mesh, 0, 0, axis_index_groups=plane, tiled=True)]
    all_to_all x1 -> x0, starting transfers between devices: 13.3 us -> none  [reduce_owners(): lax.all_to_all(spread, mesh, 0, 0, axis_index_groups=plane, tiled=True)]
    all_to_all x1 -> x0, waiting for transfers between devices: 13.2 us -> none  [reduce_owners(): lax.all_to_all(spread, mesh, 0, 0, axis_index_groups=plane, tiled=True)]
    ppermute x1, waiting for transfers between devices: 9.82 us -> 6.94 us  [exchange(): bot = lax.ppermute(up, 'row', chain('row', -1))]
    pallas_call x2 -> x0, other arithmetic: 2.55 us -> none  [reduce_owners(): pl.pallas_call(functools.partial(finish_kernel, scale), out_shape=tuple((...]
    pallas_call x1, Pallas kernels: 9.09 us -> 7.03 us  [level(): pl.pallas_call(level_kernel, out_shape=(jax.ShapeDtypeStruct((32, 56, 128...]
    ppermute x1, waiting for transfers between devices: 0.01 us -> 1.97 us  [exchange(): right = lax.ppermute(going_left, 'col', chain('col', -1))]
    pallas_call x1, Pallas kernels: 2.09 us -> 0.72 us  [reduce_owners(): pl.pallas_call(spread_kernel, out_shape=(held((64, 10, 128)), held((8, 12...]
  transfers between devices with their start and end apart: 6 -> 5, of which waited for: 3 -> 4; matrix products, arithmetic and copies ran while one was open for 1% -> 0% of each run, Pallas kernels for 3% -> 3%
where the time goes in v2:
time: 88.1 us; the launch traced here: 87.6 us
  blocking collectives  41.6 us (47%)
  starting transfers between devices  16.5 us (19%)
  Pallas kernels  15.4 us (17%)
  waiting for transfers between devices  10.8 us (12%)
  local copies, waits for them, and re-layouts  2.37 us (3%)
    all_to_all x1, blocking collectives, reduce_owners(): lax.all_to_all(spread, mesh, 0, 0, axis_index_groups=plane, tiled=True)  26.1 us
    all_to_all x1, blocking collectives, reduce_owners(): got = lax.all_to_all(pair, mesh, 0, 0, axis_index_groups=across, tiled=True)  15.5 us
    pallas_call x1, Pallas kernels, level(): pl.pallas_call(level_kernel, out_shape=(jax.ShapeDtypeStruct((32, 56, 128...  7.03 us
    ppermute x1, waiting for transfers between devices, exchange(): bot = lax.ppermute(up, 'row', chain('row', -1))  6.94 us
    ppermute x1, starting transfers between devices, exchange(): top = lax.ppermute(down, 'row', chain('row', 1))  6.08 us
    ppermute x1, starting transfers between devices, exchange(): right = lax.ppermute(going_left, 'col', chain('col', -1))  3.64 us
    ppermute x1, starting transfers between devices, reduce_owners(): other = lax.ppermute(send, 'col', [(i, i ^ 1) for i in range(32)])  3.55 us
    pallas_call x1, Pallas kernels, prepare_weights(): pl.pallas_call(weights_kernel, out_shape=tuple((jax.ShapeDtypeStruct(s, B...  2.88 us
  transfers between devices with their start and end apart: 5, of which 4 were waited for; matrix products, arithmetic and copies ran while one was open for 0% of the time, Pallas kernels for 3%

profile of v2, /device:TPU:8, one launch (start us, length us, event | category | flops | bytes accessed | tf_op | source)
XLA Modules:
  0.0 87.6 jit_solution(5792229739941490793)
XLA Ops:
  0.6 1.5 %rows.1 = (bf16[6,56,128]{2,1,0:T(8,128)(2,1)}, bf16[5,56,128]{2,1,0:T(8,128)(2,1)}) custom-call(bf16[32,56,128]{2,1,0:T(8,128)(2,1)} %x.1, bf16[32,56,128]{2,1,0:T(8,128)(2,1)} %x.1, bf16[32,56,128]{2,1,0:T(8,128)(2,1)} %c.1, bf16[32,56,128]{2,1,0:T(8,128)(2,1)} %c.1), custom_call_target="tpu_custom_call" | custom-call | tf_op jit(solution)/shard_map/rows/pallas_call | solution.py:338
  2.2 6.1 %collective-permute-start = (bf16[6,56,128]{2,1,0:T(8,128)(2,1)}, bf16[6,56,128]{2,1,0:T(8,128)(2,1)S(1)}, u32[]{:S(2)}, u32[]{:S(2)}) collective-permute-start(bf16[6,56,128]{2,1,0:T(8,128)(2,1)} %get-tuple-element.22), channel_id=1, source_target_pairs={{0,32},{32,64},{64,96},{96,128},{128,160},{160,192},{192,224},{224... | collective-permute-start | bytes 258056 | tf_op jit(solution)/shard_map/ppermute | solution.py:349
  8.3 1.3 %collective-permute-start.1 = (bf16[5,56,128]{2,1,0:T(8,128)(2,1)}, bf16[5,56,128]{2,1,0:T(8,128)(2,1)S(1)}, u32[]{:S(2)}, u32[]{:S(2)}) collective-permute-start(bf16[5,56,128]{2,1,0:T(8,128)(2,1)} %get-tuple-element.23), channel_id=1, source_target_pairs={{32,0},{64,32},{96,64},{128,96},{160,128},{192,160},{224,192},{256... | collective-permute-start | bytes 215048 | tf_op jit(solution)/shard_map/ppermute | solution.py:350
  9.6 2.9 %weights.1 = (bf16[3,512,256]{2,1,0:T(8,128)(2,1)}, bf16[3,256,512]{2,1,0:T(8,128)(2,1)}, bf16[256,512]{1,0:T(8,128)(2,1)}, bf16[256,512]{1,0:T(8,128)(2,1)}, bf16[256,1024]{1,0:T(8,128)(2,1)}) custom-call(bf16[3,3,128,128]{3,2,1,0:T(8,128)(2,1)} %wc.1, bf16[3,3,128,256]{3,2,1,0:T(8,128)(2,1)} %wd.1, bf16[2,2,256,128]{3,2,1,0:T(8,128)(2,1)} %wu.1), custom_call_target="tpu_custom_call" | custom-call | tf_op jit(solution)/shard_map/weights/pallas_call | solution.py:68
  12.4 6.9 %collective-permute-done.1.bot = bf16[5,56,128]{2,1,0:T(8,128)(2,1)S(1)} collective-permute-done((bf16[5,56,128]{2,1,0:T(8,128)(2,1)}, bf16[5,56,128]{2,1,0:T(8,128)(2,1)S(1)}, u32[]{:S(2)}, u32[]{:S(2)}) %collective-permute-start.1) | collective-permute-done | bytes 71712 | tf_op jit(solution)/shard_map/ppermute | solution.py:350
  19.4 0.0 collective-permute-done.top
  19.4 0.0 copy-start
  19.4 0.0 copy-start.1
  19.4 0.0 copy-start.2
  19.4 0.0 copy-start.3
  19.4 0.0 copy-start.6
  19.4 0.0 copy-start.7
  19.4 1.8 %cols.1 = (bf16[75,4,128]{2,1,0:T(4,128)(2,1)}, bf16[75,4,128]{2,1,0:T(4,128)(2,1)}) custom-call(bf16[32,56,128]{2,1,0:T(8,128)(2,1)} %x.1, bf16[32,56,128]{2,1,0:T(8,128)(2,1)} %x.1, bf16[32,56,128]{2,1,0:T(8,128)(2,1)} %c.1, bf16[32,56,128]{2,1,0:T(8,128)(2,1)} %c.1, bf16[6,56,128]{2,1,0:T(8,128)(2,1)S(1)} %collective-permute-done.top, ...), custom_call_target="tpu_custom_call" | custom-call | tf_op jit(solution)/shard_map/cols/pallas_call | solution.py:352
  21.2 1.9 %collective-permute-start.2 = (bf16[75,4,128]{2,1,0:T(4,128)(2,1)}, bf16[75,4,128]{2,1,0:T(4,128)(2,1)S(1)}, u32[]{:S(2)}, u32[]{:S(2)}) collective-permute-start(bf16[75,4,128]{2,1,0:T(4,128)(2,1)} %get-tuple-element.25), channel_id=1, source_target_pairs={{0,1},{1,2},{2,3},{3,4},{4,5},{5,6},{6,7},{7,8},{8,9},{9,10},{10,1... | collective-permute-start | bytes 230408 | tf_op jit(solution)/shard_map/ppermute | solution.py:361
  23.2 3.6 %collective-permute-start.3 = (bf16[75,4,128]{2,1,0:T(4,128)(2,1)}, bf16[75,4,128]{2,1,0:T(4,128)(2,1)S(1)}, u32[]{:S(2)}, u32[]{:S(2)}) collective-permute-start(bf16[75,4,128]{2,1,0:T(4,128)(2,1)} %get-tuple-element.26), channel_id=1, source_target_pairs={{1,0},{2,1},{3,2},{4,3},{5,4},{6,5},{7,6},{8,7},{9,8},{10,9},{11,1... | collective-permute-start | bytes 230408 | tf_op jit(solution)/shard_map/ppermute | solution.py:362
  26.8 0.1 concatenate.3.edge
  26.9 0.0 copy-start.8
  26.9 0.2 collective-permute-done.2.left
  27.1 2.0 %collective-permute-done.3.right = bf16[75,4,128]{2,1,0:T(4,128)(2,1)S(1)} collective-permute-done((bf16[75,4,128]{2,1,0:T(4,128)(2,1)}, bf16[75,4,128]{2,1,0:T(4,128)(2,1)S(1)}, u32[]{:S(2)}, u32[]{:S(2)}) %collective-permute-start.3) | collective-permute-done | bytes 76832 | tf_op jit(solution)/shard_map/ppermute | solution.py:362
  29.1 0.0 copy-done
  29.1 0.0 copy-done.1
  29.1 0.0 copy-done.2
  29.1 0.0 copy-done.3
  29.1 0.0 copy-done.6
  29.1 0.0 copy-done.7
  29.1 0.0 copy-start.4
  29.2 1.1 %copy-done.4 = bf16[3,512,256]{2,1,0:T(8,128)(2,1)S(1)} copy-done((bf16[3,512,256]{2,1,0:T(8,128)(2,1)S(1)}, bf16[3,512,256]{2,1,0:T(8,128)(2,1)}, u32[]{:S(2)}) %copy-start.4) | copy-done | bytes 786456
  30.3 0.0 copy-start.5
  30.3 1.1 %copy-done.5 = bf16[3,256,512]{2,1,0:T(8,128)(2,1)S(1)} copy-done((bf16[3,256,512]{2,1,0:T(8,128)(2,1)S(1)}, bf16[3,256,512]{2,1,0:T(8,128)(2,1)}, u32[]{:S(2)}) %copy-start.5) | copy-done | bytes 786456
  31.4 7.0 %level.1 = (bf16[32,56,128]{2,1,0:T(8,128)(2,1)}, bf16[32,56,128]{2,1,0:T(8,128)(2,1)}, bf16[4,640,128]{2,1,0:T(8,128)(2,1)S(1)}, bf16[4,640,128]{2,1,0:T(8,128)(2,1)S(1)}) custom-call(s32[6]{0:T(128)S(1)} %concatenate.3.edge, bf16[32,56,128]{2,1,0:T(8,128)(2,1)S(1)} %copy-done, bf16[32,56,128]{2,1,0:T(8,128)(2,1)S(1)} %copy-done.1, ...), custom_call_target="tpu_custom_call" | custom-call | tf_op jit(solution)/shard_map/level/pallas_call | solution.py:268
  38.4 0.0 copy-done.8
  38.5 3.6 %collective-permute-start.4 = (bf16[4,640,128]{2,1,0:T(8,128)(2,1)S(1)}, bf16[4,640,128]{2,1,0:T(8,128)(2,1)S(1)}, u32[]{:S(2)}, u32[]{:S(2)}) collective-permute-start(bf16[4,640,128]{2,1,0:T(8,128)(2,1)S(1)} %get-tuple-element.34), channel_id=1, source_target_pairs={{0,1},{1,0},{2,3},{3,2},{4,5},{5,4},{6,7},{7,6},{8,9},{9,8},{10,11... | collective-permute-start | bytes 1966088 | tf_op jit(solution)/shard_map/ppermute | solution.py:422
  42.0 1.7 %collective-permute-done.4 = bf16[4,640,128]{2,1,0:T(8,128)(2,1)S(1)} collective-permute-done((bf16[4,640,128]{2,1,0:T(8,128)(2,1)S(1)}, bf16[4,640,128]{2,1,0:T(8,128)(2,1)S(1)}, u32[]{:S(2)}, u32[]{:S(2)}) %collective-permute-start.4) | collective-permute-done | bytes 655392 | tf_op jit(solution)/shard_map/ppermute | solution.py:422
  43.7 0.2 add_convert_fusion
  43.9 15.5 %all_to_all.10.received = bf16[4,640,128]{2,1,0:T(8,128)(2,1)S(1)} all-to-all(bf16[4,640,128]{2,1,0:T(8,128)(2,1)S(1)} %add_convert_fusion), channel_id=1, replica_groups={{0,128,256,384},{1,129,257,385},{2,130,258,386},{3,131,259,387},{4,132,..., dimensions={0} | all-to-all | bytes 1310720 | tf_op jit(solution)/shard_map/all_to_all | solution.py:424
  59.4 0.7 spread.1
  60.1 26.1 %all_to_all.11.received = bf16[64,10,128]{2,1,0:T(8,128)(2,1)S(1)} all-to-all(bf16[64,10,128]{2,1,0:T(8,128)(2,1)S(1)} %get-tuple-element.35), channel_id=1, replica_groups={{0,2,4,6,8,10,12,14,16,18,20,22,24,26,28,30,32,34,36,38,40,42,44,46,48,..., dimensions={0} | all-to-all | bytes 327680 | tf_op jit(solution)/shard_map/all_to_all | solution.py:431
  86.2 1.4 %finish.1 = (f32[288]{0:T(512)}, f32[576]{0:T(1024)}, f32[256]{0:T(256)}) custom-call(s32[6]{0:T(128)} %copy-done.8, bf16[64,10,128]{2,1,0:T(8,128)(2,1)S(1)} %all_to_all.11.received), custom_call_target="tpu_custom_call" | custom-call | tf_op jit(solution)/shard_map/finish/pallas_call | solution.py:432
Async XLA Ops:
  2.2 17.2 %collective-permute-start = (bf16[6,56,128]{2,1,0:T(8,128)(2,1)}, bf16[6,56,128]{2,1,0:T(8,128)(2,1)S(1)}, u32[]{:S(2)}, u32[]{:S(2)}) collective-permute-start(bf16[6,56,128]{2,1,0:T(8,128)(2,1)} %get-tuple-element.22), channel_id=1, source_target_pairs={{0,32},{32,64},{64,96},{96,128},{128,160},{160,192},{192,224},{224... | collective-permute-start | bytes 258056 | tf_op jit(solution)/shard_map/ppermute | solution.py:349
  8.3 11.1 %collective-permute-start.1 = (bf16[5,56,128]{2,1,0:T(8,128)(2,1)}, bf16[5,56,128]{2,1,0:T(8,128)(2,1)S(1)}, u32[]{:S(2)}, u32[]{:S(2)}) collective-permute-start(bf16[5,56,128]{2,1,0:T(8,128)(2,1)} %get-tuple-element.23), channel_id=1, source_target_pairs={{32,0},{64,32},{96,64},{128,96},{160,128},{192,160},{224,192},{256... | collective-permute-start | bytes 215048 | tf_op jit(solution)/shard_map/ppermute | solution.py:350
  19.4 9.7 %copy-start = (bf16[32,56,128]{2,1,0:T(8,128)(2,1)S(1)}, bf16[32,56,128]{2,1,0:T(8,128)(2,1)}, u32[]{:S(2)}) copy-start(bf16[32,56,128]{2,1,0:T(8,128)(2,1)} %x.1) | copy-start | bytes 1376260
  19.4 9.7 %copy-start.1 = (bf16[32,56,128]{2,1,0:T(8,128)(2,1)S(1)}, bf16[32,56,128]{2,1,0:T(8,128)(2,1)}, u32[]{:S(2)}) copy-start(bf16[32,56,128]{2,1,0:T(8,128)(2,1)} %c.1) | copy-start | bytes 1376260
  19.4 9.7 %copy-start.2 = (bf16[3,3,128,256]{3,2,1,0:T(8,128)(2,1)S(1)}, bf16[3,3,128,256]{3,2,1,0:T(8,128)(2,1)}, u32[]{:S(2)}) copy-start(bf16[3,3,128,256]{3,2,1,0:T(8,128)(2,1)} %wd.1) | copy-start | bytes 1769476
  19.4 9.7 %copy-start.3 = (bf16[256,1024]{1,0:T(8,128)(2,1)S(1)}, bf16[256,1024]{1,0:T(8,128)(2,1)}, u32[]{:S(2)}) copy-start(bf16[256,1024]{1,0:T(8,128)(2,1)} %get-tuple-element.24.w_odd) | copy-start | bytes 1572868
  19.4 9.7 %copy-start.6 = (bf16[256,512]{1,0:T(8,128)(2,1)S(1)}, bf16[256,512]{1,0:T(8,128)(2,1)}, u32[]{:S(2)}) copy-start(bf16[256,512]{1,0:T(8,128)(2,1)} %get-tuple-element.29.w_up) | copy-start | bytes 786436
  19.4 9.7 %copy-start.7 = (bf16[256,512]{1,0:T(8,128)(2,1)S(1)}, bf16[256,512]{1,0:T(8,128)(2,1)}, u32[]{:S(2)}) copy-start(bf16[256,512]{1,0:T(8,128)(2,1)} %get-tuple-element.30.w_even) | copy-start | bytes 786436
  21.2 5.9 %collective-permute-start.2 = (bf16[75,4,128]{2,1,0:T(4,128)(2,1)}, bf16[75,4,128]{2,1,0:T(4,128)(2,1)S(1)}, u32[]{:S(2)}, u32[]{:S(2)}) collective-permute-start(bf16[75,4,128]{2,1,0:T(4,128)(2,1)} %get-tuple-element.25), channel_id=1, source_target_pairs={{0,1},{1,2},{2,3},{3,4},{4,5},{5,6},{6,7},{7,8},{8,9},{9,10},{10,1... | collective-permute-start | bytes 230408 | tf_op jit(solution)/shard_map/ppermute | solution.py:361
  23.2 6.0 %collective-permute-start.3 = (bf16[75,4,128]{2,1,0:T(4,128)(2,1)}, bf16[75,4,128]{2,1,0:T(4,128)(2,1)S(1)}, u32[]{:S(2)}, u32[]{:S(2)}) collective-permute-start(bf16[75,4,128]{2,1,0:T(4,128)(2,1)} %get-tuple-element.26), channel_id=1, source_target_pairs={{1,0},{2,1},{3,2},{4,3},{5,4},{6,5},{7,6},{8,7},{9,8},{10,9},{11,1... | collective-permute-start | bytes 230408 | tf_op jit(solution)/shard_map/ppermute | solution.py:362
  26.9 11.5 %copy-start.8 = (s32[6]{0:T(128)}, s32[6]{0:T(128)S(1)}, u32[]{:S(2)}) copy-start(s32[6]{0:T(128)S(1)} %concatenate.3.edge) | copy-start | bytes 76
  29.1 1.1 %copy-start.4 = (bf16[3,512,256]{2,1,0:T(8,128)(2,1)S(1)}, bf16[3,512,256]{2,1,0:T(8,128)(2,1)}, u32[]{:S(2)}) copy-start(bf16[3,512,256]{2,1,0:T(8,128)(2,1)} %get-tuple-element.27.w_fwd) | copy-start | bytes 2359300
  30.3 1.1 %copy-start.5 = (bf16[3,256,512]{2,1,0:T(8,128)(2,1)S(1)}, bf16[3,256,512]{2,1,0:T(8,128)(2,1)}, u32[]{:S(2)}) copy-start(bf16[3,256,512]{2,1,0:T(8,128)(2,1)} %get-tuple-element.28.w_bwd) | copy-start | bytes 2359300
  38.5 5.3 %collective-permute-start.4 = (bf16[4,640,128]{2,1,0:T(8,128)(2,1)S(1)}, bf16[4,640,128]{2,1,0:T(8,128)(2,1)S(1)}, u32[]{:S(2)}, u32[]{:S(2)}) collective-permute-start(bf16[4,640,128]{2,1,0:T(8,128)(2,1)S(1)} %get-tuple-element.34), channel_id=1, source_target_pairs={{0,1},{1,0},{2,3},{3,2},{4,5},{5,4},{6,7},{7,6},{8,9},{9,8},{10,11... | collective-permute-start | bytes 1966088 | tf_op jit(solution)/shard_map/ppermute | solution.py:422

commit v3 on v2

--- a/solution.py
+++ b/solution.py
@@ -13,7 +13,7 @@
 NN = (((1,), (0,)), ((), ()))
 NT = (((1,), (1,)), ((), ()))
 TN = (((0,), (0,)), ((), ()))
-LANES = 32
+SMALL = pltpu.CompilerParams(vmem_limit_bytes=8 * 1024 * 1024)
 
 
 def held(shape, dtype=BF):
@@ -26,6 +26,11 @@
 
 def pin(*arrays):
     return tuple(pltpu.with_memory_space_constraint(a, pltpu.VMEM) for a in arrays)
+
+
+def swapped(odd, one, two):
+    one, two = one[...].astype(F32), two[...].astype(F32)
+    return jnp.where(odd, two, one), jnp.where(odd, one, two)
 
 
 def mm(left, right, dims):
@@ -67,7 +72,8 @@
     shapes = ((3, 512, 256), (3, 256, 512), (256, 512), (256, 512), (256, 1024))
     return pl.pallas_call(
         weights_kernel,
-        out_shape=tuple(jax.ShapeDtypeStruct(s, BF) for s in shapes),
+        out_shape=tuple(held(s) for s in shapes),
+        compiler_params=SMALL,
         name="weights",
     )(w_conv, w_down, w_up)
 
@@ -95,23 +101,27 @@
 
 
 def level_kernel(
-    edge, x, c, top, bot, left, right, w_fwd, w_bwd, w_down, w_up, w_even, w_odd,
+    x, c, row_a, row_b, col_a, col_b, w_fwd, w_bwd, w_down, w_up, w_even, w_odd,
     out, gx, keep, send,
     conv_acc, down_acc, up_acc, xs, cs, x4, c4, f3, slope, gs, coarse_own, g_own, g4, pre_own, mix,
 ):
     for ref in (xs, cs):
         ref[:, 0:8, :] = jnp.zeros((ref.shape[0], 8, 128), F32)
         ref[:, 64:72, :] = jnp.zeros((ref.shape[0], 8, 128), F32)
+    at_row, at_col = lax.axis_index("row"), lax.axis_index("col")
+    odd_row, odd_col = at_row % 2 == 1, at_col % 2 == 1
+    top, bot = swapped(odd_row, row_b, row_a)
+    left, right = swapped(odd_col, col_b, col_a)
     xs[4:36, 8:64, :] = x[...].astype(F32)
-    xs[0:4, 8:64, :] = top[0:4].astype(F32)
-    xs[36:39, 8:64, :] = bot[0:3].astype(F32)
-    xs[0:39, 4:8, :] = left[0:39].astype(F32)
-    xs[0:39, 64:68, :] = right[0:39].astype(F32)
+    xs[0:4, 8:64, :] = top[0:4]
+    xs[36:39, 8:64, :] = bot[0:3]
+    xs[0:39, 4:8, :] = left[0:39]
+    xs[0:39, 64:68, :] = right[0:39]
     cs[2:34, 8:64, :] = c[...].astype(F32)
-    cs[0:2, 8:64, :] = top[4:6].astype(F32)
-    cs[34:36, 8:64, :] = bot[3:5].astype(F32)
-    cs[0:36, 4:8, :] = left[39:75].astype(F32)
-    cs[0:36, 64:68, :] = right[39:75].astype(F32)
+    cs[0:2, 8:64, :] = top[4:6]
+    cs[34:36, 8:64, :] = bot[4:6]
+    cs[0:36, 4:8, :] = left[39:75]
+    cs[0:36, 64:68, :] = right[39:75]
     for r in range(39):
         for k in range(4):
             x4[r, :, k * 128 : (k + 1) * 128] = xs[r, pl.ds(3 + k, 32, stride=2), :].astype(BF)
@@ -124,8 +134,8 @@
                     2 * ai + p, pl.ds(4 + q, 32, stride=2), :
                 ].astype(BF)
 
-    is_top, is_bot = edge[0] > 0, edge[1] > 0
-    is_left, is_right = edge[2] > 0, edge[3] > 0
+    is_top, is_bot = at_row == 0, at_row == lax.axis_size("row") - 1
+    is_left, is_right = at_col == 0, at_col == lax.axis_size("col") - 1
     half = lax.broadcasted_iota(jnp.int32, (32, 256), 0) - 2
     in_grid = ((half >= 0) | jnp.logical_not(is_left)) & ((half < 28) | jnp.logical_not(is_right))
     in_grid = jnp.where(in_grid, 1.0, 0.0)
@@ -251,18 +261,18 @@
             tap = res[0:128, q * 128 : (q + 1) * 128] + res[128:256, (q + 1) * 128 : (q + 2) * 128]
             conv_acc[(3 * p + q) * 128 : (3 * p + q + 1) * 128, :] = tap.T
 
-    @pl.when(edge[4] == 0)
+    @pl.when(jnp.logical_not(odd_col))
     def _():
         pack(0, keep, conv_acc, down_acc, up_acc)
         pack(1, send, conv_acc, down_acc, up_acc)
 
-    @pl.when(edge[4] != 0)
+    @pl.when(odd_col)
     def _():
         pack(1, keep, conv_acc, down_acc, up_acc)
         pack(0, send, conv_acc, down_acc, up_acc)
 
 
-def level(edge, x, c, top, bot, left, right, weights, w_down):
+def level(x, c, halo, weights, w_down):
     w_fwd, w_bwd, w_up, w_even, w_odd = weights
     vmem = pl.BlockSpec(memory_space=pltpu.VMEM)
     return pl.pallas_call(
@@ -273,7 +283,7 @@
             held((4, 640, 128)),
             held((4, 640, 128)),
         ),
-        in_specs=[pl.BlockSpec(memory_space=pltpu.SMEM)] + [vmem] * 12,
+        in_specs=[vmem] * 12,
         out_specs=(vmem,) * 4,
         scratch_shapes=[
             pltpu.VMEM((1160, 128), F32),
@@ -295,35 +305,47 @@
         compiler_params=pltpu.CompilerParams(vmem_limit_bytes=18 * 1024 * 1024),
         name="level",
     )(
-        edge, x, c, top, bot, *pin(left, right), w_fwd, w_bwd, w_down, w_up, w_even, w_odd
+        x, c, *halo[:2], *pin(*halo[2:]), *pin(w_fwd, w_bwd), w_down, *pin(w_up, w_even, w_odd)
     )
 
 
-def chain(axis, step):
+def pairs(axis):
     count = lax.axis_size(axis)
-    return [(i, i + step) for i in range(count) if 0 <= i + step < count]
-
-
-def rows_kernel(x_last, x_first, c_last, c_first, down, up):
-    down[0:4] = x_last[...]
-    down[4:6] = c_last[...]
-    up[0:3] = x_first[0:3]
-    up[3:5] = c_first[...]
-
-
-def cols_kernel(
-    x_last, x_first, c_last, c_first, top, bot, w_odd, right, left
-):
-    for out, cols, near, x, c in (
-        (right, slice(52, 56), slice(4, 8), x_last, c_last),
-        (left, slice(0, 4), slice(0, 4), x_first, c_first),
-    ):
-        out[0:4] = top[0:4, cols, :]
-        out[4:36] = x[:, near, :]
-        out[36:39] = bot[0:3, cols, :]
-        out[39:41] = top[4:6, cols, :]
-        out[41:73] = c[:, near, :]
-        out[73:75] = bot[3:5, cols, :]
+    both = []
+    for first in (0, 1):
+        swaps = [(i, i + 1) for i in range(first, count - 1, 2)]
+        both.append(swaps + [(b, a) for a, b in swaps])
+    return both
+
+
+def store_pair(odd, forward, backward, even_first, odd_first):
+    even_first[...] = jnp.where(odd, backward, forward).astype(BF)
+    odd_first[...] = jnp.where(odd, forward, backward).astype(BF)
+
+
+def rows_kernel(x_last, x_first, c_last, c_first, row_a, row_b):
+    odd = lax.axis_index("row") % 2 == 1
+    down = jnp.concatenate([x_last[...], c_last[...]], axis=0).astype(F32)
+    up = jnp.concatenate([x_first[...], c_first[...]], axis=0).astype(F32)
+    store_pair(odd, down, up, row_a, row_b)
+
+
+def cols_kernel(x_last, x_first, c_last, c_first, row_a, row_b, col_a, col_b):
+    top, bot = swapped(lax.axis_index("row") % 2 == 1, row_b, row_a)
+
+    def side(cols, near, x, c):
+        x, c = x[...].astype(F32), c[...].astype(F32)
+        return jnp.concatenate(
+            [
+                top[0:4, cols], x[:, near], bot[0:3, cols],
+                top[4:6, cols], c[:, near], bot[4:6, cols],
+            ],
+            axis=0,
+        )
+
+    rightward = side(slice(52, 56), slice(4, 8), x_last, c_last)
+    leftward = side(slice(0, 4), slice(0, 4), x_first, c_first)
+    store_pair(lax.axis_index("col") % 2 == 1, rightward, leftward, col_a, col_b)
 
 
 def row_block(count, at):
@@ -334,44 +356,40 @@
     return pl.BlockSpec((count, 8, 128), lambda i: (0, at, 0))
 
 
-def exchange(x, c, w_odd):
-    down, up = pl.pallas_call(
+def exchange(x, c):
+    first, second = pl.pallas_call(
         rows_kernel,
         grid=(1,),
-        out_shape=(
-            jax.ShapeDtypeStruct((6, 56, 128), BF),
-            jax.ShapeDtypeStruct((5, 56, 128), BF),
-        ),
+        out_shape=(jax.ShapeDtypeStruct((6, 56, 128), BF),) * 2,
         in_specs=[row_block(4, 7), row_block(4, 0), row_block(2, 15), row_block(2, 0)],
-        out_specs=(row_block(6, 0), row_block(5, 0)),
+        out_specs=(row_block(6, 0),) * 2,
+        compiler_params=SMALL,
         name="rows",
     )(*far(x, x, c, c))
-    top = lax.ppermute(down, "row", chain("row", 1))
-    bot = lax.ppermute(up, "row", chain("row", -1))
+    even, odd = pairs("row")
+    row_a = lax.ppermute(first, "row", even)
+    row_b = lax.ppermute(second, "row", odd)
     whole = pl.BlockSpec((75, 4, 128), lambda i: (0, 0, 0))
-    going_right, going_left = pl.pallas_call(
+    first, second = pl.pallas_call(
         cols_kernel,
         grid=(1,),
         out_shape=(jax.ShapeDtypeStruct((75, 4, 128), BF),) * 2,
-        in_specs=[col_block(32, at) for at in (6, 0, 6, 0)]
-        + [row_block(6, 0), row_block(5, 0), pl.BlockSpec(memory_space=pl.ANY)],
+        in_specs=[col_block(32, at) for at in (6, 0, 6, 0)] + [row_block(6, 0)] * 2,
         out_specs=(whole, whole),
+        compiler_params=SMALL,
         name="cols",
-    )(*far(x, x, c, c), *pin(top, bot), *far(w_odd))
-    left = lax.ppermute(going_right, "col", chain("col", 1))
-    right = lax.ppermute(going_left, "col", chain("col", -1))
-    return top, bot, left, right
+    )(*far(x, x, c, c), *pin(row_a, row_b))
+    even, odd = pairs("col")
+    col_a = lax.ppermute(first, "col", even)
+    col_b = lax.ppermute(second, "col", odd)
+    return row_a, row_b, col_a, col_b
 
 
 def local_terms(inputs, cotangent, w_conv, w_down, w_up):
-    n_row, n_col = lax.axis_size("row"), lax.axis_size("col")
-    at_row, at_col = lax.axis_index("row"), lax.axis_index("col")
-    edge = jnp.array(
-        [at_row == 0, at_row == n_row - 1, at_col == 0, at_col == n_col - 1, at_col & 1, at_col & 3]
-    ).astype(jnp.int32)
-    weights = prepare_weights(w_conv, w_down, w_up)
-    halo = exchange(inputs, cotangent, weights[4])
-    return edge, level(edge, inputs, cotangent, *halo, weights, w_down.reshape(1152, 256))
+    halo = exchange(inputs, cotangent)
+    late_conv, _ = lax.optimization_barrier((w_conv, halo[0]))
+    weights = prepare_weights(late_conv, w_down, w_up)
+    return level(inputs, cotangent, halo, weights, w_down.reshape(1152, 256))
 
 
 def spread_kernel(received, out, spare, total):
@@ -383,11 +401,11 @@
             out[8 * z + y] = total[pl.ds(first, 10, stride=32), :].astype(BF)
 
 
-def finish_kernel(scale, edge, received, conv, down, up):
+def finish_kernel(scale, received, conv, down, up):
     rows = jnp.sum(received[...].astype(F32), axis=0) * scale
     for which in range(4):
 
-        @pl.when(edge[5] == which)
+        @pl.when(lax.axis_index("col") % 4 == which)
         def _():
             for ref, base, names, size in (
                 (conv, 0, CONV_ROWS, 288), (down, 3, DOWN_ROWS, 576), (up, 8, UP_ROWS, 256)
@@ -416,7 +434,7 @@
     return across, plane
 
 
-def reduce_owners(edge, keep, send, scale):
+def reduce_owners(keep, send, scale):
     mesh = ("row", "col")
     across, plane = coordinates()
     other = lax.ppermute(send, "col", [(i, i ^ 1) for i in range(32)])
@@ -426,27 +444,24 @@
         spread_kernel,
         out_shape=(held((64, 10, 128)), held((8, 128), F32)),
         scratch_shapes=[pltpu.VMEM((672, 128), F32)],
+        compiler_params=SMALL,
         name="spread",
     )(*pin(got))
     got = lax.all_to_all(spread, mesh, 0, 0, axis_index_groups=plane, tiled=True)
     sums = pl.pallas_call(
         functools.partial(finish_kernel, scale),
         out_shape=tuple(jax.ShapeDtypeStruct((n,), F32) for n in (288, 576, 256)),
-        in_specs=[
-            pl.BlockSpec(memory_space=pltpu.SMEM),
-            pl.BlockSpec(memory_space=pltpu.VMEM),
-        ],
+        compiler_params=SMALL,
         name="finish",
-    )(edge, *pin(got))
+    )(*pin(got))
     return sums
 
 
 def body(inputs, cotangent, w_conv, w_down, w_up):
-    edge, parts = local_terms(inputs, cotangent, w_conv, w_down, w_up)
-    output, grad_inputs, keep, send = parts
+    output, grad_inputs, keep, send = local_terms(inputs, cotangent, w_conv, w_down, w_up)
     rows, cols, _ = inputs.shape
     scale = 1.0 / math.sqrt(rows * lax.axis_size("row") * cols * lax.axis_size("col"))
-    return (output, grad_inputs, *reduce_owners(edge, keep, send, scale))
+    return (output, grad_inputs, *reduce_owners(keep, send, scale))
 
 
 def solution(mesh):

time: 88.1 us -> 83.3 us (0.946)
  blocking collectives: 41.6 us -> 48.9 us
  waiting for transfers between devices: 10.8 us -> 5.46 us
  Pallas kernels: 15.4 us -> 10.3 us
  local copies, waits for them, and re-layouts: 2.37 us -> 0.03 us
    all_to_all x1, blocking collectives: 15.5 us -> 21.8 us  [reduce_owners(): got = lax.all_to_all(pair, mesh, 0, 0, axis_index_groups=across, tiled=True)]
    ppermute x4, waiting for transfers between devices: 9.14 us -> 3.39 us  [the longest x1 1.7 us: exchange(): col_b = lax.ppermute(second, 'col', odd)]
    pallas_call x1, Pallas kernels: 2.88 us -> 0.3 us  [prepare_weights(): pl.pallas_call(weights_kernel, out_shape=tuple((held(s) for s in shapes))...]
    ppermute x4, starting transfers between devices: 12.9 us -> 15.4 us  [the longest x1 6.49 us: exchange(): col_b = lax.ppermute(second, 'col', odd)]
    unnamed x18 -> x10, local copies, waits for them, and re-layouts: 2.29 us -> 0.03 us
    ppermute x1, starting transfers between devices: 3.55 us -> 1.91 us  [reduce_owners(): other = lax.ppermute(send, 'col', [(i, i ^ 1) for i in range(32)])]
    all_to_all x1, blocking collectives: 26.1 us -> 27 us  [reduce_owners(): lax.all_to_all(spread, mesh, 0, 0, axis_index_groups=plane, tiled=True)]
  transfers between devices with their start and end apart: 5 -> 5, of which waited for: 4 -> 3; matrix products, arithmetic and copies ran while one was open for 0% -> 0% of each run, Pallas kernels for 3% -> 0%
where the time goes in v3:
time: 83.3 us; the launch traced here: 82.9 us
  blocking collectives  48.9 us (59%)
  starting transfers between devices  17.3 us (21%)
  Pallas kernels  10.3 us (12%)
  waiting for transfers between devices  5.46 us (7%)
    all_to_all x1, blocking collectives, reduce_owners(): lax.all_to_all(spread, mesh, 0, 0, axis_index_groups=plane, tiled=True)  27 us
    all_to_all x1, blocking collectives, reduce_owners(): got = lax.all_to_all(pair, mesh, 0, 0, axis_index_groups=across, tiled=True)  21.8 us
    pallas_call x1, Pallas kernels, level(): pl.pallas_call(level_kernel, out_shape=(jax.ShapeDtypeStruct((32, 56, 128...  6.53 us
    ppermute x1, starting transfers between devices, exchange(): col_b = lax.ppermute(second, 'col', odd)  6.49 us
    ppermute x1, starting transfers between devices, exchange(): row_a = lax.ppermute(first, 'row', even)  6.09 us
    ppermute x1, waiting for transfers between devices, reduce_owners(): other = lax.ppermute(send, 'col', [(i, i ^ 1) for i in range(32)])  2.06 us
    ppermute x1, starting transfers between devices, exchange(): col_a = lax.ppermute(first, 'col', even)  2.05 us
    ppermute x1, starting transfers between devices, reduce_owners(): other = lax.ppermute(send, 'col', [(i, i ^ 1) for i in range(32)])  1.91 us
  transfers between devices with their start and end apart: 5, of which 3 were waited for; matrix products, arithmetic and copies ran while one was open for 0% of the time, Pallas kernels for 0%

profile of v3, /device:TPU:8, one launch (start us, length us, event | category | flops | bytes accessed | tf_op | source)
XLA Modules:
  0.0 82.9 jit_solution(13543773887361343875)
XLA Ops:
  0.6 0.9 %rows.1 = (bf16[6,56,128]{2,1,0:T(8,128)(2,1)S(1)}, bf16[6,56,128]{2,1,0:T(8,128)(2,1)S(1)}) custom-call(bf16[32,56,128]{2,1,0:T(8,128)(2,1)} %x.1, bf16[32,56,128]{2,1,0:T(8,128)(2,1)} %x.1, bf16[32,56,128]{2,1,0:T(8,128)(2,1)} %c.1, bf16[32,56,128]{2,1,0:T(8,128)(2,1)} %c.1), custom_call_target="tpu_custom_call" | custom-call | tf_op jit(solution)/shard_map/rows/pallas_call | solution.py:360
  1.5 6.1 %collective-permute-start = (bf16[6,56,128]{2,1,0:T(8,128)(2,1)S(1)}, bf16[6,56,128]{2,1,0:T(8,128)(2,1)S(1)}, u32[]{:S(2)}, u32[]{:S(2)}) collective-permute-start(bf16[6,56,128]{2,1,0:T(8,128)(2,1)S(1)} %get-tuple-element.23), channel_id=1, source_target_pairs={{0,32},{64,96},{128,160},{192,224},{256,288},{320,352},{384,416},{... | collective-permute-start | bytes 258056 | tf_op jit(solution)/shard_map/ppermute | solution.py:370
  7.6 0.0 copy-start.2
  7.7 0.0 copy-start.3
  7.7 0.0 copy-start.4
  7.7 0.8 collective-permute-start.1
  8.5 1.7 %collective-permute-done.row_a = bf16[6,56,128]{2,1,0:T(8,128)(2,1)S(1)} collective-permute-done((bf16[6,56,128]{2,1,0:T(8,128)(2,1)S(1)}, bf16[6,56,128]{2,1,0:T(8,128)(2,1)S(1)}, u32[]{:S(2)}, u32[]{:S(2)}) %collective-permute-start) | collective-permute-done | bytes 86048 | tf_op jit(solution)/shard_map/ppermute | solution.py:370
  10.2 0.0 collective-permute-done.1.row_b
  10.2 1.1 %cols.1 = (bf16[75,4,128]{2,1,0:T(4,128)(2,1)S(1)}, bf16[75,4,128]{2,1,0:T(4,128)(2,1)S(1)}) custom-call(bf16[32,56,128]{2,1,0:T(8,128)(2,1)} %x.1, bf16[32,56,128]{2,1,0:T(8,128)(2,1)} %x.1, bf16[32,56,128]{2,1,0:T(8,128)(2,1)} %c.1, bf16[32,56,128]{2,1,0:T(8,128)(2,1)} %c.1, bf16[6,56,128]{2,1,0:T(8,128)(2,1)S(1)} %collective-permute-done.row_a, ...), custom_call_target="tpu_custom_call" | custom-call | tf_op jit(solution)/shard_map/cols/pallas_call | solution.py:373
  11.2 0.0 copy-start
  11.3 0.0 copy-start.1
  11.3 2.1 %collective-permute-start.2 = (bf16[75,4,128]{2,1,0:T(4,128)(2,1)S(1)}, bf16[75,4,128]{2,1,0:T(4,128)(2,1)S(1)}, u32[]{:S(2)}, u32[]{:S(2)}) collective-permute-start(bf16[75,4,128]{2,1,0:T(4,128)(2,1)S(1)} %get-tuple-element.25), channel_id=1, source_target_pairs={{0,1},{2,3},{4,5},{6,7},{8,9},{10,11},{12,13},{14,15},{16,17},{18,... | collective-permute-start | bytes 230408 | tf_op jit(solution)/shard_map/ppermute | solution.py:383
  13.3 6.5 %collective-permute-start.3 = (bf16[75,4,128]{2,1,0:T(4,128)(2,1)S(1)}, bf16[75,4,128]{2,1,0:T(4,128)(2,1)S(1)}, u32[]{:S(2)}, u32[]{:S(2)}) collective-permute-start(bf16[75,4,128]{2,1,0:T(4,128)(2,1)S(1)} %get-tuple-element.26), channel_id=1, source_target_pairs={{1,2},{3,4},{5,6},{7,8},{9,10},{11,12},{13,14},{15,16},{17,18},{19... | collective-permute-start | bytes 230408 | tf_op jit(solution)/shard_map/ppermute | solution.py:384
  19.8 0.0 copy-done.2
  19.8 0.0 copy-done.3
  19.8 0.0 copy-done.4
  19.9 0.3 weights.1
  20.2 0.0 collective-permute-done.2.col_a
  20.2 1.7 %collective-permute-done.3.col_b = bf16[75,4,128]{2,1,0:T(4,128)(2,1)S(1)} collective-permute-done((bf16[75,4,128]{2,1,0:T(4,128)(2,1)S(1)}, bf16[75,4,128]{2,1,0:T(4,128)(2,1)S(1)}, u32[]{:S(2)}, u32[]{:S(2)}) %collective-permute-start.3) | collective-permute-done | bytes 76832 | tf_op jit(solution)/shard_map/ppermute | solution.py:384
  21.9 0.0 copy-done
  21.9 0.0 copy-done.1
  21.9 6.5 %level.1 = (bf16[32,56,128]{2,1,0:T(8,128)(2,1)}, bf16[32,56,128]{2,1,0:T(8,128)(2,1)}, bf16[4,640,128]{2,1,0:T(8,128)(2,1)S(1)}, bf16[4,640,128]{2,1,0:T(8,128)(2,1)S(1)}) custom-call(bf16[32,56,128]{2,1,0:T(8,128)(2,1)S(1)} %copy-done, bf16[32,56,128]{2,1,0:T(8,128)(2,1)S(1)} %copy-done.1, bf16[6,56,128]{2,1,0:T(8,128)(2,1)S(1)} %collective-permute-done.row_a, ...), custom_call_target="tpu_custom_call" | custom-call | tf_op jit(solution)/shard_map/level/pallas_call | solution.py:278
  28.4 1.9 %collective-permute-start.4 = (bf16[4,640,128]{2,1,0:T(8,128)(2,1)S(1)}, bf16[4,640,128]{2,1,0:T(8,128)(2,1)S(1)}, u32[]{:S(2)}, u32[]{:S(2)}) collective-permute-start(bf16[4,640,128]{2,1,0:T(8,128)(2,1)S(1)} %get-tuple-element.36), channel_id=1, source_target_pairs={{0,1},{1,0},{2,3},{3,2},{4,5},{5,4},{6,7},{7,6},{8,9},{9,8},{10,11... | collective-permute-start | bytes 1966088 | tf_op jit(solution)/shard_map/ppermute | solution.py:440
  30.3 2.1 %collective-permute-done.4 = bf16[4,640,128]{2,1,0:T(8,128)(2,1)S(1)} collective-permute-done((bf16[4,640,128]{2,1,0:T(8,128)(2,1)S(1)}, bf16[4,640,128]{2,1,0:T(8,128)(2,1)S(1)}, u32[]{:S(2)}, u32[]{:S(2)}) %collective-permute-start.4) | collective-permute-done | bytes 655392 | tf_op jit(solution)/shard_map/ppermute | solution.py:440
  32.4 0.2 add_convert_fusion
  32.6 21.8 %all_to_all.10.received = bf16[4,640,128]{2,1,0:T(8,128)(2,1)S(1)} all-to-all(bf16[4,640,128]{2,1,0:T(8,128)(2,1)S(1)} %add_convert_fusion), channel_id=1, replica_groups={{0,128,256,384},{1,129,257,385},{2,130,258,386},{3,131,259,387},{4,132,..., dimensions={0} | all-to-all | bytes 1310720 | tf_op jit(solution)/shard_map/all_to_all | solution.py:442
  54.4 0.7 spread.1
  55.1 27.0 %all_to_all.11.received = bf16[64,10,128]{2,1,0:T(8,128)(2,1)S(1)} all-to-all(bf16[64,10,128]{2,1,0:T(8,128)(2,1)S(1)} %get-tuple-element.37), channel_id=1, replica_groups={{0,2,4,6,8,10,12,14,16,18,20,22,24,26,28,30,32,34,36,38,40,42,44,46,48,..., dimensions={0} | all-to-all | bytes 327680 | tf_op jit(solution)/shard_map/all_to_all | solution.py:450
  82.2 0.7 finish.1
Async XLA Ops:
  1.5 8.6 %collective-permute-start = (bf16[6,56,128]{2,1,0:T(8,128)(2,1)S(1)}, bf16[6,56,128]{2,1,0:T(8,128)(2,1)S(1)}, u32[]{:S(2)}, u32[]{:S(2)}) collective-permute-start(bf16[6,56,128]{2,1,0:T(8,128)(2,1)S(1)} %get-tuple-element.23), channel_id=1, source_target_pairs={{0,32},{64,96},{128,160},{192,224},{256,288},{320,352},{384,416},{... | collective-permute-start | bytes 258056 | tf_op jit(solution)/shard_map/ppermute | solution.py:370
  7.6 12.2 %copy-start.2 = (bf16[3,3,128,256]{3,2,1,0:T(8,128)(2,1)S(1)}, bf16[3,3,128,256]{3,2,1,0:T(8,128)(2,1)}, u32[]{:S(2)}) copy-start(bf16[3,3,128,256]{3,2,1,0:T(8,128)(2,1)} %wd.1) | copy-start | bytes 1769476
  7.7 12.2 %copy-start.3 = (bf16[3,3,128,128]{3,2,1,0:T(8,128)(2,1)S(1)}, bf16[3,3,128,128]{3,2,1,0:T(8,128)(2,1)}, u32[]{:S(2)}) copy-start(bf16[3,3,128,128]{3,2,1,0:T(8,128)(2,1)} %wc) | copy-start | bytes 884740
  7.7 12.2 %copy-start.4 = (bf16[2,2,256,128]{3,2,1,0:T(8,128)(2,1)S(1)}, bf16[2,2,256,128]{3,2,1,0:T(8,128)(2,1)}, u32[]{:S(2)}) copy-start(bf16[2,2,256,128]{3,2,1,0:T(8,128)(2,1)} %wu.1) | copy-start | bytes 786436
  7.7 2.5 %collective-permute-start.1 = (bf16[6,56,128]{2,1,0:T(8,128)(2,1)S(1)}, bf16[6,56,128]{2,1,0:T(8,128)(2,1)S(1)}, u32[]{:S(2)}, u32[]{:S(2)}) collective-permute-start(bf16[6,56,128]{2,1,0:T(8,128)(2,1)S(1)} %get-tuple-element.24), channel_id=1, source_target_pairs={{32,64},{96,128},{160,192},{224,256},{288,320},{352,384},{416,448}... | collective-permute-start | bytes 258056 | tf_op jit(solution)/shard_map/ppermute | solution.py:371
  11.2 10.6 %copy-start = (bf16[32,56,128]{2,1,0:T(8,128)(2,1)S(1)}, bf16[32,56,128]{2,1,0:T(8,128)(2,1)}, u32[]{:S(2)}) copy-start(bf16[32,56,128]{2,1,0:T(8,128)(2,1)} %x.1) | copy-start | bytes 1376260
  11.3 10.6 %copy-start.1 = (bf16[32,56,128]{2,1,0:T(8,128)(2,1)S(1)}, bf16[32,56,128]{2,1,0:T(8,128)(2,1)}, u32[]{:S(2)}) copy-start(bf16[32,56,128]{2,1,0:T(8,128)(2,1)} %c.1) | copy-start | bytes 1376260
  11.3 8.9 %collective-permute-start.2 = (bf16[75,4,128]{2,1,0:T(4,128)(2,1)S(1)}, bf16[75,4,128]{2,1,0:T(4,128)(2,1)S(1)}, u32[]{:S(2)}, u32[]{:S(2)}) collective-permute-start(bf16[75,4,128]{2,1,0:T(4,128)(2,1)S(1)} %get-tuple-element.25), channel_id=1, source_target_pairs={{0,1},{2,3},{4,5},{6,7},{8,9},{10,11},{12,13},{14,15},{16,17},{18,... | collective-permute-start | bytes 230408 | tf_op jit(solution)/shard_map/ppermute | solution.py:383
  13.3 8.6 %collective-permute-start.3 = (bf16[75,4,128]{2,1,0:T(4,128)(2,1)S(1)}, bf16[75,4,128]{2,1,0:T(4,128)(2,1)S(1)}, u32[]{:S(2)}, u32[]{:S(2)}) collective-permute-start(bf16[75,4,128]{2,1,0:T(4,128)(2,1)S(1)} %get-tuple-element.26), channel_id=1, source_target_pairs={{1,2},{3,4},{5,6},{7,8},{9,10},{11,12},{13,14},{15,16},{17,18},{19... | collective-permute-start | bytes 230408 | tf_op jit(solution)/shard_map/ppermute | solution.py:384
  28.4 4.0 %collective-permute-start.4 = (bf16[4,640,128]{2,1,0:T(8,128)(2,1)S(1)}, bf16[4,640,128]{2,1,0:T(8,128)(2,1)S(1)}, u32[]{:S(2)}, u32[]{:S(2)}) collective-permute-start(bf16[4,640,128]{2,1,0:T(8,128)(2,1)S(1)} %get-tuple-element.36), channel_id=1, source_target_pairs={{0,1},{1,0},{2,3},{3,2},{4,5},{5,4},{6,7},{7,6},{8,9},{9,8},{10,11... | collective-permute-start | bytes 1966088 | tf_op jit(solution)/shard_map/ppermute | solution.py:440

commit v4 on v3

--- a/solution.py
+++ b/solution.py
@@ -101,9 +101,9 @@
 
 
 def level_kernel(
-    x, c, row_a, row_b, col_a, col_b, w_fwd, w_bwd, w_down, w_up, w_even, w_odd,
-    out, gx, keep, send,
-    conv_acc, down_acc, up_acc, xs, cs, x4, c4, f3, slope, gs, coarse_own, g_own, g4, pre_own, mix,
+    x, c, row_a, row_b, col_a, col_b, w_fwd, w_down, w_up, w_even, w_odd,
+    keep, send, f3, coarse_own, g4,
+    conv_acc, down_acc, up_acc, xs, cs, x4, c4, slope, gs, g_own, pre_own,
 ):
     for ref in (xs, cs):
         ref[:, 0:8, :] = jnp.zeros((ref.shape[0], 8, 128), F32)
@@ -187,16 +187,6 @@
             (grad[inner].reshape(high - low, 32, 256) * own[None]).astype(BF)
         )
 
-    for first in (0, 8):
-        up = mm(coarse_own[first : first + 8].reshape(256, 256), w_up[...], NN)
-        for a in range(first, first + 8):
-            for p in range(2):
-                for q in range(2):
-                    k = 2 * p + q
-                    value = up[(a - first) * 32 : (a - first + 1) * 32, k * 128 : (k + 1) * 128]
-                    value = value + f3[2 * a + p + 3, :, 128 + q * 128 : 256 + q * 128].astype(F32)
-                    mix[2 * a + p, pl.ds(4 + q, 32, stride=2), :] = value
-    out[...] = mix[:, 8:64, :].astype(BF)
     coarse_flat = coarse_own[...].reshape(512, 256)
     res = mm(coarse_flat, c4[1:17].reshape(512, 512), TN)
     for k in range(4):
@@ -242,6 +232,35 @@
                 if 1 <= g_row <= 32:
                     pre_own[g_row - 1] = kept[ai - first]
 
+    flat = pre_own[...].reshape(1024, 256)
+    for p in range(3):
+        res = mm(flat, x4[p + 3 : p + 35].reshape(1024, 512), TN)
+        for q in range(3):
+            tap = res[0:128, q * 128 : (q + 1) * 128] + res[128:256, (q + 1) * 128 : (q + 2) * 128]
+            conv_acc[(3 * p + q) * 128 : (3 * p + q + 1) * 128, :] = tap.T
+
+    @pl.when(jnp.logical_not(odd_col))
+    def _():
+        pack(0, keep, conv_acc, down_acc, up_acc)
+        pack(1, send, conv_acc, down_acc, up_acc)
+
+    @pl.when(odd_col)
+    def _():
+        pack(1, keep, conv_acc, down_acc, up_acc)
+        pack(0, send, conv_acc, down_acc, up_acc)
+
+
+def late_kernel(f3, coarse_own, g4, w_up, w_bwd, out, gx, mix):
+    for first in (0, 8):
+        up = mm(coarse_own[first : first + 8].reshape(256, 256), w_up[...], NN)
+        for a in range(first, first + 8):
+            for p in range(2):
+                for q in range(2):
+                    k = 2 * p + q
+                    value = up[(a - first) * 32 : (a - first + 1) * 32, k * 128 : (k + 1) * 128]
+                    value = value + f3[2 * a + p + 3, :, 128 + q * 128 : 256 + q * 128].astype(F32)
+                    mix[2 * a + p, pl.ds(4 + q, 32, stride=2), :] = value
+    out[...] = mix[:, 8:64, :].astype(BF)
     for first in (0, 8, 16, 24):
         total = None
         for p in range(3):
@@ -254,22 +273,6 @@
                     (i - first) * 32 : (i - first + 1) * 32, q * 128 : (q + 1) * 128
                 ]
     gx[...] = mix[:, 8:64, :].astype(BF)
-    flat = pre_own[...].reshape(1024, 256)
-    for p in range(3):
-        res = mm(flat, x4[p + 3 : p + 35].reshape(1024, 512), TN)
-        for q in range(3):
-            tap = res[0:128, q * 128 : (q + 1) * 128] + res[128:256, (q + 1) * 128 : (q + 2) * 128]
-            conv_acc[(3 * p + q) * 128 : (3 * p + q + 1) * 128, :] = tap.T
-
-    @pl.when(jnp.logical_not(odd_col))
-    def _():
-        pack(0, keep, conv_acc, down_acc, up_acc)
-        pack(1, send, conv_acc, down_acc, up_acc)
-
-    @pl.when(odd_col)
-    def _():
-        pack(1, keep, conv_acc, down_acc, up_acc)
-        pack(0, send, conv_acc, down_acc, up_acc)
 
 
 def level(x, c, halo, weights, w_down):
@@ -278,13 +281,14 @@
     return pl.pallas_call(
         level_kernel,
         out_shape=(
-            jax.ShapeDtypeStruct((32, 56, 128), BF),
-            jax.ShapeDtypeStruct((32, 56, 128), BF),
             held((4, 640, 128)),
             held((4, 640, 128)),
+            held((38, 32, 384)),
+            held((16, 32, 256)),
+            held((34, 32, 512)),
         ),
-        in_specs=[vmem] * 12,
-        out_specs=(vmem,) * 4,
+        in_specs=[vmem] * 11,
+        out_specs=(vmem,) * 5,
         scratch_shapes=[
             pltpu.VMEM((1160, 128), F32),
             pltpu.VMEM((2, 1160, 128), F32),
@@ -293,20 +297,26 @@
             pltpu.VMEM((36, 72, 128), F32),
             pltpu.VMEM((40, 32, 512), BF),
             pltpu.VMEM((18, 32, 512), BF),
-            pltpu.VMEM((38, 32, 384), BF),
             pltpu.VMEM((38, 32, 256), F32),
             pltpu.VMEM((18, 32, 512), BF),
             pltpu.VMEM((16, 32, 256), BF),
-            pltpu.VMEM((16, 32, 256), BF),
-            pltpu.VMEM((34, 32, 512), BF),
             pltpu.VMEM((32, 32, 256), BF),
-            pltpu.VMEM((32, 72, 128), F32),
         ],
-        compiler_params=pltpu.CompilerParams(vmem_limit_bytes=18 * 1024 * 1024),
+        compiler_params=pltpu.CompilerParams(vmem_limit_bytes=16 * 1024 * 1024),
         name="level",
     )(
-        x, c, *halo[:2], *pin(*halo[2:]), *pin(w_fwd, w_bwd), w_down, *pin(w_up, w_even, w_odd)
+        x, c, *halo[:2], *pin(*halo[2:]), *pin(w_fwd), w_down, *pin(w_up, w_even, w_odd)
     )
+
+
+def late(f3, coarse_own, g4, w_up, w_bwd):
+    return pl.pallas_call(
+        late_kernel,
+        out_shape=(jax.ShapeDtypeStruct((32, 56, 128), BF),) * 2,
+        scratch_shapes=[pltpu.VMEM((32, 72, 128), F32)],
+        compiler_params=SMALL,
+        name="late",
+    )(*pin(f3, coarse_own, g4, w_up, w_bwd))
 
 
 def pairs(axis):
@@ -389,20 +399,28 @@
     halo = exchange(inputs, cotangent)
     late_conv, _ = lax.optimization_barrier((w_conv, halo[0]))
     weights = prepare_weights(late_conv, w_down, w_up)
-    return level(inputs, cotangent, halo, weights, w_down.reshape(1152, 256))
-
-
-def spread_kernel(received, out, spare, total):
-    total[0:640, :] = jnp.sum(received[...].astype(F32), axis=0)
+    keep, send, *rest = level(inputs, cotangent, halo, weights, w_down.reshape(1152, 256))
+    return keep, send, (*rest, weights[2], weights[1])
+
+
+def spread_kernel(received, out, spare, total, stage):
+    total[...] = jnp.sum(received[...].astype(F32), axis=0)
     spare[...] = jnp.zeros((8, 128), F32)
-    for z in range(8):
-        for y in range(8):
-            first = (y % 2) * 320 + z * 4 + y // 2
-            out[8 * z + y] = total[pl.ds(first, 10, stride=32), :].astype(BF)
-
-
-def finish_kernel(scale, received, conv, down, up):
-    rows = jnp.sum(received[...].astype(F32), axis=0) * scale
+    for k in range(20):
+        first = (k // 10) * 320 + k % 10
+        stage[pl.ds(first, 32, stride=10), :] = total[32 * k : 32 * k + 32, :]
+    out[...] = stage[0:640, :].astype(BF)
+
+
+def finish_kernel(scale, received, conv, down, up, stage):
+    total = received[0:80, :].astype(F32)
+    for chunk in range(1, 8):
+        total = total + received[80 * chunk : 80 * chunk + 80, :].astype(F32)
+    stage[...] = total
+    rows = stage[0:10, :]
+    for holder in range(1, 8):
+        rows = rows + stage[10 * holder : 10 * holder + 10, :]
+    rows = rows * scale
     for which in range(4):
 
         @pl.when(lax.axis_index("col") % 4 == which)
@@ -428,13 +446,13 @@
         for z in range(8) for y in range(8) for k in range(2)
     ]
     plane = [
-        [device(x, y, z, k) for z in range(8) for y in range(8)]
+        [device(x, 2 * y + low, z, k) for low in range(2) for z in range(8) for y in range(4)]
         for x in range(4) for k in range(2)
     ]
     return across, plane
 
 
-def reduce_owners(keep, send, scale):
+def reduce_owners(keep, send, scale, rest):
     mesh = ("row", "col")
     across, plane = coordinates()
     other = lax.ppermute(send, "col", [(i, i ^ 1) for i in range(32)])
@@ -442,26 +460,31 @@
     got = lax.all_to_all(pair, mesh, 0, 0, axis_index_groups=across, tiled=True)
     spread, _ = pl.pallas_call(
         spread_kernel,
-        out_shape=(held((64, 10, 128)), held((8, 128), F32)),
-        scratch_shapes=[pltpu.VMEM((672, 128), F32)],
+        out_shape=(held((640, 128)), held((8, 128), F32)),
+        scratch_shapes=[pltpu.VMEM((640, 128), F32), pltpu.VMEM((656, 128), F32)],
         compiler_params=SMALL,
         name="spread",
     )(*pin(got))
+    first, _ = lax.optimization_barrier((rest[0], spread))
+    rest = (first, *rest[1:])
+    spread = spread.reshape(64, 5, 2, 128)
     got = lax.all_to_all(spread, mesh, 0, 0, axis_index_groups=plane, tiled=True)
+    got = got.reshape(640, 128)
     sums = pl.pallas_call(
         functools.partial(finish_kernel, scale),
         out_shape=tuple(jax.ShapeDtypeStruct((n,), F32) for n in (288, 576, 256)),
+        scratch_shapes=[pltpu.VMEM((80, 128), F32)],
         compiler_params=SMALL,
         name="finish",
     )(*pin(got))
-    return sums
+    return (*late(*rest), *sums)
 
 
 def body(inputs, cotangent, w_conv, w_down, w_up):
-    output, grad_inputs, keep, send = local_terms(inputs, cotangent, w_conv, w_down, w_up)
+    keep, send, rest = local_terms(inputs, cotangent, w_conv, w_down, w_up)
     rows, cols, _ = inputs.shape
     scale = 1.0 / math.sqrt(rows * lax.axis_size("row") * cols * lax.axis_size("col"))
-    return (output, grad_inputs, *reduce_owners(keep, send, scale))
+    return reduce_owners(keep, send, scale, rest)
 
 
 def solution(mesh):

time: 83.3 us -> 80.6 us (0.968)
  blocking collectives: 48.9 us -> 21.8 us
  starting transfers between devices: 17.3 us -> 31.5 us
  waiting for transfers between devices: 5.46 us -> 14.9 us
    all_to_all x1 -> x0, blocking collectives: 27 us -> none  [reduce_owners(): lax.all_to_all(spread, mesh, 0, 0, axis_index_groups=plane, tiled=True)]
    all_to_all x0 -> x1, starting transfers between devices: none -> 14.1 us  [reduce_owners(): lax.all_to_all(spread, mesh, 0, 0, axis_index_groups=plane, tiled=True)]
    all_to_all x0 -> x1, waiting for transfers between devices: none -> 9.44 us  [reduce_owners(): lax.all_to_all(spread, mesh, 0, 0, axis_index_groups=plane, tiled=True)]
    pallas_call x2 -> x3, Pallas kernels: 7.25 us -> 7.33 us  [the longest x1 4.68 us: level(): pl.pallas_call(level_kernel, out_shape=(held((4, 640, 128)), held((4, 640...]
  transfers between devices with their start and end apart: 5 -> 6, of which waited for: 3 -> 4; matrix products, arithmetic and copies ran while one was open for 0% -> 0% of each run, Pallas kernels for 0% -> 3%
where the time goes in v4:
time: 80.6 us; the launch traced here: 80.2 us
  starting transfers between devices  31.5 us (39%)
  blocking collectives  21.8 us (27%)
  waiting for transfers between devices  14.9 us (18%)
  Pallas kernels  10.3 us (13%)
    all_to_all x1, blocking collectives, reduce_owners(): got = lax.all_to_all(pair, mesh, 0, 0, axis_index_groups=across, tiled=True)  21.8 us
    all_to_all x1, starting transfers between devices, reduce_owners(): lax.all_to_all(spread, mesh, 0, 0, axis_index_groups=plane, tiled=True)  14.1 us
    all_to_all x1, waiting for transfers between devices, reduce_owners(): lax.all_to_all(spread, mesh, 0, 0, axis_index_groups=plane, tiled=True)  9.44 us
    ppermute x1, starting transfers between devices, exchange(): col_b = lax.ppermute(second, 'col', odd)  6.49 us
    ppermute x1, starting transfers between devices, exchange(): row_a = lax.ppermute(first, 'row', even)  6.22 us
    pallas_call x1, Pallas kernels, level(): pl.pallas_call(level_kernel, out_shape=(held((4, 640, 128)), held((4, 640...  4.68 us
    ppermute x1, waiting for transfers between devices, reduce_owners(): other = lax.ppermute(send, 'col', [(i, i ^ 1) for i in range(32)])  2.06 us
    pallas_call x1, Pallas kernels, late(): pl.pallas_call(late_kernel, out_shape=(jax.ShapeDtypeStruct((32, 56, 128)...  1.95 us
  transfers between devices with their start and end apart: 6, of which 4 were waited for; matrix products, arithmetic and copies ran while one was open for 0% of the time, Pallas kernels for 3%

profile of v4, /device:TPU:8, one launch (start us, length us, event | category | flops | bytes accessed | tf_op | source)
XLA Modules:
  0.0 80.2 jit_solution(18278640086273519813)
XLA Ops:
  0.6 0.9 %rows.1 = (bf16[6,56,128]{2,1,0:T(8,128)(2,1)S(1)}, bf16[6,56,128]{2,1,0:T(8,128)(2,1)S(1)}) custom-call(bf16[32,56,128]{2,1,0:T(8,128)(2,1)} %x.1, bf16[32,56,128]{2,1,0:T(8,128)(2,1)} %x.1, bf16[32,56,128]{2,1,0:T(8,128)(2,1)} %c.1, bf16[32,56,128]{2,1,0:T(8,128)(2,1)} %c.1), custom_call_target="tpu_custom_call" | custom-call | tf_op jit(solution)/shard_map/rows/pallas_call | solution.py:370
  1.5 0.0 copy-start.2
  1.6 0.0 copy-start.3
  1.6 0.0 copy-start.4
  1.6 6.2 %collective-permute-start = (bf16[6,56,128]{2,1,0:T(8,128)(2,1)S(1)}, bf16[6,56,128]{2,1,0:T(8,128)(2,1)S(1)}, u32[]{:S(2)}, u32[]{:S(2)}) collective-permute-start(bf16[6,56,128]{2,1,0:T(8,128)(2,1)S(1)} %get-tuple-element.27), channel_id=1, source_target_pairs={{0,32},{64,96},{128,160},{192,224},{256,288},{320,352},{384,416},{... | collective-permute-start | bytes 258056 | tf_op jit(solution)/shard_map/ppermute | solution.py:380
  7.8 0.0 copy-start
  7.8 0.0 copy-start.1
  7.8 0.8 collective-permute-start.1
  8.6 1.7 %collective-permute-done.row_a = bf16[6,56,128]{2,1,0:T(8,128)(2,1)S(1)} collective-permute-done((bf16[6,56,128]{2,1,0:T(8,128)(2,1)S(1)}, bf16[6,56,128]{2,1,0:T(8,128)(2,1)S(1)}, u32[]{:S(2)}, u32[]{:S(2)}) %collective-permute-start) | collective-permute-done | bytes 86048 | tf_op jit(solution)/shard_map/ppermute | solution.py:380
  10.3 0.0 collective-permute-done.1.row_b
  10.3 1.1 %cols.1 = (bf16[75,4,128]{2,1,0:T(4,128)(2,1)S(1)}, bf16[75,4,128]{2,1,0:T(4,128)(2,1)S(1)}) custom-call(bf16[32,56,128]{2,1,0:T(8,128)(2,1)} %x.1, bf16[32,56,128]{2,1,0:T(8,128)(2,1)} %x.1, bf16[32,56,128]{2,1,0:T(8,128)(2,1)} %c.1, bf16[32,56,128]{2,1,0:T(8,128)(2,1)} %c.1, bf16[6,56,128]{2,1,0:T(8,128)(2,1)S(1)} %collective-permute-done.row_a, ...), custom_call_target="tpu_custom_call" | custom-call | tf_op jit(solution)/shard_map/cols/pallas_call | solution.py:383
  11.4 1.9 %collective-permute-start.2 = (bf16[75,4,128]{2,1,0:T(4,128)(2,1)S(1)}, bf16[75,4,128]{2,1,0:T(4,128)(2,1)S(1)}, u32[]{:S(2)}, u32[]{:S(2)}) collective-permute-start(bf16[75,4,128]{2,1,0:T(4,128)(2,1)S(1)} %get-tuple-element.29), channel_id=1, source_target_pairs={{0,1},{2,3},{4,5},{6,7},{8,9},{10,11},{12,13},{14,15},{16,17},{18,... | collective-permute-start | bytes 230408 | tf_op jit(solution)/shard_map/ppermute | solution.py:393
  13.3 6.5 %collective-permute-start.3 = (bf16[75,4,128]{2,1,0:T(4,128)(2,1)S(1)}, bf16[75,4,128]{2,1,0:T(4,128)(2,1)S(1)}, u32[]{:S(2)}, u32[]{:S(2)}) collective-permute-start(bf16[75,4,128]{2,1,0:T(4,128)(2,1)S(1)} %get-tuple-element.30), channel_id=1, source_target_pairs={{1,2},{3,4},{5,6},{7,8},{9,10},{11,12},{13,14},{15,16},{17,18},{19... | collective-permute-start | bytes 230408 | tf_op jit(solution)/shard_map/ppermute | solution.py:394
  19.8 0.0 copy-done.2
  19.8 0.0 copy-done.3
  19.9 0.0 copy-done.4
  19.9 0.3 weights.1
  20.2 0.0 collective-permute-done.2.col_a
  20.2 1.7 %collective-permute-done.3.col_b = bf16[75,4,128]{2,1,0:T(4,128)(2,1)S(1)} collective-permute-done((bf16[75,4,128]{2,1,0:T(4,128)(2,1)S(1)}, bf16[75,4,128]{2,1,0:T(4,128)(2,1)S(1)}, u32[]{:S(2)}, u32[]{:S(2)}) %collective-permute-start.3) | collective-permute-done | bytes 76832 | tf_op jit(solution)/shard_map/ppermute | solution.py:394
  21.9 0.0 copy-done
  21.9 0.0 copy-done.1
  21.9 4.7 %level.1 = (bf16[4,640,128]{2,1,0:T(8,128)(2,1)S(1)}, bf16[4,640,128]{2,1,0:T(8,128)(2,1)S(1)}, bf16[38,32,384]{2,1,0:T(8,128)(2,1)S(1)}, bf16[16,32,256]{2,1,0:T(8,128)(2,1)S(1)}, bf16[34,32,512]{2,1,0:T(8,128)(2,1)S(1)}) custom-call(bf16[32,56,128]{2,1,0:T(8,128)(2,1)S(1)} %copy-done, bf16[32,56,128]{2,1,0:T(8,128)(2,1)S(1)} %copy-done.1, ...), custom_call_target="tpu_custom_call" | custom-call | tf_op jit(solution)/shard_map/level/pallas_call | solution.py:281
  26.6 1.9 %collective-permute-start.4 = (bf16[4,640,128]{2,1,0:T(8,128)(2,1)S(1)}, bf16[4,640,128]{2,1,0:T(8,128)(2,1)S(1)}, u32[]{:S(2)}, u32[]{:S(2)}) collective-permute-start(bf16[4,640,128]{2,1,0:T(8,128)(2,1)S(1)} %get-tuple-element.38), channel_id=1, source_target_pairs={{0,1},{1,0},{2,3},{3,2},{4,5},{5,4},{6,7},{7,6},{8,9},{9,8},{10,11... | collective-permute-start | bytes 1966088 | tf_op jit(solution)/shard_map/ppermute | solution.py:458
  28.5 2.1 %collective-permute-done.4 = bf16[4,640,128]{2,1,0:T(8,128)(2,1)S(1)} collective-permute-done((bf16[4,640,128]{2,1,0:T(8,128)(2,1)S(1)}, bf16[4,640,128]{2,1,0:T(8,128)(2,1)S(1)}, u32[]{:S(2)}, u32[]{:S(2)}) %collective-permute-start.4) | collective-permute-done | bytes 655392 | tf_op jit(solution)/shard_map/ppermute | solution.py:458
  30.6 0.2 add_convert_fusion
  30.8 21.8 %all_to_all.10.received = bf16[4,640,128]{2,1,0:T(8,128)(2,1)S(1)} all-to-all(bf16[4,640,128]{2,1,0:T(8,128)(2,1)S(1)} %add_convert_fusion), channel_id=1, replica_groups={{0,128,256,384},{1,129,257,385},{2,130,258,386},{3,131,259,387},{4,132,..., dimensions={0} | all-to-all | bytes 1310720 | tf_op jit(solution)/shard_map/all_to_all | solution.py:460
  52.6 0.7 spread.1
  53.3 0.0 copy-start.5
  53.3 0.7 copy-done.5
  53.9 14.1 %all-to-all-start.1 = ((bf16[64,5,2,128]{3,2,1,0:T(2,128)(2,1)}), bf16[64,5,2,128]{3,2,1,0:T(2,128)(2,1)S(1)}, u32[]{:S(2)}, u32[]{:S(2)}) async-start(bf16[64,5,2,128]{3,2,1,0:T(2,128)(2,1)} %bitcast.5), calls=%async_computation.1 | async-start | bytes 327680 | tf_op jit(solution)/shard_map/all_to_all | solution.py:471
  68.1 1.9 %late.1 = (bf16[32,56,128]{2,1,0:T(8,128)(2,1)}, bf16[32,56,128]{2,1,0:T(8,128)(2,1)}) custom-call(bf16[38,32,384]{2,1,0:T(8,128)(2,1)S(1)} %get-tuple-element.40.f3, bf16[16,32,256]{2,1,0:T(8,128)(2,1)S(1)} %get-tuple-element.41.coarse_own, bf16[34,32,512]{2,1,0:T(8,128)(2,1)S(1)} %get-tuple-element.42.g4, bf16[256,512]{1,0:T(8,128)(2,1)S(1)} %get-tuple-element.33.w_up, ...), custom_call_target="tpu_custom_call" | custom-call | tf_op jit(solution)/shard_map/late/pallas_call | solution.py:313
  70.0 9.4 %all-to-all-done.1 = bf16[64,5,2,128]{3,2,1,0:T(2,128)(2,1)S(1)} async-done(((bf16[64,5,2,128]{3,2,1,0:T(2,128)(2,1)}), bf16[64,5,2,128]{3,2,1,0:T(2,128)(2,1)S(1)}, u32[]{:S(2)}, u32[]{:S(2)}) %all-to-all-start.1) | async-done | bytes 163872 | tf_op jit(solution)/shard_map/all_to_all | solution.py:471
  79.5 0.7 finish.1
Async XLA Ops:
  1.5 18.3 %copy-start.2 = (bf16[3,3,128,256]{3,2,1,0:T(8,128)(2,1)S(1)}, bf16[3,3,128,256]{3,2,1,0:T(8,128)(2,1)}, u32[]{:S(2)}) copy-start(bf16[3,3,128,256]{3,2,1,0:T(8,128)(2,1)} %wd.1) | copy-start | bytes 1769476
  1.6 18.3 %copy-start.3 = (bf16[3,3,128,128]{3,2,1,0:T(8,128)(2,1)S(1)}, bf16[3,3,128,128]{3,2,1,0:T(8,128)(2,1)}, u32[]{:S(2)}) copy-start(bf16[3,3,128,128]{3,2,1,0:T(8,128)(2,1)} %wc) | copy-start | bytes 884740
  1.6 18.3 %copy-start.4 = (bf16[2,2,256,128]{3,2,1,0:T(8,128)(2,1)S(1)}, bf16[2,2,256,128]{3,2,1,0:T(8,128)(2,1)}, u32[]{:S(2)}) copy-start(bf16[2,2,256,128]{3,2,1,0:T(8,128)(2,1)} %wu.1) | copy-start | bytes 786436
  1.6 8.8 %collective-permute-start = (bf16[6,56,128]{2,1,0:T(8,128)(2,1)S(1)}, bf16[6,56,128]{2,1,0:T(8,128)(2,1)S(1)}, u32[]{:S(2)}, u32[]{:S(2)}) collective-permute-start(bf16[6,56,128]{2,1,0:T(8,128)(2,1)S(1)} %get-tuple-element.27), channel_id=1, source_target_pairs={{0,32},{64,96},{128,160},{192,224},{256,288},{320,352},{384,416},{... | collective-permute-start | bytes 258056 | tf_op jit(solution)/shard_map/ppermute | solution.py:380
  7.8 14.1 %copy-start = (bf16[32,56,128]{2,1,0:T(8,128)(2,1)S(1)}, bf16[32,56,128]{2,1,0:T(8,128)(2,1)}, u32[]{:S(2)}) copy-start(bf16[32,56,128]{2,1,0:T(8,128)(2,1)} %x.1) | copy-start | bytes 1376260
  7.8 14.1 %copy-start.1 = (bf16[32,56,128]{2,1,0:T(8,128)(2,1)S(1)}, bf16[32,56,128]{2,1,0:T(8,128)(2,1)}, u32[]{:S(2)}) copy-start(bf16[32,56,128]{2,1,0:T(8,128)(2,1)} %c.1) | copy-start | bytes 1376260
  7.8 2.5 %collective-permute-start.1 = (bf16[6,56,128]{2,1,0:T(8,128)(2,1)S(1)}, bf16[6,56,128]{2,1,0:T(8,128)(2,1)S(1)}, u32[]{:S(2)}, u32[]{:S(2)}) collective-permute-start(bf16[6,56,128]{2,1,0:T(8,128)(2,1)S(1)} %get-tuple-element.28), channel_id=1, source_target_pairs={{32,64},{96,128},{160,192},{224,256},{288,320},{352,384},{416,448}... | collective-permute-start | bytes 258056 | tf_op jit(solution)/shard_map/ppermute | solution.py:381
  11.4 8.8 %collective-permute-start.2 = (bf16[75,4,128]{2,1,0:T(4,128)(2,1)S(1)}, bf16[75,4,128]{2,1,0:T(4,128)(2,1)S(1)}, u32[]{:S(2)}, u32[]{:S(2)}) collective-permute-start(bf16[75,4,128]{2,1,0:T(4,128)(2,1)S(1)} %get-tuple-element.29), channel_id=1, source_target_pairs={{0,1},{2,3},{4,5},{6,7},{8,9},{10,11},{12,13},{14,15},{16,17},{18,... | collective-permute-start | bytes 230408 | tf_op jit(solution)/shard_map/ppermute | solution.py:393
  13.3 8.6 %collective-permute-start.3 = (bf16[75,4,128]{2,1,0:T(4,128)(2,1)S(1)}, bf16[75,4,128]{2,1,0:T(4,128)(2,1)S(1)}, u32[]{:S(2)}, u32[]{:S(2)}) collective-permute-start(bf16[75,4,128]{2,1,0:T(4,128)(2,1)S(1)} %get-tuple-element.30), channel_id=1, source_target_pairs={{1,2},{3,4},{5,6},{7,8},{9,10},{11,12},{13,14},{15,16},{17,18},{19... | collective-permute-start | bytes 230408 | tf_op jit(solution)/shard_map/ppermute | solution.py:394
  26.6 4.0 %collective-permute-start.4 = (bf16[4,640,128]{2,1,0:T(8,128)(2,1)S(1)}, bf16[4,640,128]{2,1,0:T(8,128)(2,1)S(1)}, u32[]{:S(2)}, u32[]{:S(2)}) collective-permute-start(bf16[4,640,128]{2,1,0:T(8,128)(2,1)S(1)} %get-tuple-element.38), channel_id=1, source_target_pairs={{0,1},{1,0},{2,3},{3,2},{4,5},{5,4},{6,7},{7,6},{8,9},{9,8},{10,11... | collective-permute-start | bytes 1966088 | tf_op jit(solution)/shard_map/ppermute | solution.py:458
  53.3 0.7 copy-start.5
  53.9 25.5 %all-to-all-start.1 = ((bf16[64,5,2,128]{3,2,1,0:T(2,128)(2,1)}), bf16[64,5,2,128]{3,2,1,0:T(2,128)(2,1)S(1)}, u32[]{:S(2)}, u32[]{:S(2)}) async-start(bf16[64,5,2,128]{3,2,1,0:T(2,128)(2,1)} %bitcast.5), calls=%async_computation.1 | async-start | bytes 327680 | tf_op jit(solution)/shard_map/all_to_all | solution.py:471

commit v5 on v4

v5 whole, which is shorter than its diff:
```python
import functools
import math

import jax
import jax.numpy as jnp
from jax import lax
from jax.experimental import pallas as pl
from jax.experimental.pallas import tpu as pltpu
from jax.sharding import PartitionSpec as P

BF = jnp.bfloat16
F32 = jnp.float32
NN = (((1,), (0,)), ((), ()))
NT = (((1,), (1,)), ((), ()))
TN = (((0,), (0,)), ((), ()))
SMALL = pltpu.CompilerParams(vmem_limit_bytes=8 * 1024 * 1024)


def held(shape, dtype=BF):
    return pltpu.VMEM(shape, dtype)


def far(*arrays):
    return tuple(pltpu.with_memory_space_constraint(a, pltpu.HBM) for a in arrays)


def pin(*arrays):
    return tuple(pltpu.with_memory_space_constraint(a, pltpu.VMEM) for a in arrays)


def swapped(odd, one, two):
    one, two = one[...].astype(F32), two[...].astype(F32)
    return jnp.where(odd, two, one), jnp.where(odd, one, two)


def mm(left, right, dims):
    return lax.dot_general(left, right, dims, preferred_element_type=F32)


def sigmoid(value):
    return 1.0 / (1.0 + jnp.exp(-value))


def weights_kernel(wc, wd, wu, conv_fwd, conv_bwd, up, down_even, down_odd):
    zero = jnp.zeros((128, 128), BF)
    for p in range(3):
        for blk in range(4):
            rows = slice(blk * 128, (blk + 1) * 128)
            conv_fwd[p, rows, 0:128] = wc[p, blk] if blk < 3 else zero
            conv_fwd[p, rows, 128:256] = wc[p, blk - 1] if blk > 0 else zero
            conv_bwd[p, 0:128, rows] = wc[p, 2 - blk] if blk < 3 else zero
            conv_bwd[p, 128:256, rows] = wc[p, 3 - blk] if blk > 0 else zero
    for p in range(2):
        for q in range(2):
            up[:, (2 * p + q) * 128 : (2 * p + q + 1) * 128] = wu[p, q]
    wide = jnp.zeros((128, 256), BF)
    down_even[0:128, 0:256] = wd[1, 1]
    down_even[0:128, 256:512] = wide
    down_even[128:256, 0:256] = wd[1, 2]
    down_even[128:256, 256:512] = wd[1, 0]
    down_odd[0:128, 0:256] = wd[2, 1]
    down_odd[0:128, 256:512] = wide
    down_odd[0:128, 512:768] = wd[0, 1]
    down_odd[0:128, 768:1024] = wide
    down_odd[128:256, 0:256] = wd[2, 2]
    down_odd[128:256, 256:512] = wd[2, 0]
    down_odd[128:256, 512:768] = wd[0, 2]
    down_odd[128:256, 768:1024] = wd[0, 0]


def prepare_weights(w_conv, w_down, w_up):
    shapes = ((3, 512, 256), (3, 256, 512), (256, 512), (256, 512), (256, 1024))
    return pl.pallas_call(
        weights_kernel,
        out_shape=tuple(held(s) for s in shapes),
        compiler_params=SMALL,
        name="weights",
    )(w_conv, w_down, w_up)


CONV_ROWS = ((0, 1, 2), (2, 3, 4), (4, 5, 6), (6, 7, 8))
DOWN_ROWS = ((0, 1, 2, 3, 4), (4, 5, 6, 7, 8), (9, 10, 11, 12, 13), (13, 14, 15, 16, 17))
UP_ROWS = ((0, 1), (2, 3), (4, 5), (6, 7))


def pack(core, ref, conv_acc, down_acc, up_acc):
    k = 0
    for owner in (core, core + 2):
        for row in CONV_ROWS[owner]:
            value = conv_acc[pl.ds(row, 128, stride=9), :]
            ref[:, 32 * k : 32 * k + 32, :] = value.reshape(4, 32, 128).astype(BF)
            k += 1
        for row in DOWN_ROWS[owner]:
            value = down_acc[row % 2, pl.ds(row // 2, 128, stride=9), :]
            ref[:, 32 * k : 32 * k + 32, :] = value.reshape(4, 32, 128).astype(BF)
            k += 1
        for row in UP_ROWS[owner]:
            value = up_acc[pl.ds(row, 128, stride=8), :]
            ref[:, 32 * k : 32 * k + 32, :] = value.reshape(4, 32, 128).astype(BF)
            k += 1


def rows_at(parts, indices):
    found = []
    for index in indices:
        for first, count, ref, place in parts:
            if first <= index < first + count:
                found.append(ref[place + index - first])
                break
    return jnp.concatenate(found, axis=0)


def x4_parts(inner, rim):
    return ((0, 4, rim, 0), (4, 32, inner, 0), (36, 4, rim, 4))


def c4_parts(inner, rim):
    return ((0, 1, rim, 0), (1, 16, inner, 0), (17, 1, rim, 1))


def f3_parts(inner, rim):
    return ((0, 4, rim, 0), (4, 30, inner, 0), (34, 4, rim, 4))


def gs_parts(inner, rim):
    return ((0, 2, rim, 0), (2, 14, inner, 0), (16, 2, rim, 2))


def own_parts(inner, rim):
    return ((0, 1, rim, 0), (1, 14, inner, 0), (15, 1, rim, 1))


def column_masks():
    at_col = lax.axis_index("col")
    half = lax.broadcasted_iota(jnp.int32, (32, 256), 0) - 2
    own = (half >= 0) & (half < 28)
    last = lax.axis_size("col") - 1
    in_grid = ((half >= 0) | (at_col != 0)) & ((half < 28) | (at_col != last))
    return jnp.where(in_grid, 1.0, 0.0), jnp.where(own, 1.0, 0.0)


def row_masks():
    at_row = lax.axis_index("row")
    last = lax.axis_size("row") - 1
    return jnp.where(at_row == 0, 0.0, 1.0), jnp.where(at_row == last, 0.0, 1.0)


def per_row(value, mask):
    count = value.shape[0] // 32
    return (value.reshape(count, 32, 256) * mask[None]).reshape(count * 32, 256)


def clear_sides(ref):
    ref[:, 0:8, :] = jnp.zeros((ref.shape[0], 8, 128), F32)
    ref[:, 64:72, :] = jnp.zeros((ref.shape[0], 8, 128), F32)


def split_x(xs, x4, places):
    for r, place in enumerate(places):
        for k in range(4):
            x4[place, :, k * 128 : (k + 1) * 128] = xs[r, pl.ds(3 + k, 32, stride=2), :].astype(BF)


def split_c(cs, c4):
    for ai in range(c4.shape[0]):
        for p in range(2):
            for q in range(2):
                k = 2 * p + q
                c4[ai, :, k * 128 : (k + 1) * 128] = cs[
                    2 * ai + p, pl.ds(4 + q, 32, stride=2), :
                ].astype(BF)


def fine_rows(x4, indices, w_fwd, in_grid):
    pre = None
    for p in range(3):
        term = mm(rows_at(x4, [i + p for i in indices]), w_fwd[p], NN)
        pre = term if pre is None else pre + term
    sig = sigmoid(pre)
    return per_row(pre * sig, in_grid), sig * (1.0 + pre * (1.0 - sig))


def store_fine(fine, slopes, f3, slope, first, count):
    behind = pltpu.roll(fine[:, 128:256], 1, 0).astype(BF).reshape(count, 32, 128)
    f3[first : first + count, :, 0:128] = behind
    f3[first : first + count, :, 128:384] = fine.astype(BF).reshape(count, 32, 256)
    slope[first : first + count] = slopes.reshape(count, 32, 256)


def coarse_rows(f3, c4, ais, w_down, w_up):
    parts = [rows_at(f3, [2 * ai + p for ai in ais]) for p in range(3)]
    cpre = mm(jnp.concatenate(parts, axis=1), w_down[...], NN)
    sig = sigmoid(cpre)
    grad = mm(rows_at(c4, ais), w_up[...], NT) * (sig * (1.0 + cpre * (1.0 - sig)))
    return cpre * sig, grad


def store_coarse(grad, gs, first, count):
    ahead = pltpu.roll(grad, count * 32 - 1, 0)
    gs[first : first + count, :, 0:256] = grad.astype(BF).reshape(count, 32, 256)
    gs[first : first + count, :, 256:512] = ahead.astype(BF).reshape(count, 32, 256)


def early_kernel(
    x, c, col_a, col_b, w_fwd, w_down, w_up,
    x4, c4, f3, slope, gs, coarse_own, g_own,
    xs, cs,
):
    left, right = swapped(lax.axis_index("col") % 2 == 1, col_b, col_a)
    for ref, own_block, first in ((xs, x, 0), (cs, c, 32)):
        clear_sides(ref)
        ref[:, 8:64, :] = own_block[...].astype(F32)
        ref[:, 4:8, :] = left[first : first + 32]
        ref[:, 64:68, :] = right[first : first + 32]
    split_x(xs, x4, range(32))
    split_c(cs, c4)
    in_grid, own = column_masks()
    for first, count in ((4, 8), (12, 8), (20, 8), (28, 6)):
        fine, slopes = fine_rows(
            x4_parts(x4, None), range(first, first + count), w_fwd, in_grid
        )
        store_fine(fine, slopes, f3, slope, first - 4, count)
    for first in (2, 9):
        coarse, grad = coarse_rows(
            f3_parts(f3, None), c4_parts(c4, None), range(first, first + 7), w_down, w_up
        )
        store_coarse(grad, gs, first - 2, 7)
        coarse_own[first - 2 : first + 5] = per_row(coarse, own).astype(BF).reshape(7, 32, 256)
        g_own[first - 2 : first + 5] = per_row(grad, own).astype(BF).reshape(7, 32, 256)


def level_kernel(
    row_a, row_b, x4_in, c4_in, f3_in, slope_in, gs_in, coarse_in, g_in,
    w_fwd, w_down, w_up, w_even, w_odd,
    keep, send, f3_rim, coarse_rim, g4,
    conv_acc, down_acc, up_acc, xs, cs, x4_rim, c4_rim, slope_rim, gs_rim, g_rim, pre_own,
):
    top, bot = swapped(lax.axis_index("row") % 2 == 1, row_b, row_a)
    for ref, at, value in (
        (xs, slice(0, 4), top[0:4]), (xs, slice(4, 7), bot[0:3]),
        (cs, slice(0, 2), top[4:6]), (cs, slice(2, 4), bot[4:6]),
    ):
        ref[at, 0:8, :] = jnp.zeros((value.shape[0], 8, 128), F32)
        ref[at, 64:72, :] = jnp.zeros((value.shape[0], 8, 128), F32)
        ref[at, 8:68, :] = value[:, 0:60]
        ref[at, 4:8, :] = value[:, 60:64]
    split_x(xs, x4_rim, range(7))
    x4_rim[7] = jnp.zeros((32, 512), BF)
    split_c(cs, c4_rim)
    in_grid, own = column_masks()
    keep_top, keep_bot = row_masks()
    x4, c4 = x4_parts(x4_in, x4_rim), c4_parts(c4_in, c4_rim)
    f3, slope = f3_parts(f3_in, f3_rim), f3_parts(slope_in, slope_rim)
    gs = gs_parts(gs_in, gs_rim)

    fine, slopes = fine_rows(x4, (0, 1, 2, 3, 34, 35, 36, 37), w_fwd, in_grid)
    fine = jnp.concatenate(
        [fine[0:96] * keep_top, fine[96:160], fine[160:256] * keep_bot], axis=0
    )
    store_fine(fine, slopes, f3_rim, slope_rim, 0, 8)

    coarse, grad = coarse_rows(f3, c4, (0, 1, 16, 17), w_down, w_up)
    store_coarse(grad, gs_rim, 0, 4)
    coarse_rim[...] = per_row(coarse[32:96], own).astype(BF).reshape(2, 32, 256)
    g_rim[...] = per_row(grad[32:96], own).astype(BF).reshape(2, 32, 256)

    coarse_flat = rows_at(own_parts(coarse_in, coarse_rim), range(16))
    res = mm(coarse_flat, rows_at(c4, range(1, 17)), TN)
    for k in range(4):
        up_acc[k * 256 : (k + 1) * 256, :] = res[:, k * 128 : (k + 1) * 128]
    g_flat = rows_at(own_parts(g_in, g_rim), range(16))
    for p in range(3):
        res = mm(rows_at(f3, [2 * a + p + 2 for a in range(16)]), g_flat, TN)
        for side in range(2):
            down_acc[side, p * 384 : (p + 1) * 384, :] = res[:, side * 128 : (side + 1) * 128]

    for first, count in ((0, 9), (9, 8)):
        ais = range(first, first + count)
        nexts = range(first + 1, first + 1 + count)
        for odd in (True, False):
            below = rows_at(gs, nexts)
            if odd:
                spread = mm(jnp.concatenate([rows_at(gs, ais), below], axis=1), w_odd[...], NT)
                cot = rows_at(c4, ais)[:, 256:512]
                at = 2
            else:
                spread = mm(below, w_even[...], NT)
                cot = rows_at(c4, nexts)[:, 0:256]
                at = 3
            slopes = rows_at(slope, [2 * ai + at for ai in ais])
            grad = per_row((cot.astype(F32) + spread) * slopes, in_grid)
            if first == 0 and odd:
                grad = jnp.concatenate([grad[0:32] * keep_top, grad[32:]], axis=0)
            if first != 0 and not odd:
                edge = (count - 1) * 32
                grad = jnp.concatenate([grad[:edge], grad[edge:] * keep_bot], axis=0)
            behind = pltpu.roll(grad[:, 128:256], 1, 0).astype(BF)
            ahead = pltpu.roll(grad[:, 0:128], count * 32 - 1, 0).astype(BF)
            rounded = grad.astype(BF)
            kept = per_row(grad, own).astype(BF)
            for ai in ais:
                g_row = 2 * ai + (0 if odd else 1)
                rows = slice((ai - first) * 32, (ai - first + 1) * 32)
                g4[g_row, :, 0:128] = behind[rows]
                g4[g_row, :, 128:384] = rounded[rows]
                g4[g_row, :, 384:512] = ahead[rows]
                if 1 <= g_row <= 32:
                    pre_own[g_row - 1] = kept[rows]

    flat = pre_own[...].reshape(1024, 256)
    for p in range(3):
        res = mm(flat, rows_at(x4, range(p + 3, p + 35)), TN)
        for q in range(3):
            tap = res[0:128, q * 128 : (q + 1) * 128] + res[128:256, (q + 1) * 128 : (q + 2) * 128]
            conv_acc[(3 * p + q) * 128 : (3 * p + q + 1) * 128, :] = tap.T

    odd_col = lax.axis_index("col") % 2 == 1

    @pl.when(jnp.logical_not(odd_col))
    def _():
        pack(0, keep, conv_acc, down_acc, up_acc)
        pack(1, send, conv_acc, down_acc, up_acc)

    @pl.when(odd_col)
    def _():
        pack(1, keep, conv_acc, down_acc, up_acc)
        pack(0, send, conv_acc, down_acc, up_acc)


def late_kernel(f3_in, f3_rim, coarse_in, coarse_rim, g4, w_up, w_bwd, out, gx, mix):
    f3 = f3_parts(f3_in, f3_rim)
    coarse = own_parts(coarse_in, coarse_rim)
    for first in (0, 8):
        up = mm(rows_at(coarse, range(first, first + 8)), w_up[...], NN)
        for a in range(first, first + 8):
            for p in range(2):
                for q in range(2):
                    k = 2 * p + q
                    value = up[(a - first) * 32 : (a - first + 1) * 32, k * 128 : (k + 1) * 128]
                    fine = rows_at(f3, [2 * a + p + 3])[:, 128 + q * 128 : 256 + q * 128]
                    value = value + fine.astype(F32)
                    mix[2 * a + p, pl.ds(4 + q, 32, stride=2), :] = value
    out[...] = mix[:, 8:64, :].astype(BF)
    for first in (0, 8, 16, 24):
        total = None
        for p in range(3):
            window = g4[first + 2 - p : first + 10 - p].reshape(256, 512)
            term = mm(window, w_bwd[p], NT)
            total = term if total is None else total + term
        for i in range(first, first + 8):
            for q in range(2):
                mix[i, pl.ds(4 + q, 32, stride=2), :] = total[
                    (i - first) * 32 : (i - first + 1) * 32, q * 128 : (q + 1) * 128
                ]
    gx[...] = mix[:, 8:64, :].astype(BF)


LARGE = pltpu.CompilerParams(vmem_limit_bytes=14 * 1024 * 1024)


def early(x, c, cols, weights, w_down):
    return pl.pallas_call(
        early_kernel,
        out_shape=(
            held((32, 32, 512)),
            held((16, 32, 512)),
            held((30, 32, 384)),
            held((30, 32, 256), F32),
            held((14, 32, 512)),
            held((14, 32, 256)),
            held((14, 32, 256)),
        ),
        scratch_shapes=[pltpu.VMEM((32, 72, 128), F32)] * 2,
        compiler_params=LARGE,
        name="early",
    )(x, c, *pin(*cols, weights[0]), w_down, *pin(weights[2]))


def level(rows, inner, weights, w_down):
    w_fwd, w_bwd, w_up, w_even, w_odd = weights
    return pl.pallas_call(
        level_kernel,
        out_shape=(
            held((4, 640, 128)),
            held((4, 640, 128)),
            held((8, 32, 384)),
            held((2, 32, 256)),
            held((34, 32, 512)),
        ),
        scratch_shapes=[
            pltpu.VMEM((1160, 128), F32),
            pltpu.VMEM((2, 1160, 128), F32),
            pltpu.VMEM((1032, 128), F32),
            pltpu.VMEM((7, 72, 128), F32),
            pltpu.VMEM((4, 72, 128), F32),
            pltpu.VMEM((8, 32, 512), BF),
            pltpu.VMEM((2, 32, 512), BF),
            pltpu.VMEM((8, 32, 256), F32),
            pltpu.VMEM((4, 32, 512), BF),
            pltpu.VMEM((2, 32, 256), BF),
            pltpu.VMEM((32, 32, 256), BF),
        ],
        compiler_params=LARGE,
        name="level",
    )(*pin(*rows, *inner, w_fwd), w_down, *pin(w_up, w_even, w_odd))


def late(*args):
    return pl.pallas_call(
        late_kernel,
        out_shape=(jax.ShapeDtypeStruct((32, 56, 128), BF),) * 2,
        scratch_shapes=[pltpu.VMEM((32, 72, 128), F32)],
        compiler_params=SMALL,
        name="late",
    )(*pin(*args))


def pairs(axis):
    count = lax.axis_size(axis)
    both = []
    for first in (0, 1):
        swaps = [(i, i + 1) for i in range(first, count - 1, 2)]
        both.append(swaps + [(b, a) for a, b in swaps])
    return both


def store_pair(odd, forward, backward, even_first, odd_first):
    even_first[...] = jnp.where(odd, backward, forward).astype(BF)
    odd_first[...] = jnp.where(odd, forward, backward).astype(BF)


def cols_kernel(x_last, x_first, c_last, c_first, col_a, col_b):
    rightward = jnp.concatenate([x_last[:, 4:8], c_last[:, 4:8]], axis=0).astype(F32)
    leftward = jnp.concatenate([x_first[:, 0:4], c_first[:, 0:4]], axis=0).astype(F32)
    store_pair(lax.axis_index("col") % 2 == 1, rightward, leftward, col_a, col_b)


def rows_kernel(x_last, x_first, c_last, c_first, col_a, col_b, row_a, row_b):
    left, right = swapped(lax.axis_index("col") % 2 == 1, col_b, col_a)

    def side(x, c, x_rows, c_rows):
        own = jnp.concatenate([x[...], c[...]], axis=0).astype(F32)
        after = jnp.concatenate([right[x_rows], right[c_rows]], axis=0)
        before = jnp.concatenate([left[x_rows], left[c_rows]], axis=0)
        return jnp.concatenate([own, after, before], axis=1)

    down = side(x_last, c_last, slice(28, 32), slice(62, 64))
    up = side(x_first, c_first, slice(0, 4), slice(32, 34))
    store_pair(lax.axis_index("row") % 2 == 1, down, up, row_a, row_b)


def row_block(count, at):
    return pl.BlockSpec((count, 56, 128), lambda i: (at, 0, 0))


def col_block(at):
    return pl.BlockSpec((32, 8, 128), lambda i: (0, at, 0))


def column_halo(x, c):
    whole = pl.BlockSpec((64, 4, 128), lambda i: (0, 0, 0))
    first, second = pl.pallas_call(
        cols_kernel,
        grid=(1,),
        out_shape=(jax.ShapeDtypeStruct((64, 4, 128), BF),) * 2,
        in_specs=[col_block(at) for at in (6, 0, 6, 0)],
        out_specs=(whole, whole),
        compiler_params=SMALL,
        name="cols",
    )(*far(x, x, c, c))
    even, odd = pairs("col")
    return lax.ppermute(first, "col", even), lax.ppermute(second, "col", odd)


def row_halo(x, c, cols):
    whole = pl.BlockSpec((6, 64, 128), lambda i: (0, 0, 0))
    first, second = pl.pallas_call(
        rows_kernel,
        grid=(1,),
        out_shape=(jax.ShapeDtypeStruct((6, 64, 128), BF),) * 2,
        in_specs=[row_block(4, 7), row_block(4, 0), row_block(2, 15), row_block(2, 0)]
        + [pl.BlockSpec((64, 4, 128), lambda i: (0, 0, 0))] * 2,
        out_specs=(whole, whole),
        compiler_params=SMALL,
        name="rows",
    )(*far(x, x, c, c), *pin(*cols))
    even, odd = pairs("row")
    return lax.ppermute(first, "row", even), lax.ppermute(second, "row", odd)


def local_terms(inputs, cotangent, w_conv, w_down, w_up):
    flat_down = w_down.reshape(1152, 256)
    weights = prepare_weights(w_conv, w_down, w_up)
    cols = column_halo(inputs, cotangent)
    rows = row_halo(inputs, cotangent, cols)
    inner = early(inputs, cotangent, cols, weights, flat_down)
    keep, send, f3_rim, coarse_rim, g4 = level(rows, inner, weights, flat_down)
    return keep, send, (inner[2], f3_rim, inner[5], coarse_rim, g4, weights[2], weights[1])


def spread_kernel(received, out, total, stage):
    total[...] = jnp.sum(received[...].astype(F32), axis=0)
    for k in range(20):
        first = (k // 10) * 320 + k % 10
        stage[pl.ds(first, 32, stride=10), :] = total[32 * k : 32 * k + 32, :]
    out[...] = stage[0:640, :].astype(BF)


def finish_kernel(scale, received, conv, down, up, stage):
    total = received[0:80, :].astype(F32)
    for chunk in range(1, 8):
        total = total + received[80 * chunk : 80 * chunk + 80, :].astype(F32)
    stage[...] = total
    rows = stage[0:10, :]
    for holder in range(1, 8):
        rows = rows + stage[10 * holder : 10 * holder + 10, :]
    rows = rows * scale
    for which in range(4):

        @pl.when(lax.axis_index("col") % 4 == which)
        def _():
            for ref, base, names, size in (
                (conv, 0, CONV_ROWS, 288), (down, 3, DOWN_ROWS, 576), (up, 8, UP_ROWS, 256)
            ):
                start = (base - names[which][0]) * 128 + which * size
                done = 0
                while done < size:
                    row, lane = divmod(start + done, 128)
                    count = min(128 - lane, size - done)
                    ref[pl.ds(done, count)] = rows[row, lane : lane + count]
                    done += count


def coordinates():
    def device(x, y, z, core):
        return (x * 4 + z // 2) * 32 + (z % 2) * 16 + y * 2 + core

    across = [
        [device(x, y, z, k) for x in range(4)]
        for z in range(8) for y in range(8) for k in range(2)
    ]
    plane = [
        [device(x, 2 * y + low, z, k) for low in range(2) for z in range(8) for y in range(4)]
        for x in range(4) for k in range(2)
    ]
    return across, plane


def reduce_owners(keep, send, scale, rest):
    mesh = ("row", "col")
    across, plane = coordinates()
    other = lax.ppermute(send, "col", [(i, i ^ 1) for i in range(32)])
    pair = (keep.astype(F32) + other.astype(F32)).astype(BF)
    got = lax.all_to_all(pair, mesh, 0, 0, axis_index_groups=across, tiled=True)
    spread = pl.pallas_call(
        spread_kernel,
        out_shape=jax.ShapeDtypeStruct((640, 128), BF),
        scratch_shapes=[pltpu.VMEM((640, 128), F32), pltpu.VMEM((656, 128), F32)],
        compiler_params=SMALL,
        name="spread",
    )(*pin(got))
    g4, _ = lax.optimization_barrier((rest[4], spread))
    rest = (*rest[:4], g4, *rest[5:])
    spread = spread.reshape(64, 5, 2, 128)
    got = lax.all_to_all(spread, mesh, 0, 0, axis_index_groups=plane, tiled=True)
    got = got.reshape(640, 128)
    sums = pl.pallas_call(
        functools.partial(finish_kernel, scale),
        out_shape=tuple(jax.ShapeDtypeStruct((n,), F32) for n in (288, 576, 256)),
        scratch_shapes=[pltpu.VMEM((80, 128), F32)],
        compiler_params=SMALL,
        name="finish",
    )(*pin(got))
    return (*late(*rest), *sums)


def body(inputs, cotangent, w_conv, w_down, w_up):
    keep, send, rest = local_terms(inputs, cotangent, w_conv, w_down, w_up)
    rows, cols, _ = inputs.shape
    scale = 1.0 / math.sqrt(rows * lax.axis_size("row") * cols * lax.axis_size("col"))
    return reduce_owners(keep, send, scale, rest)


def solution(mesh):
    grid = P("row", "col", None)
    flat = P(("row", "col"))
    return jax.shard_map(
        body,
        mesh=mesh,
        in_specs=(grid, grid, P(), P(), P()),
        out_specs=(grid, grid, flat, flat, flat),
        check_vma=False,
    )
```

time: 80.6 us -> 78.8 us (0.978)
  starting transfers between devices: 31.5 us -> 28.9 us
  waiting for transfers between devices: 14.9 us -> 16.7 us
  blocking collectives: 21.8 us -> 20.8 us
    ppermute x4, starting transfers between devices: 15.4 us -> 12.6 us  [the longest x2 10 us: column_halo(): return (lax.ppermute(first, 'col', even), lax.ppermute(second, 'col', odd))]
    pallas_call x3 -> x4, Pallas kernels: 2.68 us -> 4.71 us  [the longest x1 1.94 us: early(): pl.pallas_call(early_kernel, out_shape=(held((32, 32, 512)), held((16, 32...]
    ppermute x4, waiting for transfers between devices: 3.4 us -> 5.23 us  [the longest x2 3.3 us: row_halo(): return (lax.ppermute(first, 'row', even), lax.ppermute(second, 'row', odd))]
    pallas_call x1, Pallas kernels: 4.68 us -> 3.27 us  [level(): pl.pallas_call(level_kernel, out_shape=(held((4, 640, 128)), held((4, 640...]
    all_to_all x1, blocking collectives: 21.8 us -> 20.8 us  [reduce_owners(): got = lax.all_to_all(pair, mesh, 0, 0, axis_index_groups=across, tiled=True)]
  transfers between devices with their start and end apart: 6 -> 6, of which waited for: 4 -> 4; matrix products, arithmetic and copies ran while one was open for 0% -> 0% of each run, Pallas kernels for 3% -> 5%
where the time goes in v5:
time: 78.8 us; the launch traced here: 78.3 us
  starting transfers between devices  28.9 us (37%)
  blocking collectives  20.8 us (26%)
  waiting for transfers between devices  16.7 us (21%)
  Pallas kernels  10.9 us (14%)
  between operations  0.8 us (1%)
    all_to_all x1, blocking collectives, reduce_owners(): got = lax.all_to_all(pair, mesh, 0, 0, axis_index_groups=across, tiled=True)  20.8 us
    all_to_all x1, starting transfers between devices, reduce_owners(): lax.all_to_all(spread, mesh, 0, 0, axis_index_groups=plane, tiled=True)  14.3 us
    ppermute x2, starting transfers between devices, column_halo(): return (lax.ppermute(first, 'col', even), lax.ppermute(second, 'col', odd))  10 us
    all_to_all x1, waiting for transfers between devices, reduce_owners(): lax.all_to_all(spread, mesh, 0, 0, axis_index_groups=plane, tiled=True)  9.44 us
    ppermute x2, waiting for transfers between devices, row_halo(): return (lax.ppermute(first, 'row', even), lax.ppermute(second, 'row', odd))  3.3 us
    pallas_call x1, Pallas kernels, level(): pl.pallas_call(level_kernel, out_shape=(held((4, 640, 128)), held((4, 640...  3.27 us
    ppermute x2, starting transfers between devices, row_halo(): return (lax.ppermute(first, 'row', even), lax.ppermute(second, 'row', odd))  2.59 us
    ppermute x1, waiting for transfers between devices, reduce_owners(): other = lax.ppermute(send, 'col', [(i, i ^ 1) for i in range(32)])  2.06 us
  transfers between devices with their start and end apart: 6, of which 4 were waited for; matrix products, arithmetic and copies ran while one was open for 0% of the time, Pallas kernels for 5%

profile of v5, /device:TPU:8, one launch (start us, length us, event | category | flops | bytes accessed | tf_op | source)
XLA Modules:
  0.0 78.3 jit_solution(6389235356445076428)
XLA Ops:
  0.6 1.1 %cols.1 = (bf16[64,4,128]{2,1,0:T(4,128)(2,1)S(1)}, bf16[64,4,128]{2,1,0:T(4,128)(2,1)S(1)}) custom-call(bf16[32,56,128]{2,1,0:T(8,128)(2,1)} %x_first.3, bf16[32,56,128]{2,1,0:T(8,128)(2,1)} %x_first.3, bf16[32,56,128]{2,1,0:T(8,128)(2,1)} %c_first.3, bf16[32,56,128]{2,1,0:T(8,128)(2,1)} %c_first.3), custom_call_target="tpu_custom_call" | custom-call | tf_op jit(solution)/shard_map/cols/pallas_call | solution.py:462
  1.7 0.0 copy-start.2
  1.7 0.0 copy-start.3
  1.7 0.0 copy-start.4
  1.7 2.1 %collective-permute-start = (bf16[64,4,128]{2,1,0:T(4,128)(2,1)S(1)}, bf16[64,4,128]{2,1,0:T(4,128)(2,1)S(1)}, u32[]{:S(2)}, u32[]{:S(2)}) collective-permute-start(bf16[64,4,128]{2,1,0:T(4,128)(2,1)S(1)} %get-tuple-element.32), channel_id=1, source_target_pairs={{0,1},{2,3},{4,5},{6,7},{8,9},{10,11},{12,13},{14,15},{16,17},{18,... | collective-permute-start | bytes 196616 | tf_op jit(solution)/shard_map/ppermute | solution.py:472
  3.8 0.0 copy-start
  3.8 0.0 copy-start.1
  3.8 8.0 %collective-permute-start.1 = (bf16[64,4,128]{2,1,0:T(4,128)(2,1)S(1)}, bf16[64,4,128]{2,1,0:T(4,128)(2,1)S(1)}, u32[]{:S(2)}, u32[]{:S(2)}) collective-permute-start(bf16[64,4,128]{2,1,0:T(4,128)(2,1)S(1)} %get-tuple-element.33), channel_id=1, source_target_pairs={{1,2},{3,4},{5,6},{7,8},{9,10},{11,12},{13,14},{15,16},{17,18},{19... | collective-permute-start | bytes 196616 | tf_op jit(solution)/shard_map/ppermute | solution.py:472
  11.8 0.0 collective-permute-done.col_a
  11.8 1.9 %collective-permute-done.1.col_b = bf16[64,4,128]{2,1,0:T(4,128)(2,1)S(1)} collective-permute-done((bf16[64,4,128]{2,1,0:T(4,128)(2,1)S(1)}, bf16[64,4,128]{2,1,0:T(4,128)(2,1)S(1)}, u32[]{:S(2)}, u32[]{:S(2)}) %collective-permute-start.1) | collective-permute-done | bytes 65568 | tf_op jit(solution)/shard_map/ppermute | solution.py:472
  13.7 0.9 %rows.1 = (bf16[6,64,128]{2,1,0:T(8,128)(2,1)S(1)}, bf16[6,64,128]{2,1,0:T(8,128)(2,1)S(1)}) custom-call(bf16[32,56,128]{2,1,0:T(8,128)(2,1)} %x_first.3, bf16[32,56,128]{2,1,0:T(8,128)(2,1)} %x_first.3, bf16[32,56,128]{2,1,0:T(8,128)(2,1)} %c_first.3, bf16[32,56,128]{2,1,0:T(8,128)(2,1)} %c_first.3, bf16[64,4,128]{2,1,0:T(4,128)(2,1)S(1)} %collective-permute-done.col_a, ...), custom_call_target="tpu_custom_call" | custom-call | tf_op jit(solution)/shard_map/rows/pallas_call | solution.py:477
  14.6 1.9 %collective-permute-start.2 = (bf16[6,64,128]{2,1,0:T(8,128)(2,1)S(1)}, bf16[6,64,128]{2,1,0:T(8,128)(2,1)S(1)}, u32[]{:S(2)}, u32[]{:S(2)}) collective-permute-start(bf16[6,64,128]{2,1,0:T(8,128)(2,1)S(1)} %get-tuple-element.37), channel_id=1, source_target_pairs={{0,32},{64,96},{128,160},{192,224},{256,288},{320,352},{384,416},{... | collective-permute-start | bytes 294920 | tf_op jit(solution)/shard_map/ppermute | solution.py:488
  16.6 0.7 collective-permute-start.3
  17.2 0.0 copy-done.2
  17.3 0.0 copy-done.3
  17.3 0.0 copy-done.4
  17.3 0.3 weights.1
  17.6 0.0 copy-done
  17.6 0.0 copy-done.1
  17.6 1.9 %early.1 = (bf16[32,32,512]{2,1,0:T(8,128)(2,1)S(1)}, bf16[16,32,512]{2,1,0:T(8,128)(2,1)S(1)}, bf16[30,32,384]{2,1,0:T(8,128)(2,1)S(1)}, f32[30,32,256]{2,1,0:T...) custom-call(bf16[32,56,128]{2,1,0:T(8,128)(2,1)S(1)} %copy-done, ...), custom_call_target="tpu_custom_call" | custom-call | tf_op jit(solution)/shard_map/early/pallas_call | solution.py:362
  19.6 3.3 %collective-permute-done.2.row_a = bf16[6,64,128]{2,1,0:T(8,128)(2,1)S(1)} collective-permute-done((bf16[6,64,128]{2,1,0:T(8,128)(2,1)S(1)}, bf16[6,64,128]{2,1,0:T(8,128)(2,1)S(1)}, u32[]{:S(2)}, u32[]{:S(2)}) %collective-permute-start.2) | collective-permute-done | bytes 98336 | tf_op jit(solution)/shard_map/ppermute | solution.py:488
  22.9 0.0 collective-permute-done.3.row_b
  22.9 3.3 %level.1 = (bf16[4,640,128]{2,1,0:T(8,128)(2,1)S(1)}, bf16[4,640,128]{2,1,0:T(8,128)(2,1)S(1)}, bf16[8,32,384]{2,1,0:T(8,128)(2,1)S(1)}, bf16[2,32,256]{2,1,0:T(8,128)(2,1)S(1)}, bf16[34,32,512]{2,1,0:T(8,128)(2,1)S(1)}) custom-call(bf16[6,64,128]{2,1,0:T(8,128)(2,1)S(1)} %collective-permute-done.2.row_a, ...), custom_call_target="tpu_custom_call" | custom-call | tf_op jit(solution)/shard_map/level/pallas_call | solution.py:381
  26.1 1.9 %collective-permute-start.4 = (bf16[4,640,128]{2,1,0:T(8,128)(2,1)S(1)}, bf16[4,640,128]{2,1,0:T(8,128)(2,1)S(1)}, u32[]{:S(2)}, u32[]{:S(2)}) collective-permute-start(bf16[4,640,128]{2,1,0:T(8,128)(2,1)S(1)} %get-tuple-element.51), channel_id=1, source_target_pairs={{0,1},{1,0},{2,3},{3,2},{4,5},{5,4},{6,7},{7,6},{8,9},{9,8},{10,11... | collective-permute-start | bytes 1966088 | tf_op jit(solution)/shard_map/ppermute | solution.py:552
  28.1 2.1 %collective-permute-done.4 = bf16[4,640,128]{2,1,0:T(8,128)(2,1)S(1)} collective-permute-done((bf16[4,640,128]{2,1,0:T(8,128)(2,1)S(1)}, bf16[4,640,128]{2,1,0:T(8,128)(2,1)S(1)}, u32[]{:S(2)}, u32[]{:S(2)}) %collective-permute-start.4) | collective-permute-done | bytes 655392 | tf_op jit(solution)/shard_map/ppermute | solution.py:552
  30.1 0.2 add_convert_fusion
  30.3 20.8 %all_to_all.10.received = bf16[4,640,128]{2,1,0:T(8,128)(2,1)S(1)} all-to-all(bf16[4,640,128]{2,1,0:T(8,128)(2,1)S(1)} %add_convert_fusion), channel_id=1, replica_groups={{0,128,256,384},{1,129,257,385},{2,130,258,386},{3,131,259,387},{4,132,..., dimensions={0} | all-to-all | bytes 1310720 | tf_op jit(solution)/shard_map/all_to_all | solution.py:554
  51.1 0.8 %spread.1 = bf16[640,128]{1,0:T(8,128)(2,1)} custom-call(bf16[4,640,128]{2,1,0:T(8,128)(2,1)S(1)} %all_to_all.10.received), custom_call_target="tpu_custom_call" | custom-call | tf_op jit(solution)/shard_map/spread/pallas_call | solution.py:555
  51.9 14.3 %all-to-all-start.1 = ((bf16[64,5,2,128]{3,2,1,0:T(2,128)(2,1)}), bf16[64,5,2,128]{3,2,1,0:T(2,128)(2,1)S(1)}, u32[]{:S(2)}, u32[]{:S(2)}) async-start(bf16[64,5,2,128]{3,2,1,0:T(2,128)(2,1)} %bitcast.1), calls=%async_computation.1 | async-start | bytes 327680 | tf_op jit(solution)/shard_map/all_to_all | solution.py:565
  66.3 1.9 %late.1 = (bf16[32,56,128]{2,1,0:T(8,128)(2,1)}, bf16[32,56,128]{2,1,0:T(8,128)(2,1)}) custom-call(bf16[30,32,384]{2,1,0:T(8,128)(2,1)S(1)} %get-tuple-element.36.f3_in, bf16[8,32,384]{2,1,0:T(8,128)(2,1)S(1)} %get-tuple-element.47.f3_rim, bf16[14,32,256]{2,1,0:T(8,128)(2,1)S(1)} %get-tuple-element.43.coarse_in, ...), custom_call_target="tpu_custom_call" | custom-call | tf_op jit(solution)/shard_map/late/pallas_call | solution.py:409
  68.2 9.4 %all-to-all-done.1 = bf16[64,5,2,128]{3,2,1,0:T(2,128)(2,1)S(1)} async-done(((bf16[64,5,2,128]{3,2,1,0:T(2,128)(2,1)}), bf16[64,5,2,128]{3,2,1,0:T(2,128)(2,1)S(1)}, u32[]{:S(2)}, u32[]{:S(2)}) %all-to-all-start.1) | async-done | bytes 163872 | tf_op jit(solution)/shard_map/all_to_all | solution.py:565
  77.7 0.7 finish.1
Async XLA Ops:
  1.7 15.6 %copy-start.2 = (bf16[3,3,128,256]{3,2,1,0:T(8,128)(2,1)S(1)}, bf16[3,3,128,256]{3,2,1,0:T(8,128)(2,1)}, u32[]{:S(2)}) copy-start(bf16[3,3,128,256]{3,2,1,0:T(8,128)(2,1)} %wd.1) | copy-start | bytes 1769476
  1.7 15.6 %copy-start.3 = (bf16[3,3,128,128]{3,2,1,0:T(8,128)(2,1)S(1)}, bf16[3,3,128,128]{3,2,1,0:T(8,128)(2,1)}, u32[]{:S(2)}) copy-start(bf16[3,3,128,128]{3,2,1,0:T(8,128)(2,1)} %wc.1) | copy-start | bytes 884740
  1.7 15.6 %copy-start.4 = (bf16[2,2,256,128]{3,2,1,0:T(8,128)(2,1)S(1)}, bf16[2,2,256,128]{3,2,1,0:T(8,128)(2,1)}, u32[]{:S(2)}) copy-start(bf16[2,2,256,128]{3,2,1,0:T(8,128)(2,1)} %wu.1) | copy-start | bytes 786436
  1.7 10.1 %collective-permute-start = (bf16[64,4,128]{2,1,0:T(4,128)(2,1)S(1)}, bf16[64,4,128]{2,1,0:T(4,128)(2,1)S(1)}, u32[]{:S(2)}, u32[]{:S(2)}) collective-permute-start(bf16[64,4,128]{2,1,0:T(4,128)(2,1)S(1)} %get-tuple-element.32), channel_id=1, source_target_pairs={{0,1},{2,3},{4,5},{6,7},{8,9},{10,11},{12,13},{14,15},{16,17},{18,... | collective-permute-start | bytes 196616 | tf_op jit(solution)/shard_map/ppermute | solution.py:472
  3.8 13.8 %copy-start = (bf16[32,56,128]{2,1,0:T(8,128)(2,1)S(1)}, bf16[32,56,128]{2,1,0:T(8,128)(2,1)}, u32[]{:S(2)}) copy-start(bf16[32,56,128]{2,1,0:T(8,128)(2,1)} %x_first.3) | copy-start | bytes 1376260
  3.8 13.8 %copy-start.1 = (bf16[32,56,128]{2,1,0:T(8,128)(2,1)S(1)}, bf16[32,56,128]{2,1,0:T(8,128)(2,1)}, u32[]{:S(2)}) copy-start(bf16[32,56,128]{2,1,0:T(8,128)(2,1)} %c_first.3) | copy-start | bytes 1376260
  3.8 9.9 %collective-permute-start.1 = (bf16[64,4,128]{2,1,0:T(4,128)(2,1)S(1)}, bf16[64,4,128]{2,1,0:T(4,128)(2,1)S(1)}, u32[]{:S(2)}, u32[]{:S(2)}) collective-permute-start(bf16[64,4,128]{2,1,0:T(4,128)(2,1)S(1)} %get-tuple-element.33), channel_id=1, source_target_pairs={{1,2},{3,4},{5,6},{7,8},{9,10},{11,12},{13,14},{15,16},{17,18},{19... | collective-permute-start | bytes 196616 | tf_op jit(solution)/shard_map/ppermute | solution.py:472
  14.6 8.2 %collective-permute-start.2 = (bf16[6,64,128]{2,1,0:T(8,128)(2,1)S(1)}, bf16[6,64,128]{2,1,0:T(8,128)(2,1)S(1)}, u32[]{:S(2)}, u32[]{:S(2)}) collective-permute-start(bf16[6,64,128]{2,1,0:T(8,128)(2,1)S(1)} %get-tuple-element.37), channel_id=1, source_target_pairs={{0,32},{64,96},{128,160},{192,224},{256,288},{320,352},{384,416},{... | collective-permute-start | bytes 294920 | tf_op jit(solution)/shard_map/ppermute | solution.py:488
  16.6 6.3 %collective-permute-start.3 = (bf16[6,64,128]{2,1,0:T(8,128)(2,1)S(1)}, bf16[6,64,128]{2,1,0:T(8,128)(2,1)S(1)}, u32[]{:S(2)}, u32[]{:S(2)}) collective-permute-start(bf16[6,64,128]{2,1,0:T(8,128)(2,1)S(1)} %get-tuple-element.38), channel_id=1, source_target_pairs={{32,64},{96,128},{160,192},{224,256},{288,320},{352,384},{416,448}... | collective-permute-start | bytes 294920 | tf_op jit(solution)/shard_map/ppermute | solution.py:488
  26.1 4.0 %collective-permute-start.4 = (bf16[4,640,128]{2,1,0:T(8,128)(2,1)S(1)}, bf16[4,640,128]{2,1,0:T(8,128)(2,1)S(1)}, u32[]{:S(2)}, u32[]{:S(2)}) collective-permute-start(bf16[4,640,128]{2,1,0:T(8,128)(2,1)S(1)} %get-tuple-element.51), channel_id=1, source_target_pairs={{0,1},{1,0},{2,3},{3,2},{4,5},{5,4},{6,7},{7,6},{8,9},{9,8},{10,11... | collective-permute-start | bytes 1966088 | tf_op jit(solution)/shard_map/ppermute | solution.py:552
  51.9 25.7 %all-to-all-start.1 = ((bf16[64,5,2,128]{3,2,1,0:T(2,128)(2,1)}), bf16[64,5,2,128]{3,2,1,0:T(2,128)(2,1)S(1)}, u32[]{:S(2)}, u32[]{:S(2)}) async-start(bf16[64,5,2,128]{3,2,1,0:T(2,128)(2,1)} %bitcast.1), calls=%async_computation.1 | async-start | bytes 327680 | tf_op jit(solution)/shard_map/all_to_all | solution.py:565

commit v6 on v5

--- a/solution.py
+++ b/solution.py
@@ -201,10 +201,49 @@
     gs[first : first + count, :, 256:512] = ahead.astype(BF).reshape(count, 32, 256)
 
 
+def grad_rows(gs, c4, slope, ais, odd, w_even, w_odd, in_grid):
+    nexts = [ai + 1 for ai in ais]
+    below = rows_at(gs, nexts)
+    if odd:
+        spread = mm(jnp.concatenate([rows_at(gs, ais), below], axis=1), w_odd[...], NT)
+        cot = rows_at(c4, ais)[:, 256:512]
+    else:
+        spread = mm(below, w_even[...], NT)
+        cot = rows_at(c4, nexts)[:, 0:256]
+    slopes = rows_at(slope, [2 * ai + (2 if odd else 3) for ai in ais])
+    return per_row((cot.astype(F32) + spread) * slopes, in_grid)
+
+
+def store_grad(grad, own, g4, pre_own, places, own_places):
+    behind = pltpu.roll(grad[:, 128:256], 1, 0).astype(BF)
+    ahead = pltpu.roll(grad[:, 0:128], grad.shape[0] - 1, 0).astype(BF)
+    rounded = grad.astype(BF)
+    kept = per_row(grad, own).astype(BF)
+    for i, (place, own_place) in enumerate(zip(places, own_places)):
+        rows = slice(i * 32, i * 32 + 32)
+        g4[place, :, 0:128] = behind[rows]
+        g4[place, :, 128:384] = rounded[rows]
+        g4[place, :, 384:512] = ahead[rows]
+        if own_place is not None:
+            pre_own[own_place] = kept[rows]
+
+
+def conv_taps(pre, x4, rows, p):
+    res = mm(pre, rows_at(x4, [i + p + 3 for i in rows]), TN)
+    return [
+        res[0:128, q * 128 : (q + 1) * 128] + res[128:256, (q + 1) * 128 : (q + 2) * 128]
+        for q in range(3)
+    ]
+
+
+def g4_parts(inner, rim):
+    return ((0, 3, rim, 0), (3, 27, inner, 0), (30, 4, rim, 3))
+
+
 def early_kernel(
-    x, c, col_a, col_b, w_fwd, w_down, w_up,
-    x4, c4, f3, slope, gs, coarse_own, g_own,
-    xs, cs,
+    x, c, col_b, col_a, w_fwd, w_down, w_up, w_even, w_odd,
+    x4, c4, f3, slope, gs, g4, coarse_own, conv_part, up_part, down_part,
+    xs, cs, g_own, pre_own,
 ):
     left, right = swapped(lax.axis_index("col") % 2 == 1, col_b, col_a)
     for ref, own_block, first in ((xs, x, 0), (cs, c, 32)):
@@ -227,13 +266,29 @@
         store_coarse(grad, gs, first - 2, 7)
         coarse_own[first - 2 : first + 5] = per_row(coarse, own).astype(BF).reshape(7, 32, 256)
         g_own[first - 2 : first + 5] = per_row(grad, own).astype(BF).reshape(7, 32, 256)
+    x4_all, c4_all, f3_all = x4_parts(x4, None), c4_parts(c4, None), f3_parts(f3, None)
+    gs_all, slope_all = gs_parts(gs, None), f3_parts(slope, None)
+    coarse_flat = coarse_own[...].reshape(448, 256)
+    up_part[...] = mm(coarse_flat, rows_at(c4_all, range(2, 16)), TN)
+    g_flat = g_own[...].reshape(448, 256)
+    for p in range(3):
+        window = rows_at(f3_all, [2 * a + p + 2 for a in range(1, 15)])
+        down_part[p * 384 : (p + 1) * 384, :] = mm(window, g_flat, TN)
+    for odd, ais in ((True, range(2, 9)), (True, range(9, 15)), (False, range(1, 8)), (False, range(8, 15))):
+        grad = grad_rows(gs_all, c4_all, slope_all, ais, odd, w_even, w_odd, in_grid)
+        at = [2 * ai - 3 + (0 if odd else 1) for ai in ais]
+        store_grad(grad, own, g4, pre_own, at, at)
+    flat = pre_own[...].reshape(864, 256)
+    for p in range(3):
+        for q, tap in enumerate(conv_taps(flat, x4_all, range(2, 29), p)):
+            conv_part[:, (3 * p + q) * 128 : (3 * p + q + 1) * 128] = tap
 
 
 def level_kernel(
-    row_a, row_b, x4_in, c4_in, f3_in, slope_in, gs_in, coarse_in, g_in,
+    row_b, row_a, x4_in, c4_in, f3_in, slope_in, gs_in, conv_part, up_part, down_part,
     w_fwd, w_down, w_up, w_even, w_odd,
-    keep, send, f3_rim, coarse_rim, g4,
-    conv_acc, down_acc, up_acc, xs, cs, x4_rim, c4_rim, slope_rim, gs_rim, g_rim, pre_own,
+    keep, send, f3_rim, coarse_rim, g4_rim,
+    conv_acc, down_acc, up_acc, xs, cs, x4_rim, c4_rim, slope_rim, gs_rim, g_rim, pre_rim,
 ):
     top, bot = swapped(lax.axis_index("row") % 2 == 1, row_b, row_a)
     for ref, at, value in (
@@ -264,55 +319,28 @@
     coarse_rim[...] = per_row(coarse[32:96], own).astype(BF).reshape(2, 32, 256)
     g_rim[...] = per_row(grad[32:96], own).astype(BF).reshape(2, 32, 256)
 
-    coarse_flat = rows_at(own_parts(coarse_in, coarse_rim), range(16))
-    res = mm(coarse_flat, rows_at(c4, range(1, 17)), TN)
+    res = up_part[...] + mm(coarse_rim[...].reshape(64, 256), rows_at(c4, (1, 16)), TN)
     for k in range(4):
         up_acc[k * 256 : (k + 1) * 256, :] = res[:, k * 128 : (k + 1) * 128]
-    g_flat = rows_at(own_parts(g_in, g_rim), range(16))
+    g_flat = g_rim[...].reshape(64, 256)
     for p in range(3):
-        res = mm(rows_at(f3, [2 * a + p + 2 for a in range(16)]), g_flat, TN)
+        at = slice(p * 384, (p + 1) * 384)
+        res = down_part[at, :] + mm(rows_at(f3, (p + 2, p + 32)), g_flat, TN)
         for side in range(2):
-            down_acc[side, p * 384 : (p + 1) * 384, :] = res[:, side * 128 : (side + 1) * 128]
-
-    for first, count in ((0, 9), (9, 8)):
-        ais = range(first, first + count)
-        nexts = range(first + 1, first + 1 + count)
-        for odd in (True, False):
-            below = rows_at(gs, nexts)
-            if odd:
-                spread = mm(jnp.concatenate([rows_at(gs, ais), below], axis=1), w_odd[...], NT)
-                cot = rows_at(c4, ais)[:, 256:512]
-                at = 2
-            else:
-                spread = mm(below, w_even[...], NT)
-                cot = rows_at(c4, nexts)[:, 0:256]
-                at = 3
-            slopes = rows_at(slope, [2 * ai + at for ai in ais])
-            grad = per_row((cot.astype(F32) + spread) * slopes, in_grid)
-            if first == 0 and odd:
-                grad = jnp.concatenate([grad[0:32] * keep_top, grad[32:]], axis=0)
-            if first != 0 and not odd:
-                edge = (count - 1) * 32
-                grad = jnp.concatenate([grad[:edge], grad[edge:] * keep_bot], axis=0)
-            behind = pltpu.roll(grad[:, 128:256], 1, 0).astype(BF)
-            ahead = pltpu.roll(grad[:, 0:128], count * 32 - 1, 0).astype(BF)
-            rounded = grad.astype(BF)
-            kept = per_row(grad, own).astype(BF)
-            for ai in ais:
-                g_row = 2 * ai + (0 if odd else 1)
-                rows = slice((ai - first) * 32, (ai - first + 1) * 32)
-                g4[g_row, :, 0:128] = behind[rows]
-                g4[g_row, :, 128:384] = rounded[rows]
-                g4[g_row, :, 384:512] = ahead[rows]
-                if 1 <= g_row <= 32:
-                    pre_own[g_row - 1] = kept[rows]
-
-    flat = pre_own[...].reshape(1024, 256)
+            down_acc[side, at, :] = res[:, side * 128 : (side + 1) * 128]
+
+    grad = grad_rows(gs, c4, slope, (0, 1, 15, 16), True, w_even, w_odd, in_grid)
+    grad = jnp.concatenate([grad[0:32] * keep_top, grad[32:]], axis=0)
+    store_grad(grad, own, g4_rim, pre_rim, (0, 2, 3, 5), (None, 1, 2, 4))
+    grad = grad_rows(gs, c4, slope, (0, 15, 16), False, w_even, w_odd, in_grid)
+    grad = jnp.concatenate([grad[0:64], grad[64:] * keep_bot], axis=0)
+    store_grad(grad, own, g4_rim, pre_rim, (1, 4, 6), (0, 3, None))
+
+    flat = pre_rim[...].reshape(160, 256)
     for p in range(3):
-        res = mm(flat, rows_at(x4, range(p + 3, p + 35)), TN)
-        for q in range(3):
-            tap = res[0:128, q * 128 : (q + 1) * 128] + res[128:256, (q + 1) * 128 : (q + 2) * 128]
-            conv_acc[(3 * p + q) * 128 : (3 * p + q + 1) * 128, :] = tap.T
+        for q, tap in enumerate(conv_taps(flat, x4, (0, 1, 29, 30, 31), p)):
+            at = slice((3 * p + q) * 128, (3 * p + q + 1) * 128)
+            conv_acc[at, :] = (conv_part[:, at] + tap).T
 
     odd_col = lax.axis_index("col") % 2 == 1
 
@@ -327,7 +355,10 @@
         pack(0, send, conv_acc, down_acc, up_acc)
 
 
-def late_kernel(f3_in, f3_rim, coarse_in, coarse_rim, g4, w_up, w_bwd, out, gx, mix):
+def late_kernel(
+    f3_in, f3_rim, coarse_in, coarse_rim, g4_in, g4_rim, w_up, w_bwd, out, gx, mix
+):
+    g4 = g4_parts(g4_in, g4_rim)
     f3 = f3_parts(f3_in, f3_rim)
     coarse = own_parts(coarse_in, coarse_rim)
     for first in (0, 8):
@@ -344,7 +375,7 @@
     for first in (0, 8, 16, 24):
         total = None
         for p in range(3):
-            window = g4[first + 2 - p : first + 10 - p].reshape(256, 512)
+            window = rows_at(g4, range(first + 2 - p, first + 10 - p))
             term = mm(window, w_bwd[p], NT)
             total = term if total is None else total + term
         for i in range(first, first + 8):
@@ -355,7 +386,7 @@
     gx[...] = mix[:, 8:64, :].astype(BF)
 
 
-LARGE = pltpu.CompilerParams(vmem_limit_bytes=14 * 1024 * 1024)
+LARGE = pltpu.CompilerParams(vmem_limit_bytes=16 * 1024 * 1024)
 
 
 def early(x, c, cols, weights, w_down):
@@ -367,13 +398,17 @@
             held((30, 32, 384)),
             held((30, 32, 256), F32),
             held((14, 32, 512)),
+            held((27, 32, 512)),
             held((14, 32, 256)),
-            held((14, 32, 256)),
+            held((128, 1152), F32),
+            held((256, 512), F32),
+            held((1152, 256), F32),
         ),
-        scratch_shapes=[pltpu.VMEM((32, 72, 128), F32)] * 2,
+        scratch_shapes=[pltpu.VMEM((32, 72, 128), F32)] * 2
+        + [pltpu.VMEM((14, 32, 256), BF), pltpu.VMEM((27, 32, 256), BF)],
         compiler_params=LARGE,
         name="early",
-    )(x, c, *pin(*cols, weights[0]), w_down, *pin(weights[2]))
+    )(x, c, *pin(*cols, weights[0]), w_down, *pin(*weights[2:]))
 
 
 def level(rows, inner, weights, w_down):
@@ -385,7 +420,7 @@
             held((4, 640, 128)),
             held((8, 32, 384)),
             held((2, 32, 256)),
-            held((34, 32, 512)),
+            held((7, 32, 512)),
         ),
         scratch_shapes=[
             pltpu.VMEM((1160, 128), F32),
@@ -398,11 +433,11 @@
             pltpu.VMEM((8, 32, 256), F32),
             pltpu.VMEM((4, 32, 512), BF),
             pltpu.VMEM((2, 32, 256), BF),
-            pltpu.VMEM((32, 32, 256), BF),
+            pltpu.VMEM((5, 32, 256), BF),
         ],
         compiler_params=LARGE,
         name="level",
-    )(*pin(*rows, *inner, w_fwd), w_down, *pin(w_up, w_even, w_odd))
+    )(*pin(*rows, *inner[:5], *inner[7:], w_fwd), w_down, *pin(w_up, w_even, w_odd))
 
 
 def late(*args):
@@ -424,18 +459,23 @@
     return both
 
 
+def swap(longer, shorter, axis):
+    even, odd = pairs(axis)
+    return lax.ppermute(longer, axis, odd), lax.ppermute(shorter, axis, even)
+
+
 def store_pair(odd, forward, backward, even_first, odd_first):
     even_first[...] = jnp.where(odd, backward, forward).astype(BF)
     odd_first[...] = jnp.where(odd, forward, backward).astype(BF)
 
 
-def cols_kernel(x_last, x_first, c_last, c_first, col_a, col_b):
+def cols_kernel(x_last, x_first, c_last, c_first, col_b, col_a):
     rightward = jnp.concatenate([x_last[:, 4:8], c_last[:, 4:8]], axis=0).astype(F32)
     leftward = jnp.concatenate([x_first[:, 0:4], c_first[:, 0:4]], axis=0).astype(F32)
     store_pair(lax.axis_index("col") % 2 == 1, rightward, leftward, col_a, col_b)
 
 
-def rows_kernel(x_last, x_first, c_last, c_first, col_a, col_b, row_a, row_b):
+def rows_kernel(x_last, x_first, c_last, c_first, col_b, col_a, row_b, row_a):
     left, right = swapped(lax.axis_index("col") % 2 == 1, col_b, col_a)
 
     def side(x, c, x_rows, c_rows):
@@ -468,8 +508,7 @@
         compiler_params=SMALL,
         name="cols",
     )(*far(x, x, c, c))
-    even, odd = pairs("col")
-    return lax.ppermute(first, "col", even), lax.ppermute(second, "col", odd)
+    return swap(first, second, "col")
 
 
 def row_halo(x, c, cols):
@@ -484,8 +523,7 @@
         compiler_params=SMALL,
         name="rows",
     )(*far(x, x, c, c), *pin(*cols))
-    even, odd = pairs("row")
-    return lax.ppermute(first, "row", even), lax.ppermute(second, "row", odd)
+    return swap(first, second, "row")
 
 
 def local_terms(inputs, cotangent, w_conv, w_down, w_up):
@@ -494,8 +532,9 @@
     cols = column_halo(inputs, cotangent)
     rows = row_halo(inputs, cotangent, cols)
     inner = early(inputs, cotangent, cols, weights, flat_down)
-    keep, send, f3_rim, coarse_rim, g4 = level(rows, inner, weights, flat_down)
-    return keep, send, (inner[2], f3_rim, inner[5], coarse_rim, g4, weights[2], weights[1])
+    keep, send, f3_rim, coarse_rim, g4_rim = level(rows, inner, weights, flat_down)
+    held_back = (inner[2], f3_rim, inner[6], coarse_rim, inner[5], g4_rim, weights[2], weights[1])
+    return keep, send, held_back
 
 
 def spread_kernel(received, out, total, stage):
@@ -559,8 +598,8 @@
         compiler_params=SMALL,
         name="spread",
     )(*pin(got))
-    g4, _ = lax.optimization_barrier((rest[4], spread))
-    rest = (*rest[:4], g4, *rest[5:])
+    rim, _ = lax.optimization_barrier((rest[5], spread))
+    rest = (*rest[:5], rim, *rest[6:])
     spread = spread.reshape(64, 5, 2, 128)
     got = lax.all_to_all(spread, mesh, 0, 0, axis_index_groups=plane, tiled=True)
     got = got.reshape(640, 128)

time: 78.8 us -> 73.9 us (0.938)
  waiting for transfers between devices: 16.7 us -> 12.4 us
  blocking collectives: 20.8 us -> 18.2 us
  Pallas kernels: 10.9 us -> 12 us
  starting transfers between devices: 28.9 us -> 29.9 us
    ppermute x4, starting transfers between devices: 12.6 us -> 19.2 us  [swap(): return (lax.ppermute(longer, axis, odd), lax.ppermute(shorter, axis, even))]
    all_to_all x1, starting transfers between devices: 14.3 us -> 8.81 us  [reduce_owners(): lax.all_to_all(spread, mesh, 0, 0, axis_index_groups=plane, tiled=True)]
    ppermute x4, waiting for transfers between devices: 5.23 us -> 0.88 us  [swap(): return (lax.ppermute(longer, axis, odd), lax.ppermute(shorter, axis, even))]
    all_to_all x1, blocking collectives: 20.8 us -> 18.2 us  [reduce_owners(): got = lax.all_to_all(pair, mesh, 0, 0, axis_index_groups=across, tiled=True)]
    pallas_call x1, Pallas kernels: 1.94 us -> 3.93 us  [early(): pl.pallas_call(early_kernel, out_shape=(held((32, 32, 512)), held((16, 32...]
    pallas_call x1, Pallas kernels: 3.27 us -> 2.34 us  [level(): pl.pallas_call(level_kernel, out_shape=(held((4, 640, 128)), held((4, 640...]
  transfers between devices with their start and end apart: 6 -> 6, of which waited for: 4 -> 3; matrix products, arithmetic and copies ran while one was open for 0% -> 0% of each run, Pallas kernels for 5% -> 8%
where the time goes in v6:
time: 73.9 us; the launch traced here: 73.4 us
  starting transfers between devices  29.9 us (40%)
  blocking collectives  18.2 us (25%)
  waiting for transfers between devices  12.4 us (17%)
  Pallas kernels  12 us (16%)
  between operations  0.82 us (1%)
    ppermute x4, starting transfers between devices, swap(): return (lax.ppermute(longer, axis, odd), lax.ppermute(shorter, axis, even))  19.2 us
    all_to_all x1, blocking collectives, reduce_owners(): got = lax.all_to_all(pair, mesh, 0, 0, axis_index_groups=across, tiled=True)  18.2 us
    all_to_all x1, waiting for transfers between devices, reduce_owners(): lax.all_to_all(spread, mesh, 0, 0, axis_index_groups=plane, tiled=True)  9.42 us
    all_to_all x1, starting transfers between devices, reduce_owners(): lax.all_to_all(spread, mesh, 0, 0, axis_index_groups=plane, tiled=True)  8.81 us
    pallas_call x1, Pallas kernels, early(): pl.pallas_call(early_kernel, out_shape=(held((32, 32, 512)), held((16, 32...  3.93 us
    pallas_call x1, Pallas kernels, level(): pl.pallas_call(level_kernel, out_shape=(held((4, 640, 128)), held((4, 640...  2.34 us
    ppermute x1, waiting for transfers between devices, reduce_owners(): other = lax.ppermute(send, 'col', [(i, i ^ 1) for i in range(32)])  2.06 us
    pallas_call x1, Pallas kernels, late(): pl.pallas_call(late_kernel, out_shape=(jax.ShapeDtypeStruct((32, 56, 128)...  1.97 us
  transfers between devices with their start and end apart: 6, of which 3 were waited for; matrix products, arithmetic and copies ran while one was open for 0% of the time, Pallas kernels for 8%

profile of v6, /device:TPU:8, one launch (start us, length us, event | category | flops | bytes accessed | tf_op | source)
XLA Modules:
  0.0 73.4 jit_solution(912451448821438067)
XLA Ops:
  0.6 1.1 %cols.1 = (bf16[64,4,128]{2,1,0:T(4,128)(2,1)S(1)}, bf16[64,4,128]{2,1,0:T(4,128)(2,1)S(1)}) custom-call(bf16[32,56,128]{2,1,0:T(8,128)(2,1)} %x_first.3, bf16[32,56,128]{2,1,0:T(8,128)(2,1)} %x_first.3, bf16[32,56,128]{2,1,0:T(8,128)(2,1)} %c_first.3, bf16[32,56,128]{2,1,0:T(8,128)(2,1)} %c_first.3), custom_call_target="tpu_custom_call" | custom-call | tf_op jit(solution)/shard_map/cols/pallas_call | solution.py:502
  1.7 0.0 copy-start.2
  1.7 0.0 copy-start.3
  1.7 0.0 copy-start.4
  1.7 2.1 %collective-permute-start = (bf16[64,4,128]{2,1,0:T(4,128)(2,1)S(1)}, bf16[64,4,128]{2,1,0:T(4,128)(2,1)S(1)}, u32[]{:S(2)}, u32[]{:S(2)}) collective-permute-start(bf16[64,4,128]{2,1,0:T(4,128)(2,1)S(1)} %get-tuple-element.35), channel_id=1, source_target_pairs={{1,2},{3,4},{5,6},{7,8},{9,10},{11,12},{13,14},{15,16},{17,18},{19... | collective-permute-start | bytes 196616 | tf_op jit(solution)/shard_map/ppermute | solution.py:464
  3.8 0.0 copy-start
  3.8 0.0 copy-start.1
  3.8 3.7 %collective-permute-start.1 = (bf16[64,4,128]{2,1,0:T(4,128)(2,1)S(1)}, bf16[64,4,128]{2,1,0:T(4,128)(2,1)S(1)}, u32[]{:S(2)}, u32[]{:S(2)}) collective-permute-start(bf16[64,4,128]{2,1,0:T(4,128)(2,1)S(1)} %get-tuple-element.36), channel_id=1, source_target_pairs={{0,1},{2,3},{4,5},{6,7},{8,9},{10,11},{12,13},{14,15},{16,17},{18,... | collective-permute-start | bytes 196616 | tf_op jit(solution)/shard_map/ppermute | solution.py:464
  7.5 0.0 collective-permute-done.col_b
  7.5 0.9 %collective-permute-done.1.col_a = bf16[64,4,128]{2,1,0:T(4,128)(2,1)S(1)} collective-permute-done((bf16[64,4,128]{2,1,0:T(4,128)(2,1)S(1)}, bf16[64,4,128]{2,1,0:T(4,128)(2,1)S(1)}, u32[]{:S(2)}, u32[]{:S(2)}) %collective-permute-start.1) | collective-permute-done | bytes 65568 | tf_op jit(solution)/shard_map/ppermute | solution.py:464
  8.4 0.9 %rows.1 = (bf16[6,64,128]{2,1,0:T(8,128)(2,1)S(1)}, bf16[6,64,128]{2,1,0:T(8,128)(2,1)S(1)}) custom-call(bf16[32,56,128]{2,1,0:T(8,128)(2,1)} %x_first.3, bf16[32,56,128]{2,1,0:T(8,128)(2,1)} %x_first.3, bf16[32,56,128]{2,1,0:T(8,128)(2,1)} %c_first.3, bf16[32,56,128]{2,1,0:T(8,128)(2,1)} %c_first.3, bf16[64,4,128]{2,1,0:T(4,128)(2,1)S(1)} %collective-permute-done.col_b, ...), custom_call_target="tpu_custom_call" | custom-call | tf_op jit(solution)/shard_map/rows/pallas_call | solution.py:516
  9.3 0.7 collective-permute-start.2
  10.0 12.7 %collective-permute-start.3 = (bf16[6,64,128]{2,1,0:T(8,128)(2,1)S(1)}, bf16[6,64,128]{2,1,0:T(8,128)(2,1)S(1)}, u32[]{:S(2)}, u32[]{:S(2)}) collective-permute-start(bf16[6,64,128]{2,1,0:T(8,128)(2,1)S(1)} %get-tuple-element.43), channel_id=1, source_target_pairs={{0,32},{64,96},{128,160},{192,224},{256,288},{320,352},{384,416},{... | collective-permute-start | bytes 294920 | tf_op jit(solution)/shard_map/ppermute | solution.py:464
  22.7 0.0 copy-done.2
  22.8 0.0 copy-done.3
  22.8 0.0 copy-done.4
  22.8 0.3 weights.1
  23.1 0.0 copy-done
  23.1 0.0 copy-done.1
  23.1 3.9 %early.1 = (bf16[32,32,512]{2,1,0:T(8,128)(2,1)S(1)}, bf16[16,32,512]{2,1,0:T(8,128)(2,1)S(1)}, bf16[30,32,384]{2,1,0:T(8,128)(2,1)S(1)}, f32[30,32,256]{2,1,0:T...) custom-call(bf16[32,56,128]{2,1,0:T(8,128)(2,1)S(1)} %copy-done, ...), custom_call_target="tpu_custom_call" | custom-call | tf_op jit(solution)/shard_map/early/pallas_call | solution.py:393
  27.0 0.0 collective-permute-done.2.row_b
  27.1 0.0 collective-permute-done.3.row_a
  27.1 2.3 %level.1 = (bf16[4,640,128]{2,1,0:T(8,128)(2,1)S(1)}, bf16[4,640,128]{2,1,0:T(8,128)(2,1)S(1)}, bf16[8,32,384]{2,1,0:T(8,128)(2,1)S(1)}, bf16[2,32,256]{2,1,0:T(8,128)(2,1)S(1)}, bf16[7,32,512]{2,1,0:T(8,128)(2,1)S(1)}) custom-call(bf16[6,64,128]{2,1,0:T(8,128)(2,1)S(1)} %collective-permute-done.2.row_b, ...), custom_call_target="tpu_custom_call" | custom-call | tf_op jit(solution)/shard_map/level/pallas_call | solution.py:416
  29.4 1.9 %collective-permute-start.4 = (bf16[4,640,128]{2,1,0:T(8,128)(2,1)S(1)}, bf16[4,640,128]{2,1,0:T(8,128)(2,1)S(1)}, u32[]{:S(2)}, u32[]{:S(2)}) collective-permute-start(bf16[4,640,128]{2,1,0:T(8,128)(2,1)S(1)} %get-tuple-element.57), channel_id=1, source_target_pairs={{0,1},{1,0},{2,3},{3,2},{4,5},{5,4},{6,7},{7,6},{8,9},{9,8},{10,11... | collective-permute-start | bytes 1966088 | tf_op jit(solution)/shard_map/ppermute | solution.py:591
  31.3 2.1 %collective-permute-done.4 = bf16[4,640,128]{2,1,0:T(8,128)(2,1)S(1)} collective-permute-done((bf16[4,640,128]{2,1,0:T(8,128)(2,1)S(1)}, bf16[4,640,128]{2,1,0:T(8,128)(2,1)S(1)}, u32[]{:S(2)}, u32[]{:S(2)}) %collective-permute-start.4) | collective-permute-done | bytes 655392 | tf_op jit(solution)/shard_map/ppermute | solution.py:591
  33.4 0.2 add_convert_fusion
  33.6 18.2 %all_to_all.10.received = bf16[4,640,128]{2,1,0:T(8,128)(2,1)S(1)} all-to-all(bf16[4,640,128]{2,1,0:T(8,128)(2,1)S(1)} %add_convert_fusion), channel_id=1, replica_groups={{0,128,256,384},{1,129,257,385},{2,130,258,386},{3,131,259,387},{4,132,..., dimensions={0} | all-to-all | bytes 1310720 | tf_op jit(solution)/shard_map/all_to_all | solution.py:593
  51.8 0.8 %spread.1 = bf16[640,128]{1,0:T(8,128)(2,1)} custom-call(bf16[4,640,128]{2,1,0:T(8,128)(2,1)S(1)} %all_to_all.10.received), custom_call_target="tpu_custom_call" | custom-call | tf_op jit(solution)/shard_map/spread/pallas_call | solution.py:594
  52.5 8.8 %all-to-all-start.1 = ((bf16[64,5,2,128]{3,2,1,0:T(2,128)(2,1)}), bf16[64,5,2,128]{3,2,1,0:T(2,128)(2,1)S(1)}, u32[]{:S(2)}, u32[]{:S(2)}) async-start(bf16[64,5,2,128]{3,2,1,0:T(2,128)(2,1)} %bitcast.1), calls=%async_computation.1 | async-start | bytes 327680 | tf_op jit(solution)/shard_map/all_to_all | solution.py:604
  61.4 2.0 %late.1 = (bf16[32,56,128]{2,1,0:T(8,128)(2,1)}, bf16[32,56,128]{2,1,0:T(8,128)(2,1)}) custom-call(bf16[30,32,384]{2,1,0:T(8,128)(2,1)S(1)} %get-tuple-element.41.f3_in, bf16[8,32,384]{2,1,0:T(8,128)(2,1)S(1)} %get-tuple-element.51.f3_rim, bf16[14,32,256]{2,1,0:T(8,128)(2,1)S(1)} %get-tuple-element.52.coarse_in, ...), custom_call_target="tpu_custom_call" | custom-call | tf_op jit(solution)/shard_map/late/pallas_call | solution.py:444
  63.3 9.4 %all-to-all-done.1 = bf16[64,5,2,128]{3,2,1,0:T(2,128)(2,1)S(1)} async-done(((bf16[64,5,2,128]{3,2,1,0:T(2,128)(2,1)}), bf16[64,5,2,128]{3,2,1,0:T(2,128)(2,1)S(1)}, u32[]{:S(2)}, u32[]{:S(2)}) %all-to-all-start.1) | async-done | bytes 163872 | tf_op jit(solution)/shard_map/all_to_all | solution.py:604
  72.8 0.7 finish.1
Async XLA Ops:
  1.7 21.1 %copy-start.2 = (bf16[3,3,128,256]{3,2,1,0:T(8,128)(2,1)S(1)}, bf16[3,3,128,256]{3,2,1,0:T(8,128)(2,1)}, u32[]{:S(2)}) copy-start(bf16[3,3,128,256]{3,2,1,0:T(8,128)(2,1)} %wd.1) | copy-start | bytes 1769476
  1.7 21.1 %copy-start.3 = (bf16[3,3,128,128]{3,2,1,0:T(8,128)(2,1)S(1)}, bf16[3,3,128,128]{3,2,1,0:T(8,128)(2,1)}, u32[]{:S(2)}) copy-start(bf16[3,3,128,128]{3,2,1,0:T(8,128)(2,1)} %wc.1) | copy-start | bytes 884740
  1.7 21.1 %copy-start.4 = (bf16[2,2,256,128]{3,2,1,0:T(8,128)(2,1)S(1)}, bf16[2,2,256,128]{3,2,1,0:T(8,128)(2,1)}, u32[]{:S(2)}) copy-start(bf16[2,2,256,128]{3,2,1,0:T(8,128)(2,1)} %wu.1) | copy-start | bytes 786436
  1.7 5.8 %collective-permute-start = (bf16[64,4,128]{2,1,0:T(4,128)(2,1)S(1)}, bf16[64,4,128]{2,1,0:T(4,128)(2,1)S(1)}, u32[]{:S(2)}, u32[]{:S(2)}) collective-permute-start(bf16[64,4,128]{2,1,0:T(4,128)(2,1)S(1)} %get-tuple-element.35), channel_id=1, source_target_pairs={{1,2},{3,4},{5,6},{7,8},{9,10},{11,12},{13,14},{15,16},{17,18},{19... | collective-permute-start | bytes 196616 | tf_op jit(solution)/shard_map/ppermute | solution.py:464
  3.8 19.3 %copy-start = (bf16[32,56,128]{2,1,0:T(8,128)(2,1)S(1)}, bf16[32,56,128]{2,1,0:T(8,128)(2,1)}, u32[]{:S(2)}) copy-start(bf16[32,56,128]{2,1,0:T(8,128)(2,1)} %x_first.3) | copy-start | bytes 1376260
  3.8 19.3 %copy-start.1 = (bf16[32,56,128]{2,1,0:T(8,128)(2,1)S(1)}, bf16[32,56,128]{2,1,0:T(8,128)(2,1)}, u32[]{:S(2)}) copy-start(bf16[32,56,128]{2,1,0:T(8,128)(2,1)} %c_first.3) | copy-start | bytes 1376260
  3.8 4.6 %collective-permute-start.1 = (bf16[64,4,128]{2,1,0:T(4,128)(2,1)S(1)}, bf16[64,4,128]{2,1,0:T(4,128)(2,1)S(1)}, u32[]{:S(2)}, u32[]{:S(2)}) collective-permute-start(bf16[64,4,128]{2,1,0:T(4,128)(2,1)S(1)} %get-tuple-element.36), channel_id=1, source_target_pairs={{0,1},{2,3},{4,5},{6,7},{8,9},{10,11},{12,13},{14,15},{16,17},{18,... | collective-permute-start | bytes 196616 | tf_op jit(solution)/shard_map/ppermute | solution.py:464
  9.3 17.7 %collective-permute-start.2 = (bf16[6,64,128]{2,1,0:T(8,128)(2,1)S(1)}, bf16[6,64,128]{2,1,0:T(8,128)(2,1)S(1)}, u32[]{:S(2)}, u32[]{:S(2)}) collective-permute-start(bf16[6,64,128]{2,1,0:T(8,128)(2,1)S(1)} %get-tuple-element.42), channel_id=1, source_target_pairs={{32,64},{96,128},{160,192},{224,256},{288,320},{352,384},{416,448}... | collective-permute-start | bytes 294920 | tf_op jit(solution)/shard_map/ppermute | solution.py:464
  10.0 17.0 %collective-permute-start.3 = (bf16[6,64,128]{2,1,0:T(8,128)(2,1)S(1)}, bf16[6,64,128]{2,1,0:T(8,128)(2,1)S(1)}, u32[]{:S(2)}, u32[]{:S(2)}) collective-permute-start(bf16[6,64,128]{2,1,0:T(8,128)(2,1)S(1)} %get-tuple-element.43), channel_id=1, source_target_pairs={{0,32},{64,96},{128,160},{192,224},{256,288},{320,352},{384,416},{... | collective-permute-start | bytes 294920 | tf_op jit(solution)/shard_map/ppermute | solution.py:464
  29.4 4.0 %collective-permute-start.4 = (bf16[4,640,128]{2,1,0:T(8,128)(2,1)S(1)}, bf16[4,640,128]{2,1,0:T(8,128)(2,1)S(1)}, u32[]{:S(2)}, u32[]{:S(2)}) collective-permute-start(bf16[4,640,128]{2,1,0:T(8,128)(2,1)S(1)} %get-tuple-element.57), channel_id=1, source_target_pairs={{0,1},{1,0},{2,3},{3,2},{4,5},{5,4},{6,7},{7,6},{8,9},{9,8},{10,11... | collective-permute-start | bytes 1966088 | tf_op jit(solution)/shard_map/ppermute | solution.py:591
  52.5 20.2 %all-to-all-start.1 = ((bf16[64,5,2,128]{3,2,1,0:T(2,128)(2,1)}), bf16[64,5,2,128]{3,2,1,0:T(2,128)(2,1)S(1)}, u32[]{:S(2)}, u32[]{:S(2)}) async-start(bf16[64,5,2,128]{3,2,1,0:T(2,128)(2,1)} %bitcast.1), calls=%async_computation.1 | async-start | bytes 327680 | tf_op jit(solution)/shard_map/all_to_all | solution.py:604

commit v7 on v6

--- a/solution.py
+++ b/solution.py
@@ -228,12 +228,20 @@
             pre_own[own_place] = kept[rows]
 
 
-def conv_taps(pre, x4, rows, p):
-    res = mm(pre, rows_at(x4, [i + p + 3 for i in rows]), TN)
-    return [
-        res[0:128, q * 128 : (q + 1) * 128] + res[128:256, (q + 1) * 128 : (q + 2) * 128]
-        for q in range(3)
-    ]
+def conv_taps(pre, x4, rows, p, flip):
+    window = rows_at(x4, [i + p + 3 for i in rows])
+    taps = []
+    if flip:
+        res = mm(window, pre, TN)
+        for q in range(3):
+            one, two = slice(q * 128, q * 128 + 128), slice(q * 128 + 128, q * 128 + 256)
+            taps.append(res[one, 0:128] + res[two, 128:256])
+    else:
+        res = mm(pre, window, TN)
+        for q in range(3):
+            one, two = slice(q * 128, q * 128 + 128), slice(q * 128 + 128, q * 128 + 256)
+            taps.append((res[0:128, one] + res[128:256, two]).T)
+    return taps
 
 
 def g4_parts(inner, rim):
@@ -280,8 +288,8 @@
         store_grad(grad, own, g4, pre_own, at, at)
     flat = pre_own[...].reshape(864, 256)
     for p in range(3):
-        for q, tap in enumerate(conv_taps(flat, x4_all, range(2, 29), p)):
-            conv_part[:, (3 * p + q) * 128 : (3 * p + q + 1) * 128] = tap
+        for q, tap in enumerate(conv_taps(flat, x4_all, range(2, 29), p, False)):
+            conv_part[(3 * p + q) * 128 : (3 * p + q + 1) * 128, :] = tap
 
 
 def level_kernel(
@@ -338,9 +346,9 @@
 
     flat = pre_rim[...].reshape(160, 256)
     for p in range(3):
-        for q, tap in enumerate(conv_taps(flat, x4, (0, 1, 29, 30, 31), p)):
+        for q, tap in enumerate(conv_taps(flat, x4, (0, 1, 29, 30, 31), p, True)):
             at = slice((3 * p + q) * 128, (3 * p + q + 1) * 128)
-            conv_acc[at, :] = (conv_part[:, at] + tap).T
+            conv_acc[at, :] = conv_part[at, :] + tap
 
     odd_col = lax.axis_index("col") % 2 == 1
 
@@ -400,7 +408,7 @@
             held((14, 32, 512)),
             held((27, 32, 512)),
             held((14, 32, 256)),
-            held((128, 1152), F32),
+            held((1152, 128), F32),
             held((256, 512), F32),
             held((1152, 256), F32),
         ),
@@ -522,7 +530,7 @@
         out_specs=(whole, whole),
         compiler_params=SMALL,
         name="rows",
-    )(*far(x, x, c, c), *pin(*cols))
+    )(x, x, c, c, *pin(*cols))
     return swap(first, second, "row")
 
 

time: 73.9 us -> 72.6 us (0.982)
  Pallas kernels: 12 us -> 11.2 us
    pallas_call x1, Pallas kernels: 0.92 us -> 0.07 us  [row_halo(): pl.pallas_call(rows_kernel, grid=(1,), out_shape=(jax.ShapeDtypeStruct((6...]
  transfers between devices with their start and end apart: 6 -> 6, of which waited for: 3 -> 4; matrix products, arithmetic and copies ran while one was open for 0% -> 0% of each run, Pallas kernels for 8% -> 9%
where the time goes in v7:
time: 72.6 us; the launch traced here: 72.3 us
  starting transfers between devices  29.6 us (41%)
  blocking collectives  18.1 us (25%)
  waiting for transfers between devices  12.4 us (17%)
  Pallas kernels  11.2 us (15%)
  between operations  0.8 us (1%)
    ppermute x4, starting transfers between devices, swap(): return (lax.ppermute(longer, axis, odd), lax.ppermute(shorter, axis, even))  19 us
    all_to_all x1, blocking collectives, reduce_owners(): got = lax.all_to_all(pair, mesh, 0, 0, axis_index_groups=across, tiled=True)  18.1 us
    all_to_all x1, waiting for transfers between devices, reduce_owners(): lax.all_to_all(spread, mesh, 0, 0, axis_index_groups=plane, tiled=True)  9.42 us
    all_to_all x1, starting transfers between devices, reduce_owners(): lax.all_to_all(spread, mesh, 0, 0, axis_index_groups=plane, tiled=True)  8.65 us
    pallas_call x1, Pallas kernels, early(): pl.pallas_call(early_kernel, out_shape=(held((32, 32, 512)), held((16, 32...  4 us
    pallas_call x1, Pallas kernels, level(): pl.pallas_call(level_kernel, out_shape=(held((4, 640, 128)), held((4, 640...  2.22 us
    ppermute x1, waiting for transfers between devices, reduce_owners(): other = lax.ppermute(send, 'col', [(i, i ^ 1) for i in range(32)])  2.06 us
    pallas_call x1, Pallas kernels, late(): pl.pallas_call(late_kernel, out_shape=(jax.ShapeDtypeStruct((32, 56, 128)...  1.97 us
  transfers between devices with their start and end apart: 6, of which 4 were waited for; matrix products, arithmetic and copies ran while one was open for 0% of the time, Pallas kernels for 9%

profile of v7, /device:TPU:8, one launch (start us, length us, event | category | flops | bytes accessed | tf_op | source)
XLA Modules:
  0.0 72.3 jit_solution(10162853385498234262)
XLA Ops:
  0.6 0.0 copy-start.1
  0.6 0.0 copy-start
  0.7 1.1 %cols.1 = (bf16[64,4,128]{2,1,0:T(4,128)(2,1)S(1)}, bf16[64,4,128]{2,1,0:T(4,128)(2,1)S(1)}) custom-call(bf16[32,56,128]{2,1,0:T(8,128)(2,1)} %x_first.3, bf16[32,56,128]{2,1,0:T(8,128)(2,1)} %x_first.3, bf16[32,56,128]{2,1,0:T(8,128)(2,1)} %c_first.3, bf16[32,56,128]{2,1,0:T(8,128)(2,1)} %c_first.3), custom_call_target="tpu_custom_call" | custom-call | tf_op jit(solution)/shard_map/cols/pallas_call | solution.py:510
  1.8 0.0 copy-start.2
  1.8 0.0 copy-start.3
  1.8 0.0 copy-start.4
  1.8 2.1 %collective-permute-start = (bf16[64,4,128]{2,1,0:T(4,128)(2,1)S(1)}, bf16[64,4,128]{2,1,0:T(4,128)(2,1)S(1)}, u32[]{:S(2)}, u32[]{:S(2)}) collective-permute-start(bf16[64,4,128]{2,1,0:T(4,128)(2,1)S(1)} %get-tuple-element.35), channel_id=1, source_target_pairs={{1,2},{3,4},{5,6},{7,8},{9,10},{11,12},{13,14},{15,16},{17,18},{19... | collective-permute-start | bytes 196616 | tf_op jit(solution)/shard_map/ppermute | solution.py:472
  3.9 3.6 %collective-permute-start.1 = (bf16[64,4,128]{2,1,0:T(4,128)(2,1)S(1)}, bf16[64,4,128]{2,1,0:T(4,128)(2,1)S(1)}, u32[]{:S(2)}, u32[]{:S(2)}) collective-permute-start(bf16[64,4,128]{2,1,0:T(4,128)(2,1)S(1)} %get-tuple-element.36), channel_id=1, source_target_pairs={{0,1},{2,3},{4,5},{6,7},{8,9},{10,11},{12,13},{14,15},{16,17},{18,... | collective-permute-start | bytes 196616 | tf_op jit(solution)/shard_map/ppermute | solution.py:472
  7.5 0.1 collective-permute-done.col_b
  7.5 0.8 %collective-permute-done.1.col_a = bf16[64,4,128]{2,1,0:T(4,128)(2,1)S(1)} collective-permute-done((bf16[64,4,128]{2,1,0:T(4,128)(2,1)S(1)}, bf16[64,4,128]{2,1,0:T(4,128)(2,1)S(1)}, u32[]{:S(2)}, u32[]{:S(2)}) %collective-permute-start.1) | collective-permute-done | bytes 65568 | tf_op jit(solution)/shard_map/ppermute | solution.py:472
  8.4 0.0 copy-done.1
  8.4 0.0 copy-done
  8.4 0.1 rows.1
  8.4 0.7 collective-permute-start.2
  9.1 12.7 %collective-permute-start.3 = (bf16[6,64,128]{2,1,0:T(8,128)(2,1)S(1)}, bf16[6,64,128]{2,1,0:T(8,128)(2,1)S(1)}, u32[]{:S(2)}, u32[]{:S(2)}) collective-permute-start(bf16[6,64,128]{2,1,0:T(8,128)(2,1)S(1)} %get-tuple-element.43), channel_id=1, source_target_pairs={{0,32},{64,96},{128,160},{192,224},{256,288},{320,352},{384,416},{... | collective-permute-start | bytes 294920 | tf_op jit(solution)/shard_map/ppermute | solution.py:472
  21.8 0.0 copy-done.2
  21.8 0.0 copy-done.3
  21.9 0.0 copy-done.4
  21.9 0.3 weights.1
  22.2 4.0 %early.1 = (bf16[32,32,512]{2,1,0:T(8,128)(2,1)S(1)}, bf16[16,32,512]{2,1,0:T(8,128)(2,1)S(1)}, bf16[30,32,384]{2,1,0:T(8,128)(2,1)S(1)}, f32[30,32,256]{2,1,0:T...) custom-call(bf16[32,56,128]{2,1,0:T(8,128)(2,1)S(1)} %copy-done, ...), custom_call_target="tpu_custom_call" | custom-call | tf_op jit(solution)/shard_map/early/pallas_call | solution.py:401
  26.2 0.0 collective-permute-done.2.row_b
  26.2 0.0 collective-permute-done.3.row_a
  26.2 2.2 %level.1 = (bf16[4,640,128]{2,1,0:T(8,128)(2,1)S(1)}, bf16[4,640,128]{2,1,0:T(8,128)(2,1)S(1)}, bf16[8,32,384]{2,1,0:T(8,128)(2,1)S(1)}, bf16[2,32,256]{2,1,0:T(8,128)(2,1)S(1)}, bf16[7,32,512]{2,1,0:T(8,128)(2,1)S(1)}) custom-call(bf16[6,64,128]{2,1,0:T(8,128)(2,1)S(1)} %collective-permute-done.2.row_b, ...), custom_call_target="tpu_custom_call" | custom-call | tf_op jit(solution)/shard_map/level/pallas_call | solution.py:424
  28.4 1.9 %collective-permute-start.4 = (bf16[4,640,128]{2,1,0:T(8,128)(2,1)S(1)}, bf16[4,640,128]{2,1,0:T(8,128)(2,1)S(1)}, u32[]{:S(2)}, u32[]{:S(2)}) collective-permute-start(bf16[4,640,128]{2,1,0:T(8,128)(2,1)S(1)} %get-tuple-element.57), channel_id=1, source_target_pairs={{0,1},{1,0},{2,3},{3,2},{4,5},{5,4},{6,7},{7,6},{8,9},{9,8},{10,11... | collective-permute-start | bytes 1966088 | tf_op jit(solution)/shard_map/ppermute | solution.py:599
  30.4 2.1 %collective-permute-done.4 = bf16[4,640,128]{2,1,0:T(8,128)(2,1)S(1)} collective-permute-done((bf16[4,640,128]{2,1,0:T(8,128)(2,1)S(1)}, bf16[4,640,128]{2,1,0:T(8,128)(2,1)S(1)}, u32[]{:S(2)}, u32[]{:S(2)}) %collective-permute-start.4) | collective-permute-done | bytes 655392 | tf_op jit(solution)/shard_map/ppermute | solution.py:599
  32.4 0.2 add_convert_fusion
  32.6 18.1 %all_to_all.10.received = bf16[4,640,128]{2,1,0:T(8,128)(2,1)S(1)} all-to-all(bf16[4,640,128]{2,1,0:T(8,128)(2,1)S(1)} %add_convert_fusion), channel_id=1, replica_groups={{0,128,256,384},{1,129,257,385},{2,130,258,386},{3,131,259,387},{4,132,..., dimensions={0} | all-to-all | bytes 1310720 | tf_op jit(solution)/shard_map/all_to_all | solution.py:601
  50.7 0.8 %spread.1 = bf16[640,128]{1,0:T(8,128)(2,1)} custom-call(bf16[4,640,128]{2,1,0:T(8,128)(2,1)S(1)} %all_to_all.10.received), custom_call_target="tpu_custom_call" | custom-call | tf_op jit(solution)/shard_map/spread/pallas_call | solution.py:602
  51.5 8.7 %all-to-all-start.1 = ((bf16[64,5,2,128]{3,2,1,0:T(2,128)(2,1)}), bf16[64,5,2,128]{3,2,1,0:T(2,128)(2,1)S(1)}, u32[]{:S(2)}, u32[]{:S(2)}) async-start(bf16[64,5,2,128]{3,2,1,0:T(2,128)(2,1)} %bitcast.1), calls=%async_computation.1 | async-start | bytes 327680 | tf_op jit(solution)/shard_map/all_to_all | solution.py:612
  60.2 2.0 %late.1 = (bf16[32,56,128]{2,1,0:T(8,128)(2,1)}, bf16[32,56,128]{2,1,0:T(8,128)(2,1)}) custom-call(bf16[30,32,384]{2,1,0:T(8,128)(2,1)S(1)} %get-tuple-element.41.f3_in, bf16[8,32,384]{2,1,0:T(8,128)(2,1)S(1)} %get-tuple-element.51.f3_rim, bf16[14,32,256]{2,1,0:T(8,128)(2,1)S(1)} %get-tuple-element.52.coarse_in, ...), custom_call_target="tpu_custom_call" | custom-call | tf_op jit(solution)/shard_map/late/pallas_call | solution.py:452
  62.1 9.4 %all-to-all-done.1 = bf16[64,5,2,128]{3,2,1,0:T(2,128)(2,1)S(1)} async-done(((bf16[64,5,2,128]{3,2,1,0:T(2,128)(2,1)}), bf16[64,5,2,128]{3,2,1,0:T(2,128)(2,1)S(1)}, u32[]{:S(2)}, u32[]{:S(2)}) %all-to-all-start.1) | async-done | bytes 163872 | tf_op jit(solution)/shard_map/all_to_all | solution.py:612
  71.6 0.7 finish.1
Async XLA Ops:
  0.6 7.7 %copy-start.1 = (bf16[32,56,128]{2,1,0:T(8,128)(2,1)S(1)}, bf16[32,56,128]{2,1,0:T(8,128)(2,1)}, u32[]{:S(2)}) copy-start(bf16[32,56,128]{2,1,0:T(8,128)(2,1)} %c_first.3) | copy-start | bytes 1376260
  0.6 7.7 %copy-start = (bf16[32,56,128]{2,1,0:T(8,128)(2,1)S(1)}, bf16[32,56,128]{2,1,0:T(8,128)(2,1)}, u32[]{:S(2)}) copy-start(bf16[32,56,128]{2,1,0:T(8,128)(2,1)} %x_first.3) | copy-start | bytes 1376260
  1.8 20.1 %copy-start.2 = (bf16[3,3,128,256]{3,2,1,0:T(8,128)(2,1)S(1)}, bf16[3,3,128,256]{3,2,1,0:T(8,128)(2,1)}, u32[]{:S(2)}) copy-start(bf16[3,3,128,256]{3,2,1,0:T(8,128)(2,1)} %wd.1) | copy-start | bytes 1769476
  1.8 20.1 %copy-start.3 = (bf16[3,3,128,128]{3,2,1,0:T(8,128)(2,1)S(1)}, bf16[3,3,128,128]{3,2,1,0:T(8,128)(2,1)}, u32[]{:S(2)}) copy-start(bf16[3,3,128,128]{3,2,1,0:T(8,128)(2,1)} %wc.1) | copy-start | bytes 884740
  1.8 20.1 %copy-start.4 = (bf16[2,2,256,128]{3,2,1,0:T(8,128)(2,1)S(1)}, bf16[2,2,256,128]{3,2,1,0:T(8,128)(2,1)}, u32[]{:S(2)}) copy-start(bf16[2,2,256,128]{3,2,1,0:T(8,128)(2,1)} %wu.1) | copy-start | bytes 786436
  1.8 5.7 %collective-permute-start = (bf16[64,4,128]{2,1,0:T(4,128)(2,1)S(1)}, bf16[64,4,128]{2,1,0:T(4,128)(2,1)S(1)}, u32[]{:S(2)}, u32[]{:S(2)}) collective-permute-start(bf16[64,4,128]{2,1,0:T(4,128)(2,1)S(1)} %get-tuple-element.35), channel_id=1, source_target_pairs={{1,2},{3,4},{5,6},{7,8},{9,10},{11,12},{13,14},{15,16},{17,18},{19... | collective-permute-start | bytes 196616 | tf_op jit(solution)/shard_map/ppermute | solution.py:472
  3.9 4.5 %collective-permute-start.1 = (bf16[64,4,128]{2,1,0:T(4,128)(2,1)S(1)}, bf16[64,4,128]{2,1,0:T(4,128)(2,1)S(1)}, u32[]{:S(2)}, u32[]{:S(2)}) collective-permute-start(bf16[64,4,128]{2,1,0:T(4,128)(2,1)S(1)} %get-tuple-element.36), channel_id=1, source_target_pairs={{0,1},{2,3},{4,5},{6,7},{8,9},{10,11},{12,13},{14,15},{16,17},{18,... | collective-permute-start | bytes 196616 | tf_op jit(solution)/shard_map/ppermute | solution.py:472
  8.4 17.8 %collective-permute-start.2 = (bf16[6,64,128]{2,1,0:T(8,128)(2,1)S(1)}, bf16[6,64,128]{2,1,0:T(8,128)(2,1)S(1)}, u32[]{:S(2)}, u32[]{:S(2)}) collective-permute-start(bf16[6,64,128]{2,1,0:T(8,128)(2,1)S(1)} %get-tuple-element.42), channel_id=1, source_target_pairs={{32,64},{96,128},{160,192},{224,256},{288,320},{352,384},{416,448}... | collective-permute-start | bytes 294920 | tf_op jit(solution)/shard_map/ppermute | solution.py:472
  9.1 17.1 %collective-permute-start.3 = (bf16[6,64,128]{2,1,0:T(8,128)(2,1)S(1)}, bf16[6,64,128]{2,1,0:T(8,128)(2,1)S(1)}, u32[]{:S(2)}, u32[]{:S(2)}) collective-permute-start(bf16[6,64,128]{2,1,0:T(8,128)(2,1)S(1)} %get-tuple-element.43), channel_id=1, source_target_pairs={{0,32},{64,96},{128,160},{192,224},{256,288},{320,352},{384,416},{... | collective-permute-start | bytes 294920 | tf_op jit(solution)/shard_map/ppermute | solution.py:472
  28.4 4.0 %collective-permute-start.4 = (bf16[4,640,128]{2,1,0:T(8,128)(2,1)S(1)}, bf16[4,640,128]{2,1,0:T(8,128)(2,1)S(1)}, u32[]{:S(2)}, u32[]{:S(2)}) collective-permute-start(bf16[4,640,128]{2,1,0:T(8,128)(2,1)S(1)} %get-tuple-element.57), channel_id=1, source_target_pairs={{0,1},{1,0},{2,3},{3,2},{4,5},{5,4},{6,7},{7,6},{8,9},{9,8},{10,11... | collective-permute-start | bytes 1966088 | tf_op jit(solution)/shard_map/ppermute | solution.py:599
  51.5 20.1 %all-to-all-start.1 = ((bf16[64,5,2,128]{3,2,1,0:T(2,128)(2,1)}), bf16[64,5,2,128]{3,2,1,0:T(2,128)(2,1)S(1)}, u32[]{:S(2)}, u32[]{:S(2)}) async-start(bf16[64,5,2,128]{3,2,1,0:T(2,128)(2,1)} %bitcast.1), calls=%async_computation.1 | async-start | bytes 327680 | tf_op jit(solution)/shard_map/all_to_all | solution.py:612

commit v8 on v7

--- a/solution.py
+++ b/solution.py
@@ -538,6 +538,7 @@
     flat_down = w_down.reshape(1152, 256)
     weights = prepare_weights(w_conv, w_down, w_up)
     cols = column_halo(inputs, cotangent)
+    weights, cols = lax.optimization_barrier((weights, cols))
     rows = row_halo(inputs, cotangent, cols)
     inner = early(inputs, cotangent, cols, weights, flat_down)
     keep, send, f3_rim, coarse_rim, g4_rim = level(rows, inner, weights, flat_down)

time: 72.6 us -> 72.7 us (level)
  local copies, waits for them, and re-layouts: 0.03 us -> 0.96 us
  waiting for transfers between devices: 12.4 us -> 11.5 us
    unnamed x10, local copies, waits for them, and re-layouts: 0.03 us -> 0.96 us
    ppermute x4, waiting for transfers between devices: 0.88 us -> 0.01 us  [swap(): return (lax.ppermute(longer, axis, odd), lax.ppermute(shorter, axis, even))]
  transfers between devices with their start and end apart: 6 -> 6, of which waited for: 4 -> 2; matrix products, arithmetic and copies ran while one was open for 0% -> 0% of each run, Pallas kernels for 9% -> 9%
where the time goes in v8:
time: 72.7 us; the launch traced here: 72.4 us
  starting transfers between devices  29.6 us (41%)
  blocking collectives  18.1 us (25%)
  waiting for transfers between devices  11.5 us (16%)
  Pallas kernels  11.2 us (15%)
  local copies, waits for them, and re-layouts  0.96 us (1%)
  between operations  0.82 us (1%)
    ppermute x4, starting transfers between devices, swap(): return (lax.ppermute(longer, axis, odd), lax.ppermute(shorter, axis, even))  18.9 us
    all_to_all x1, blocking collectives, reduce_owners(): got = lax.all_to_all(pair, mesh, 0, 0, axis_index_groups=across, tiled=True)  18.1 us
    all_to_all x1, waiting for transfers between devices, reduce_owners(): lax.all_to_all(spread, mesh, 0, 0, axis_index_groups=plane, tiled=True)  9.42 us
    all_to_all x1, starting transfers between devices, reduce_owners(): lax.all_to_all(spread, mesh, 0, 0, axis_index_groups=plane, tiled=True)  8.75 us
    pallas_call x1, Pallas kernels, early(): pl.pallas_call(early_kernel, out_shape=(held((32, 32, 512)), held((16, 32...  4 us
    pallas_call x1, Pallas kernels, level(): pl.pallas_call(level_kernel, out_shape=(held((4, 640, 128)), held((4, 640...  2.22 us
    ppermute x1, waiting for transfers between devices, reduce_owners(): other = lax.ppermute(send, 'col', [(i, i ^ 1) for i in range(32)])  2.06 us
    pallas_call x1, Pallas kernels, late(): pl.pallas_call(late_kernel, out_shape=(jax.ShapeDtypeStruct((32, 56, 128)...  1.97 us
  transfers between devices with their start and end apart: 6, of which 2 were waited for; matrix products, arithmetic and copies ran while one was open for 0% of the time, Pallas kernels for 9%

profile of v8, /device:TPU:8, one launch (start us, length us, event | category | flops | bytes accessed | tf_op | source)
XLA Modules:
  0.0 72.4 jit_solution(5083715994972638009)
XLA Ops:
  0.6 0.0 copy-start.1
  0.6 0.0 copy-start
  0.7 0.0 copy-start.2
  0.7 0.0 copy-start.3
  0.7 1.2 %cols.1 = (bf16[64,4,128]{2,1,0:T(4,128)(2,1)S(1)}, bf16[64,4,128]{2,1,0:T(4,128)(2,1)S(1)}) custom-call(bf16[32,56,128]{2,1,0:T(8,128)(2,1)} %x_first.3, bf16[32,56,128]{2,1,0:T(8,128)(2,1)} %x_first.3, bf16[32,56,128]{2,1,0:T(8,128)(2,1)} %c_first.3, bf16[32,56,128]{2,1,0:T(8,128)(2,1)} %c_first.3), custom_call_target="tpu_custom_call" | custom-call | tf_op jit(solution)/shard_map/cols/pallas_call | solution.py:510
  1.8 1.9 %collective-permute-start = (bf16[64,4,128]{2,1,0:T(4,128)(2,1)S(1)}, bf16[64,4,128]{2,1,0:T(4,128)(2,1)S(1)}, u32[]{:S(2)}, u32[]{:S(2)}) collective-permute-start(bf16[64,4,128]{2,1,0:T(4,128)(2,1)S(1)} %get-tuple-element.47), channel_id=1, source_target_pairs={{1,2},{3,4},{5,6},{7,8},{9,10},{11,12},{13,14},{15,16},{17,18},{19... | collective-permute-start | bytes 196616 | tf_op jit(solution)/shard_map/ppermute | solution.py:472
  3.8 3.6 %collective-permute-start.1 = (bf16[64,4,128]{2,1,0:T(4,128)(2,1)S(1)}, bf16[64,4,128]{2,1,0:T(4,128)(2,1)S(1)}, u32[]{:S(2)}, u32[]{:S(2)}) collective-permute-start(bf16[64,4,128]{2,1,0:T(4,128)(2,1)S(1)} %get-tuple-element.48), channel_id=1, source_target_pairs={{0,1},{2,3},{4,5},{6,7},{8,9},{10,11},{12,13},{14,15},{16,17},{18,... | collective-permute-start | bytes 196616 | tf_op jit(solution)/shard_map/ppermute | solution.py:472
  7.4 0.0 copy-done.2
  7.4 0.0 copy-done.3
  7.4 0.0 copy-start.4
  7.4 0.9 %copy-done.4 = bf16[2,2,256,128]{3,2,1,0:T(8,128)(2,1)S(1)} copy-done((bf16[2,2,256,128]{3,2,1,0:T(8,128)(2,1)S(1)}, bf16[2,2,256,128]{3,2,1,0:T(8,128)(2,1)}, u32[]{:S(2)}) %copy-start.4) | copy-done | bytes 262168
  8.3 0.3 weights.1
  8.7 0.0 collective-permute-done.col_b
  8.7 0.0 collective-permute-done.1.col_a
  8.7 0.0 copy-done.1
  8.7 0.0 copy-done
  8.7 0.1 rows.1
  8.8 0.7 collective-permute-start.2
  9.5 12.7 %collective-permute-start.3 = (bf16[6,64,128]{2,1,0:T(8,128)(2,1)S(1)}, bf16[6,64,128]{2,1,0:T(8,128)(2,1)S(1)}, u32[]{:S(2)}, u32[]{:S(2)}) collective-permute-start(bf16[6,64,128]{2,1,0:T(8,128)(2,1)S(1)} %get-tuple-element.57), channel_id=1, source_target_pairs={{0,32},{64,96},{128,160},{192,224},{256,288},{320,352},{384,416},{... | collective-permute-start | bytes 294920 | tf_op jit(solution)/shard_map/ppermute | solution.py:472
  22.2 4.0 %early.1 = (bf16[32,32,512]{2,1,0:T(8,128)(2,1)S(1)}, bf16[16,32,512]{2,1,0:T(8,128)(2,1)S(1)}, bf16[30,32,384]{2,1,0:T(8,128)(2,1)S(1)}, f32[30,32,256]{2,1,0:T...) custom-call(bf16[32,56,128]{2,1,0:T(8,128)(2,1)S(1)} %copy-done, ...), custom_call_target="tpu_custom_call" | custom-call | tf_op jit(solution)/shard_map/early/pallas_call | solution.py:401
  26.2 0.0 collective-permute-done.2.row_b
  26.2 0.0 collective-permute-done.3.row_a
  26.2 2.2 %level.1 = (bf16[4,640,128]{2,1,0:T(8,128)(2,1)S(1)}, bf16[4,640,128]{2,1,0:T(8,128)(2,1)S(1)}, bf16[8,32,384]{2,1,0:T(8,128)(2,1)S(1)}, bf16[2,32,256]{2,1,0:T(8,128)(2,1)S(1)}, bf16[7,32,512]{2,1,0:T(8,128)(2,1)S(1)}) custom-call(bf16[6,64,128]{2,1,0:T(8,128)(2,1)S(1)} %collective-permute-done.2.row_b, ...), custom_call_target="tpu_custom_call" | custom-call | tf_op jit(solution)/shard_map/level/pallas_call | solution.py:424
  28.4 1.9 %collective-permute-start.4 = (bf16[4,640,128]{2,1,0:T(8,128)(2,1)S(1)}, bf16[4,640,128]{2,1,0:T(8,128)(2,1)S(1)}, u32[]{:S(2)}, u32[]{:S(2)}) collective-permute-start(bf16[4,640,128]{2,1,0:T(8,128)(2,1)S(1)} %get-tuple-element.71), channel_id=1, source_target_pairs={{0,1},{1,0},{2,3},{3,2},{4,5},{5,4},{6,7},{7,6},{8,9},{9,8},{10,11... | collective-permute-start | bytes 1966088 | tf_op jit(solution)/shard_map/ppermute | solution.py:600
  30.4 2.1 %collective-permute-done.4 = bf16[4,640,128]{2,1,0:T(8,128)(2,1)S(1)} collective-permute-done((bf16[4,640,128]{2,1,0:T(8,128)(2,1)S(1)}, bf16[4,640,128]{2,1,0:T(8,128)(2,1)S(1)}, u32[]{:S(2)}, u32[]{:S(2)}) %collective-permute-start.4) | collective-permute-done | bytes 655392 | tf_op jit(solution)/shard_map/ppermute | solution.py:600
  32.4 0.2 add_convert_fusion
  32.6 18.1 %all_to_all.10.received = bf16[4,640,128]{2,1,0:T(8,128)(2,1)S(1)} all-to-all(bf16[4,640,128]{2,1,0:T(8,128)(2,1)S(1)} %add_convert_fusion), channel_id=1, replica_groups={{0,128,256,384},{1,129,257,385},{2,130,258,386},{3,131,259,387},{4,132,..., dimensions={0} | all-to-all | bytes 1310720 | tf_op jit(solution)/shard_map/all_to_all | solution.py:602
  50.7 0.8 %spread.1 = bf16[640,128]{1,0:T(8,128)(2,1)} custom-call(bf16[4,640,128]{2,1,0:T(8,128)(2,1)S(1)} %all_to_all.10.received), custom_call_target="tpu_custom_call" | custom-call | tf_op jit(solution)/shard_map/spread/pallas_call | solution.py:603
  51.5 8.8 %all-to-all-start.1 = ((bf16[64,5,2,128]{3,2,1,0:T(2,128)(2,1)}), bf16[64,5,2,128]{3,2,1,0:T(2,128)(2,1)S(1)}, u32[]{:S(2)}, u32[]{:S(2)}) async-start(bf16[64,5,2,128]{3,2,1,0:T(2,128)(2,1)} %bitcast.1), calls=%async_computation.1 | async-start | bytes 327680 | tf_op jit(solution)/shard_map/all_to_all | solution.py:613
  60.3 2.0 %late.1 = (bf16[32,56,128]{2,1,0:T(8,128)(2,1)}, bf16[32,56,128]{2,1,0:T(8,128)(2,1)}) custom-call(bf16[30,32,384]{2,1,0:T(8,128)(2,1)S(1)} %get-tuple-element.55.f3_in, bf16[8,32,384]{2,1,0:T(8,128)(2,1)S(1)} %get-tuple-element.65.f3_rim, bf16[14,32,256]{2,1,0:T(8,128)(2,1)S(1)} %get-tuple-element.66.coarse_in, ...), custom_call_target="tpu_custom_call" | custom-call | tf_op jit(solution)/shard_map/late/pallas_call | solution.py:452
  62.2 9.4 %all-to-all-done.1 = bf16[64,5,2,128]{3,2,1,0:T(2,128)(2,1)S(1)} async-done(((bf16[64,5,2,128]{3,2,1,0:T(2,128)(2,1)}), bf16[64,5,2,128]{3,2,1,0:T(2,128)(2,1)S(1)}, u32[]{:S(2)}, u32[]{:S(2)}) %all-to-all-start.1) | async-done | bytes 163872 | tf_op jit(solution)/shard_map/all_to_all | solution.py:613
  71.7 0.7 finish.1
Async XLA Ops:
  0.6 8.0 %copy-start.1 = (bf16[32,56,128]{2,1,0:T(8,128)(2,1)S(1)}, bf16[32,56,128]{2,1,0:T(8,128)(2,1)}, u32[]{:S(2)}) copy-start(bf16[32,56,128]{2,1,0:T(8,128)(2,1)} %c_first.3) | copy-start | bytes 1376260
  0.6 8.0 %copy-start = (bf16[32,56,128]{2,1,0:T(8,128)(2,1)S(1)}, bf16[32,56,128]{2,1,0:T(8,128)(2,1)}, u32[]{:S(2)}) copy-start(bf16[32,56,128]{2,1,0:T(8,128)(2,1)} %x_first.3) | copy-start | bytes 1376260
  0.7 6.7 %copy-start.2 = (bf16[3,3,128,256]{3,2,1,0:T(8,128)(2,1)S(1)}, bf16[3,3,128,256]{3,2,1,0:T(8,128)(2,1)}, u32[]{:S(2)}) copy-start(bf16[3,3,128,256]{3,2,1,0:T(8,128)(2,1)} %wd.1) | copy-start | bytes 1769476
  0.7 6.7 %copy-start.3 = (bf16[3,3,128,128]{3,2,1,0:T(8,128)(2,1)S(1)}, bf16[3,3,128,128]{3,2,1,0:T(8,128)(2,1)}, u32[]{:S(2)}) copy-start(bf16[3,3,128,128]{3,2,1,0:T(8,128)(2,1)} %wc.1) | copy-start | bytes 884740
  1.8 6.8 %collective-permute-start = (bf16[64,4,128]{2,1,0:T(4,128)(2,1)S(1)}, bf16[64,4,128]{2,1,0:T(4,128)(2,1)S(1)}, u32[]{:S(2)}, u32[]{:S(2)}) collective-permute-start(bf16[64,4,128]{2,1,0:T(4,128)(2,1)S(1)} %get-tuple-element.47), channel_id=1, source_target_pairs={{1,2},{3,4},{5,6},{7,8},{9,10},{11,12},{13,14},{15,16},{17,18},{19... | collective-permute-start | bytes 196616 | tf_op jit(solution)/shard_map/ppermute | solution.py:472
  3.8 4.9 %collective-permute-start.1 = (bf16[64,4,128]{2,1,0:T(4,128)(2,1)S(1)}, bf16[64,4,128]{2,1,0:T(4,128)(2,1)S(1)}, u32[]{:S(2)}, u32[]{:S(2)}) collective-permute-start(bf16[64,4,128]{2,1,0:T(4,128)(2,1)S(1)} %get-tuple-element.48), channel_id=1, source_target_pairs={{0,1},{2,3},{4,5},{6,7},{8,9},{10,11},{12,13},{14,15},{16,17},{18,... | collective-permute-start | bytes 196616 | tf_op jit(solution)/shard_map/ppermute | solution.py:472
  7.4 1.0 %copy-start.4 = (bf16[2,2,256,128]{3,2,1,0:T(8,128)(2,1)S(1)}, bf16[2,2,256,128]{3,2,1,0:T(8,128)(2,1)}, u32[]{:S(2)}) copy-start(bf16[2,2,256,128]{3,2,1,0:T(8,128)(2,1)} %wu.1) | copy-start | bytes 786436
  8.8 17.4 %collective-permute-start.2 = (bf16[6,64,128]{2,1,0:T(8,128)(2,1)S(1)}, bf16[6,64,128]{2,1,0:T(8,128)(2,1)S(1)}, u32[]{:S(2)}, u32[]{:S(2)}) collective-permute-start(bf16[6,64,128]{2,1,0:T(8,128)(2,1)S(1)} %get-tuple-element.56), channel_id=1, source_target_pairs={{32,64},{96,128},{160,192},{224,256},{288,320},{352,384},{416,448}... | collective-permute-start | bytes 294920 | tf_op jit(solution)/shard_map/ppermute | solution.py:472
  9.5 16.7 %collective-permute-start.3 = (bf16[6,64,128]{2,1,0:T(8,128)(2,1)S(1)}, bf16[6,64,128]{2,1,0:T(8,128)(2,1)S(1)}, u32[]{:S(2)}, u32[]{:S(2)}) collective-permute-start(bf16[6,64,128]{2,1,0:T(8,128)(2,1)S(1)} %get-tuple-element.57), channel_id=1, source_target_pairs={{0,32},{64,96},{128,160},{192,224},{256,288},{320,352},{384,416},{... | collective-permute-start | bytes 294920 | tf_op jit(solution)/shard_map/ppermute | solution.py:472
  28.4 4.0 %collective-permute-start.4 = (bf16[4,640,128]{2,1,0:T(8,128)(2,1)S(1)}, bf16[4,640,128]{2,1,0:T(8,128)(2,1)S(1)}, u32[]{:S(2)}, u32[]{:S(2)}) collective-permute-start(bf16[4,640,128]{2,1,0:T(8,128)(2,1)S(1)} %get-tuple-element.71), channel_id=1, source_target_pairs={{0,1},{1,0},{2,3},{3,2},{4,5},{5,4},{6,7},{7,6},{8,9},{9,8},{10,11... | collective-permute-start | bytes 1966088 | tf_op jit(solution)/shard_map/ppermute | solution.py:600
  51.5 20.1 %all-to-all-start.1 = ((bf16[64,5,2,128]{3,2,1,0:T(2,128)(2,1)}), bf16[64,5,2,128]{3,2,1,0:T(2,128)(2,1)S(1)}, u32[]{:S(2)}, u32[]{:S(2)}) async-start(bf16[64,5,2,128]{3,2,1,0:T(2,128)(2,1)} %bitcast.1), calls=%async_computation.1 | async-start | bytes 327680 | tf_op jit(solution)/shard_map/all_to_all | solution.py:613
